TPU v7x, 32 devices: a whole 2x2x4 slice. The times are simulated.
32 devices in a mesh: tower: 2 (over core), batch: 2 (over x), mp: 8 (over z, y).
Axes of the slice: x: 2, y: 2, z: 4, core: 2. Of those that a mesh axis runs over, the one named last changes fastest.
Arguments:
- acts: bfloat16 [2, 6144, 9216], P('tower', ('batch', 'mp')), may hold values from -6 to 6
- fc_weight: bfloat16 [2, 9216, 4096], P('tower', None, 'mp'), may hold values from -0.0625 to 0.0625
- fc_bias: bfloat16 [2, 4096], P('tower', 'mp'), may hold values from -3 to 3
- stitch: float32 [2, 2, 4096], P('tower', None, 'mp'), may hold values from 0.2 to 1
- image_grad: bfloat16 [2, 2048, 4096], P('tower', 'batch', 'mp'), may hold values from -8 to 8
- crop_counts: int32 [2048], P('batch'), may hold values from 1 to 3
- row_image: int32 [6144], P('batch'), may hold values from 0 to 2047, as said below
- row_live: int32 [6144], P('batch'), may hold values from 0 to 1, as said below
Outputs:
- stitched_out: bfloat16 [2, 6144, 4096], P('tower', 'batch', 'mp')
- acts_grad: bfloat16 [2, 6144, 9216], P('tower', ('batch', 'mp'))
- weight_grad: float32 [2, 9216, 4096], P('tower', None, 'mp')
- bias_grad: float32 [2, 4096], P('tower', 'mp')
- stitch_grad: float32 [2, 2, 4096], P('tower', None, 'mp')
Inputs may be any that keep to these rules, and one draw needn't show every extreme that they name: `row_image`: each image's crop rows are consecutive slots of the 3072 slots of its index of batch, images in order; image i lies in batch block i // 1024; crop_counts[i] is the number of live rows of image i; every batch block has padding rows at its end, and padding rows name an image of their own block. `row_live`: live rows come first in each block of 3072 slots.
All inputs are finite; a program needn't handle non-finite values.
Results may differ from a plain program's by a relative error of at most 0.008.
Values may be sent and summed in bfloat16 or wider, within the bound.
No kernel may reach another device: no remote copies, remote signals or barrier semaphores. Data moves between devices by JAX's collectives and lax.ppermute only.
A program may use at most 320 MiB of HBM per device.

v0:
```python
import jax
import jax.numpy as jnp
from jax import lax
from jax.sharding import PartitionSpec as P


def swapped(block, axis, bit):
    count = lax.axis_size(axis)
    route = []
    for low in range(count):
        high = low | 1 << bit
        if high != low and high < count:
            route += [(low, high), (high, low)]
    return lax.ppermute(block, axis, route)


def per_device(acts, fc_weight, fc_bias, stitch, image_grad, crop_counts, row_image, row_live):
    feature_rows = acts[0]
    weight_matrix = fc_weight[0]
    layer_bias = fc_bias[0].astype(jnp.float32)
    coefs = stitch[0]
    grads_img = image_grad[0]
    gathered = lax.all_gather(feature_rows, "mp", axis=0, tiled=True)
    preactivation = (
        jnp.dot(gathered, weight_matrix, preferred_element_type=jnp.float32) + layer_bias[None, :]
    )
    active = preactivation > 0
    hidden = jnp.maximum(preactivation, 0.0).astype(jnp.bfloat16)
    tower = lax.axis_index("tower")
    self_coefficient = jnp.where(tower == 0, coefs[0], coefs[1])
    other_coef = jnp.where(tower == 0, coefs[1], coefs[0])
    partner = swapped(hidden, "tower", 0)
    hidden_wide = hidden.astype(jnp.float32)
    partner_wide = partner.astype(jnp.float32)
    stitched = self_coefficient[None, :] * hidden_wide + other_coef[None, :] * partner_wide
    live = row_live.astype(jnp.float32)
    stitched_out = (stitched * live[:, None]).astype(jnp.bfloat16)
    img_dev = crop_counts.shape[0]
    local_img = row_image - lax.axis_index("batch") * img_dev
    match = local_img[:, None] == jnp.arange(img_dev, dtype=jnp.int32)[None, :]
    per_row = jnp.sum(jnp.where(match, crop_counts[None, :].astype(jnp.float32), 0.0), axis=1)
    row_weighting_scale = live / per_row
    picked = jnp.dot(match.astype(jnp.bfloat16), grads_img, preferred_element_type=jnp.float32)
    out_grad = (picked * row_weighting_scale[:, None]).astype(jnp.bfloat16)
    out_wide = out_grad.astype(jnp.float32)
    returned = swapped(other_coef[None, :] * out_wide, "tower", 0)
    hidden_grad = (self_coefficient[None, :] * out_wide + returned).astype(jnp.bfloat16)
    pre_grad = jnp.where(active, hidden_grad, jnp.zeros_like(hidden_grad))
    own_stitch = jnp.sum(out_wide * hidden_wide, axis=0)
    other_stitch = jnp.sum(out_wide * partner_wide, axis=0)
    stitch_grad = jnp.where(
        tower == 0, jnp.stack([own_stitch, other_stitch]), jnp.stack([other_stitch, own_stitch])
    )
    bias_grad = jnp.sum(pre_grad.astype(jnp.float32), axis=0)
    weight_grad = lax.dot_general(
        gathered, pre_grad, (((0,), (0,)), ((), ())), preferred_element_type=jnp.float32
    )
    weight_grad, bias_grad, stitch_grad = lax.psum((weight_grad, bias_grad, stitch_grad), "batch")
    input_grad = lax.psum_scatter(
        lax.dot_general(
            pre_grad, weight_matrix, (((1,), (1,)), ((), ())), preferred_element_type=jnp.float32
        ),
        "mp",
        scatter_dimension=0,
        tiled=True,
    )
    return (
        stitched_out[None],
        input_grad.astype(jnp.bfloat16)[None],
        weight_grad[None],
        bias_grad[None],
        stitch_grad[None],
    )


def solution(mesh):
    placed = (
        P("tower", ("batch", "mp"), None),
        P("tower", None, "mp"),
        P("tower", "mp"),
        P("tower", None, "mp"),
        P("tower", "batch", "mp"),
        P("batch"),
        P("batch"),
        P("batch"),
    )
    return jax.shard_map(
        per_device,
        mesh=mesh,
        in_specs=placed,
        out_specs=(
            P("tower", "batch", "mp"),
            P("tower", ("batch", "mp"), None),
            P("tower", None, "mp"),
            P("tower", "mp"),
            P("tower", None, "mp"),
        ),
        check_vma=False,
    )
```

profile of v0, /device:TPU:0, one launch (start us, length us, event | category | flops | bytes accessed | tf_op | source)
XLA Modules:
  0.0 3323.6 jit_solution(3777036886883844252)
XLA Ops:
  7.2 0.0 copy-start
  7.2 0.0 copy-start.7
  7.2 0.0 copy-start.8
  7.2 0.0 copy-start.4
  7.2 0.0 copy-start.2
  7.2 0.0 all-gather.3.cloned.1.call-start
  7.3 0.7 all-gather.3.cloned.1.call-update
  8.0 0.0 all-reduce.3.cloned.1.call-start
  8.0 0.0 copy-done.7
  8.1 0.0 copy-start.5
  8.1 2.0 select_reduce_fusion
  10.1 0.0 copy-start.9
  10.1 5.7 convert_multiply_fusion.2
  15.9 0.5 collective-permute-start.1
  16.4 9.9 collective-permute-done.1
  26.3 1056.3 %all-gather.3.cloned.1.call-done = bf16[1,3072,9216]{2,1,0:T(8,128)(2,1)} async-done(((bf16[1,384,9216]{2,1,0:T(8,128)(2,1)}), bf16[1,3072,9216]{2,1,0:T(8,128)(2,1)}) %all-gather.3.cloned.1.call-update) | async-done | bytes 56623120 | tf_op jit(solution)/shard_map/all_gather | solution.py:23
  1082.6 40.8 %convert_reduce_fusion = (f32[512]{0:T(512)S(1)}, bf16[3072,512]{1,0:T(8,128)(2,1)}, bf16[3072,512]{1,0:T(8,128)(2,1)}) fusion(f32[3072,512]{1,0:T(8,128)} %collective-permute-done.1, bf16[3072,512]{1,0:T(8,128)(2,1)} %get-tuple-element.26, f32[512]{0:T(512)S(1)} %bitcast.39, f32[512]{0:T(512)S(1)} %bitcast.46, bf16[1,9216,512]{2,1,0:T(8,128)(2,1)} %param.9, ...), kind=kOutput, calls=%fused_computation.25 | convolution fusion | flops 29008330752 | bytes 81795072 | tf_op jit(solution)/shard_map/dot_general | solution.py:25
  1123.4 38.7 %fusion.4 = f32[1,9216,512]{1,2,0:T(8,128)} fusion(bf16[3072,512]{1,0:T(8,128)(2,1)} %get-tuple-element.20, bf16[1,3072,9216]{2,1,0:T(8,128)(2,1)} %all-gather.3.cloned.1.call-done), kind=kOutput, calls=%fused_computation.4 | convolution fusion | flops 28991029248 | bytes 78643200 | tf_op jit(solution)/shard_map/dot_general | solution.py:55
  1162.1 0.0 all-reduce.3.cloned.1.call-update
  1162.1 0.0 reduce-scatter.2.cloned.1.call-start
  1162.2 47.0 %fusion.8 = f32[3072,9216]{1,0:T(8,128)} fusion(bf16[3072,512]{1,0:T(8,128)(2,1)} %get-tuple-element.20, bf16[1,9216,512]{2,1,0:T(8,128)(2,1)} %param.9), kind=kOutput, calls=%fused_computation.12 | convolution fusion | flops 28991029248 | bytes 125829120 | tf_op jit(solution)/shard_map/dot_general | solution.py:60
  1209.2 0.0 reduce-scatter.2.cloned.1.call-update
  1209.2 0.1 collective-permute-start
  1209.3 0.6 copy-done.3
  1209.9 5.3 collective-permute-done
  1215.2 0.0 copy-done.6
  1215.2 5.8 fusion.16
  1221.0 5.9 all-reduce
  1226.9 358.7 %all-reduce.3.cloned.1.call-done = f32[1,9216,512]{1,2,0:T(8,128)} async-done(((f32[1,9216,512]{1,2,0:T(8,128)}), f32[1,9216,512]{1,2,0:T(8,128)}) %all-reduce.3.cloned.1.call-update) | async-done | bytes 18874384 | tf_op jit(solution)/shard_map/psum | solution.py:58
  1585.5 18.8 copy.14
  1604.4 1703.7 %reduce-scatter.2.cloned.1.call-done = f32[384,9216]{1,0:T(8,128)} async-done(((f32[3072,9216]{1,0:T(8,128)}), f32[384,9216]{1,0:T(8,128)}) %reduce-scatter.2.cloned.1.call-update) | async-done | bytes 14155792 | tf_op jit(solution)/shard_map/reduce_scatter | solution.py:59
  3308.1 9.0 convert_bitcast_fusion
  (17 shorter events, 0.1 us)
Async XLA Ops:
  7.2 3.0 copy-start
  7.2 0.8 copy-start.7
  7.2 0.9 copy-start.8
  7.2 0.9 copy-start.4
  7.2 2.9 copy-start.2
  7.2 1075.3 %all-gather.3.cloned.1.call-start = ((), (), s32[]{:S(2)}) async-start(), calls=%async_computation.3 | async-start | bytes 63700992 | tf_op jit(solution)/shard_map/all_gather | solution.py:23
  8.0 1577.6 %all-reduce.3.cloned.1.call-start = ((), (), s32[]{:S(2)}) async-start(), calls=%async_computation.2 | async-start | bytes 37748736 | tf_op jit(solution)/shard_map/psum | solution.py:58
  8.1 7.8 copy-start.5
  10.1 6.2 copy-start.9
  15.9 10.4 collective-permute-start.1
  1162.1 2146.0 %reduce-scatter.2.cloned.1.call-start = ((), (), s32[]{:S(2)}) async-start(), calls=%async_computation.1 | async-start | bytes 127401984 | tf_op jit(solution)/shard_map/reduce_scatter | solution.py:59
  1209.2 0.7 copy-start.3
  1209.2 6.0 copy-start.6
  1209.2 5.9 collective-permute-start
  1585.5 1731.6 %copy-start.1 = (bf16[1,1024,512]{2,1,0:T(8,128)(2,1)S(1)}, bf16[1,1024,512]{2,1,0:T(8,128)(2,1)}, u32[]{:S(2)}) copy-start(bf16[1,1024,512]{2,1,0:T(8,128)(2,1)} %param.12) | copy-start | bytes 3145732
Sparse Core Ops, SparseCore 0:
  9.6 1072.9 all-gather.2
  1162.2 423.2 all-reduce.2
  1589.5 1718.5 reduce-scatter.1
where the time goes:
time: 3320 us
  waiting for transfers between devices  3130 us (94%)
  matrix products  132 us (4%)
    reduce_scatter x1, waiting for transfers between devices, per_device(): lax.psum_scatter(lax.dot_general(pre_grad, weight_matrix, (((1,), (1,)),...  1700 us
    all_gather x1, waiting for transfers between devices, per_device(): gathered = lax.all_gather(feature_rows, 'mp', axis=0, tiled=True)  1060 us
    psum x1, waiting for transfers between devices, per_device(): lax.psum((weight_grad, bias_grad, stitch_grad), 'batch')  359 us
  transfers between devices with their start and end apart: 5, of which 5 were waited for; matrix products, arithmetic and copies ran while one was open for 2% of the time, Pallas kernels for 0%

commit v1 on v0

--- a/solution.py
+++ b/solution.py
@@ -3,18 +3,16 @@
 from jax import lax
 from jax.sharding import PartitionSpec as P
 
-
-def swapped(block, axis, bit):
+BF = jnp.bfloat16
+F32 = jnp.float32
+
+
+def swapped(block, axis, mask):
     count = lax.axis_size(axis)
-    route = []
-    for low in range(count):
-        high = low | 1 << bit
-        if high != low and high < count:
-            route += [(low, high), (high, low)]
-    return lax.ppermute(block, axis, route)
-
-
-def per_device(acts, fc_weight, fc_bias, stitch, image_grad, crop_counts, row_image, row_live):
+    return lax.ppermute(block, axis, [(i, i ^ mask) for i in range(count)])
+
+
+def general(acts, fc_weight, fc_bias, stitch, image_grad, crop_counts, row_image, row_live):
     feature_rows = acts[0]
     weight_matrix = fc_weight[0]
     layer_bias = fc_bias[0].astype(jnp.float32)
@@ -29,7 +27,7 @@
     tower = lax.axis_index("tower")
     self_coefficient = jnp.where(tower == 0, coefs[0], coefs[1])
     other_coef = jnp.where(tower == 0, coefs[1], coefs[0])
-    partner = swapped(hidden, "tower", 0)
+    partner = swapped(hidden, "tower", 1)
     hidden_wide = hidden.astype(jnp.float32)
     partner_wide = partner.astype(jnp.float32)
     stitched = self_coefficient[None, :] * hidden_wide + other_coef[None, :] * partner_wide
@@ -43,7 +41,7 @@
     picked = jnp.dot(match.astype(jnp.bfloat16), grads_img, preferred_element_type=jnp.float32)
     out_grad = (picked * row_weighting_scale[:, None]).astype(jnp.bfloat16)
     out_wide = out_grad.astype(jnp.float32)
-    returned = swapped(other_coef[None, :] * out_wide, "tower", 0)
+    returned = swapped(other_coef[None, :] * out_wide, "tower", 1)
     hidden_grad = (self_coefficient[None, :] * out_wide + returned).astype(jnp.bfloat16)
     pre_grad = jnp.where(active, hidden_grad, jnp.zeros_like(hidden_grad))
     own_stitch = jnp.sum(out_wide * hidden_wide, axis=0)
@@ -69,6 +67,317 @@
         input_grad.astype(jnp.bfloat16)[None],
         weight_grad[None],
         bias_grad[None],
+        stitch_grad[None],
+    )
+
+
+def squares(acts, fc_weight, fc_bias, stitch, image_grad, crop_counts, row_image, row_live):
+    x = acts[0]
+    w = fc_weight[0]
+    rows, depth = x.shape
+    cols = w.shape[1]
+    half = cols // 2
+    me = lax.axis_index("mp")
+    b = lax.axis_index("batch")
+    tower = lax.axis_index("tower")
+    nq = 4
+    dq = depth // nq
+    nt = (((1,), (1,)), ((), ()))
+    tn = (((0,), (0,)), ((), ()))
+
+    token = []
+
+    def tie(v, *deps):
+        deps = [d for d in (*deps, *token) if d is not None]
+        return lax.optimization_barrier((v, *deps))[0] if deps else v
+
+    def wait(v):
+        v = tie(v)
+        token[:] = [v]
+        return v
+
+    def sy(v, *deps):
+        return swapped(tie(v, *deps), "mp", 1)
+
+    def sz(v, *deps):
+        return swapped(tie(v, *deps), "mp", 2)
+
+    def sp(v, *deps):
+        return swapped(tie(v, *deps), "mp", 4)
+
+    def sx(v, *deps):
+        return swapped(tie(v, *deps), "batch", 1)
+
+    def st(v, *deps):
+        return swapped(tie(v, *deps), "tower", 1)
+
+    def mine(v):
+        return lax.dynamic_slice_in_dim(v, b * half, half, v.ndim - 1)
+
+    def other(v):
+        return lax.dynamic_slice_in_dim(v, (1 - b) * half, half, v.ndim - 1)
+
+    def natural(m, o):
+        return jnp.where(b == 0, jnp.concatenate([m, o], -1), jnp.concatenate([o, m], -1))
+
+    def four(a, c):
+        return jnp.concatenate([a[..., :half], c[..., :half], a[..., half:], c[..., half:]], -1)
+
+    def quarter(v, q):
+        return v[q * dq : (q + 1) * dq]
+
+    top, low = x[: rows // 2], x[rows // 2 :]
+    z1 = sz(top)
+    y1 = sy(top)
+    w_m = mine(w)
+    p = [sp(quarter(w_m, 0)), sp(quarter(w_m, 1)), None, None]
+
+    w_o = other(w)
+    coefs = stitch[0]
+    self_c = jnp.where(tower == 0, coefs[0], coefs[1])
+    other_c = jnp.where(tower == 0, coefs[1], coefs[0])
+    small = jnp.stack([self_c, other_c, st(other_c), fc_bias[0].astype(F32)])
+    small = jnp.concatenate([mine(small), other(small)], 1)
+    grads = image_grad[0]
+    grads = jnp.concatenate([mine(grads), other(grads)], 1)
+
+    def square_rows(v):
+        v = v.reshape(-1, rows)
+        return jnp.concatenate(
+            [lax.dynamic_index_in_dim(v, me ^ o, 0, keepdims=False) for o in range(4)], 0
+        )
+
+    live = square_rows(row_live).astype(F32)
+    img_dev = crop_counts.shape[0]
+    local_img = square_rows(row_image) - b * img_dev
+    match = local_img[:, None] == jnp.arange(img_dev, dtype=jnp.int32)[None, :]
+    per_row = jnp.sum(jnp.where(match, crop_counts[None, :].astype(F32), 0.0), axis=1)
+    scale = live / per_row
+
+    def out_grad_of(g):
+        picked = jnp.dot(match.astype(BF), g, preferred_element_type=F32)
+        return (picked * scale[:, None]).astype(BF)
+
+    og_a = out_grad_of(grads)
+    oo_a = st(og_a)
+    wa = jnp.concatenate([w_m, w_o], 1)
+    pre_a = [jnp.dot(x, wa, preferred_element_type=F32)]
+
+    y1 = wait(y1)
+    y2 = sy(low)
+    z1 = wait(z1)
+    z2 = sz(low)
+    x_got = [None] * nq
+    p[0] = wait(p[0])
+    x_got[0] = sx(p[0])
+    p[1] = wait(p[1])
+    p[2] = sp(quarter(w_m, 2))
+    y2 = wait(y2)
+    d1 = sy(z1, pre_a[0])
+    x_got[0] = wait(x_got[0])
+    x_got[1] = sx(p[1])
+    x_y = jnp.concatenate([y1, y2], 0)
+    pre_a.append(jnp.dot(x_y, wa, preferred_element_type=F32))
+    z2 = wait(z2)
+    x_z = jnp.concatenate([z1, z2], 0)
+    pre_a.append(jnp.dot(x_z, wa, preferred_element_type=F32))
+    p[2] = wait(p[2])
+    p[3] = sp(quarter(w_m, 3), pre_a[1])
+    x_got[1] = wait(x_got[1])
+    x_got[2] = sx(p[2])
+    w4 = [None] * nq
+
+    def weights(q):
+        return jnp.concatenate(
+            [quarter(w_m, q), p[q], quarter(w_o, q), x_got[q]], 1
+        )
+
+    def b_cols(q):
+        return jnp.concatenate([p[q], x_got[q]], 1)
+
+    def kq(v, q):
+        return v[:, q * dq : (q + 1) * dq]
+
+    def dot_b(block, qs, acc):
+        for q in qs:
+            r = jnp.dot(kq(block, q), b_cols(q), preferred_element_type=F32)
+            acc = r if acc is None else acc + r
+        return acc
+
+    blocks = [x, x_y, x_z]
+    pre_b = [dot_b(v, (0, 1), None) for v in blocks]
+    d1 = wait(d1)
+    d2 = sy(z2, pre_a[2])
+    p[3] = wait(p[3])
+    grads_b = sp(grads)
+    small_b = sp(small)
+    x_got[2] = wait(x_got[2])
+    x_got[3] = sx(p[3], *pre_b)
+    pre_b = [dot_b(v, (2,), a) for v, a in zip(blocks, pre_b)]
+    x_got[3] = wait(x_got[3])
+    pre_b = [dot_b(v, (3,), a) for v, a in zip(blocks, pre_b)]
+    grads_b = wait(grads_b)
+    small_b = wait(small_b)
+    og_b = out_grad_of(grads_b)
+    oo_b = st(og_b)
+    vec = four(small, small_b)
+    self4, other4, cross4 = vec[0], vec[1], vec[2]
+    out_grad = four(og_a, og_b)
+    out_other = four(oo_a, oo_b)
+    out_wide = out_grad.astype(F32)
+    hidden_grad = (self4[None] * out_wide + cross4[None] * out_other.astype(F32)).astype(BF)
+
+    def activate(a, c, lo):
+        pre = four(a + small[3][None], c + small_b[3][None])
+        hg = hidden_grad[lo : lo + pre.shape[0]]
+        return jnp.maximum(pre, 0.0).astype(BF), jnp.where(pre > 0, hg, jnp.zeros_like(hg))
+
+    hid, pg = [], []
+    for o in range(3):
+        h, g = activate(pre_a[o], pre_b[o], o * rows)
+        hid.append(h)
+        pg.append(g)
+    w4 = [weights(q) for q in range(nq)]
+
+    def part(o, q):
+        return lax.dot_general(pg[o], w4[q], nt, preferred_element_type=F32)
+
+    n_half = rows // 2
+    a1 = jnp.dot(d1, wa, preferred_element_type=F32)
+    b1 = dot_b(d1, range(nq), None)
+    h1, g1 = activate(a1, b1, 3 * rows)
+    yd0 = part(1, 0).astype(BF)
+    d2 = wait(d2)
+    yd = [sy(yd0, g1)] + [None] * 3
+    a2 = jnp.dot(d2, wa, preferred_element_type=F32)
+    b2 = dot_b(d2, range(nq), None)
+    h2, g2 = activate(a2, b2, 3 * rows + n_half)
+    hid.append(jnp.concatenate([h1, h2], 0))
+    pg.append(jnp.concatenate([g1, g2], 0))
+    hidden = jnp.concatenate(hid, 0)
+    pre_grad = jnp.concatenate(pg, 0)
+    x_all = jnp.concatenate([x, y1, y2, z1, z2, d1, d2], 0)
+
+    def dw_sent(q):
+        return lax.dot_general(
+            kq(x_all, q), pre_grad[:, cols:], tn, preferred_element_type=F32
+        ).astype(BF)
+
+    def dw_kept(q, got):
+        r = lax.dot_general(kq(x_all, q), pre_grad[:, :cols], tn, preferred_element_type=F32)
+        return r + got.astype(F32)
+
+    s, k, a, t = [None] * nq, [None] * nq, [None] * nq, [None] * nq
+    dd, zz = [None] * nq, [None] * nq
+    s[0] = sx(dw_sent(0))
+    hid_other = st(hidden)
+    dq0 = part(3, 0).astype(BF)
+    nxt = dw_sent(1)
+    yd[0] = wait(yd[0])
+    dd[0] = sy(dq0)
+    hid_other = wait(hid_other)
+    hw, how = hidden.astype(F32), hid_other.astype(F32)
+    stitched = ((self4[None] * hw + other4[None] * how) * live[:, None]).astype(BF)
+    st_a = jnp.concatenate([stitched[:, :half], stitched[:, cols : cols + half]], 1)
+    st_b = jnp.concatenate([stitched[:, half:cols], stitched[:, cols + half :]], 1)
+    st_got = sp(st_b)
+    dq1 = part(3, 1).astype(BF)
+    s[0] = wait(s[0])
+    s[1] = sx(nxt)
+    kept = dw_kept(0, s[0])
+    t[0] = kept[:, :half]
+    k[0] = sp(kept[:, half:].astype(BF))
+    nxt = dw_sent(2)
+    dd[0] = wait(dd[0])
+    dd[1] = sy(dq1)
+    zz[0] = sz((part(2, 0) + dd[0].astype(F32)).astype(BF))
+    dq2 = part(3, 2).astype(BF)
+    dd[1] = wait(dd[1])
+    dd[2] = sy(dq2)
+    st_got = wait(st_got)
+    s[1] = wait(s[1])
+    s[2] = sx(nxt)
+    kept = dw_kept(1, s[1])
+    t[1] = kept[:, :half]
+    k[0] = wait(k[0])
+    k[1] = sp(kept[:, half:].astype(BF))
+    zz[0] = wait(zz[0])
+    zz[1] = sz((part(2, 1) + dd[1].astype(F32)).astype(BF))
+    nxt = dw_sent(3)
+    dq3 = part(3, 3).astype(BF)
+    dd[2] = wait(dd[2])
+    dd[3] = sy(dq3)
+    t[0] = t[0] + k[0].astype(F32)
+    s[2] = wait(s[2])
+    s[3] = sx(nxt)
+    kept = dw_kept(2, s[2])
+    t[2] = kept[:, :half]
+    k[1] = wait(k[1])
+    k[2] = sp(kept[:, half:].astype(BF))
+    zz[1] = wait(zz[1])
+    zz[2] = sz((part(2, 2) + dd[2].astype(F32)).astype(BF))
+    yd1 = part(1, 1).astype(BF)
+    dd[3] = wait(dd[3])
+    yd[1] = sy(yd1)
+    t[1] = t[1] + k[1].astype(F32)
+    s[3] = wait(s[3])
+    a[0] = sx(t[0].astype(BF))
+    kept = dw_kept(3, s[3])
+    t[3] = kept[:, :half]
+    k[2] = wait(k[2])
+    k[3] = sp(kept[:, half:].astype(BF))
+    zz[2] = wait(zz[2])
+    zz[3] = sz((part(2, 3) + dd[3].astype(F32)).astype(BF))
+    yd2 = part(1, 2).astype(BF)
+    a[0] = wait(a[0])
+    a[1] = sx(t[1].astype(BF))
+    yd[1] = wait(yd[1])
+    yd[2] = sy(yd2)
+    t[2] = t[2] + k[2].astype(F32)
+    yd3 = part(1, 3).astype(BF)
+    a[1] = wait(a[1])
+    a[2] = sx(t[2].astype(BF))
+    yd[2] = wait(yd[2])
+    yd[3] = sy(yd3)
+    own = [part(0, q) + yd[q].astype(F32) + zz[q].astype(F32) for q in range(3)]
+    outs = [natural(t[q], a[q].astype(F32)) for q in range(2)]
+    k[3] = wait(k[3])
+    t[3] = t[3] + k[3].astype(F32)
+    a[2] = wait(a[2])
+    a[3] = sx(t[3].astype(BF))
+    outs.append(natural(t[2], a[2].astype(F32)))
+    zz[3] = wait(zz[3])
+    yd[3] = wait(yd[3])
+    own.append(part(0, 3) + yd[3].astype(F32) + zz[3].astype(F32))
+    acts_grad = jnp.concatenate([v.astype(BF) for v in own], 1)
+    outs.append(natural(t[3], a[3].astype(F32)))
+    weight_grad = jnp.concatenate(outs, 0)
+
+    st_all = jnp.concatenate([st_a, st_got], 0)
+    st_all = natural(st_all[:, :half], st_all[:, half:])
+    st_all = st_all.reshape(8, rows, cols)
+    order = jnp.arange(8) ^ me
+    stitched_out = st_all[order].reshape(8 * rows, cols)
+
+    sums = jnp.stack(
+        [
+            jnp.sum(out_wide * hw, axis=0),
+            jnp.sum(out_wide * how, axis=0),
+            jnp.sum(pre_grad.astype(F32), axis=0),
+        ]
+    )
+    s_a = jnp.concatenate([sums[:, :half], sums[:, cols : cols + half]], 1)
+    s_b = jnp.concatenate([sums[:, half:cols], sums[:, cols + half :]], 1)
+    s_a = s_a + swapped(s_b, "mp", 4)
+    s_a = natural(s_a[:, :half], s_a[:, half:])
+    s_a = s_a + swapped(s_a, "batch", 1)
+    own_s, other_s = s_a[0], s_a[1]
+    stitch_grad = jnp.where(tower == 0, jnp.stack([own_s, other_s]), jnp.stack([other_s, own_s]))
+    return (
+        stitched_out[None],
+        acts_grad[None],
+        weight_grad[None],
+        s_a[2][None],
         stitch_grad[None],
     )
 
@@ -84,6 +393,7 @@
         P("batch"),
         P("batch"),
     )
+    per_device = squares if mesh.shape["mp"] == 8 and mesh.shape["batch"] == 2 else general
     return jax.shard_map(
         per_device,
         mesh=mesh,

time: 3320 us -> 932 us (0.28)
  waiting for transfers between devices: 3130 us -> 512 us
  matrix products: 132 us -> 218 us
  starting transfers between devices: 0.68 us -> 59.7 us
  local copies, waits for them, and re-layouts: 19.5 us -> 72.9 us
  other arithmetic: 16.8 us -> 61.9 us
    reduce_scatter x1 -> x0, waiting for transfers between devices: 1700 us -> none  [per_device(): lax.psum_scatter(lax.dot_general(pre_grad, weight_matrix, (((1,), (1,)),...]
    all_gather x1 -> x0, waiting for transfers between devices: 1060 us -> none  [per_device(): gathered = lax.all_gather(feature_rows, 'mp', axis=0, tiled=True)]
    ppermute x2 -> x47, waiting for transfers between devices: 15.2 us -> 512 us  [swapped(): return lax.ppermute(block, axis, [(i, i ^ mask) for i in range(count)])]
    psum x1 -> x0, waiting for transfers between devices: 359 us -> none  [per_device(): lax.psum((weight_grad, bias_grad, stitch_grad), 'batch')]
    dot_general x4 -> x51, matrix products: 132 us -> 218 us  [the longest x16 82.4 us: part(): return lax.dot_general(pg[o], w4[q], nt, preferred_element_type=F32)]
    ppermute x2 -> x47, starting transfers between devices: 0.56 us -> 59.7 us  [swapped(): return lax.ppermute(block, axis, [(i, i ^ mask) for i in range(count)])]
  transfers between devices with their start and end apart: 5 -> 47, of which waited for: 5 -> 26; matrix products, arithmetic and copies ran while one was open for 2% -> 29% of each run, Pallas kernels for 0% -> 0%
where the time goes in v1:
time: 932 us; the launch traced here: 927 us
  waiting for transfers between devices  512 us (55%)
  matrix products  218 us (23%)
  local copies, waits for them, and re-layouts  72.9 us (8%)
  other arithmetic  61.9 us (7%)
  starting transfers between devices  59.7 us (6%)
    ppermute x47, waiting for transfers between devices, swapped(): return lax.ppermute(block, axis, [(i, i ^ mask) for i in range(count)])  512 us
    dot_general x16, matrix products, part(): return lax.dot_general(pg[o], w4[q], nt, preferred_element_type=F32)  82.4 us
    ppermute x47, starting transfers between devices, swapped(): return lax.ppermute(block, axis, [(i, i ^ mask) for i in range(count)])  59.7 us
    unnamed x168, local copies, waits for them, and re-layouts  37.8 us
    dot_general x4, matrix products, dw_sent(): lax.dot_general(kq(x_all, q), pre_grad[:, cols:], tn, preferred_element_t...  34.2 us
    dot_general x4, matrix products, dw_kept(): lax.dot_general(kq(x_all, q), pre_grad[:, :cols], tn, preferred_element_t...  29.6 us
    dot_general x20, matrix products, dot_b(): r = jnp.dot(kq(block, q), b_cols(q), preferred_element_type=F32)  29.5 us
  transfers between devices with their start and end apart: 47, of which 26 were waited for; matrix products, arithmetic and copies ran while one was open for 29% of the time, Pallas kernels for 0%

profile of v1, /device:TPU:0, one launch (start us, length us, event | category | flops | bytes accessed | tf_op | source)
XLA Modules:
  0.0 927.1 jit_solution(14918948545255313582)
XLA Ops:
  44.5 42.5 %collective-permute-done.1 = bf16[192,9216]{1,0:T(8,128)(2,1)} collective-permute-done((bf16[192,9216]{1,0:T(8,128)(2,1)}, bf16[192,9216]{1,0:T(8,128)(2,1)}, u32[]{:S(2)}, u32[]{:S(2)}) %collective-permute-start.1) | collective-permute-done | bytes 3538976 | tf_op jit(solution)/shard_map/ppermute | solution.py:12
  87.0 26.7 %collective-permute-done.5 = bf16[192,9216]{1,0:T(8,128)(2,1)} collective-permute-done((bf16[192,9216]{1,0:T(8,128)(2,1)}, bf16[192,9216]{1,0:T(8,128)(2,1)}, u32[]{:S(2)}, u32[]{:S(2)}) %collective-permute-start.5) | collective-permute-done | bytes 3538976 | tf_op jit(solution)/shard_map/ppermute | solution.py:12
  123.7 90.9 %collective-permute-done.3 = bf16[2304,256]{1,0:T(8,128)(2,1)} collective-permute-done((bf16[2304,256]{1,0:T(8,128)(2,1)}, bf16[2304,256]{1,0:T(8,128)(2,1)}, u32[]{:S(2)}, u32[]{:S(2)}) %collective-permute-start.3) | collective-permute-done | bytes 1179680 | tf_op jit(solution)/shard_map/ppermute | solution.py:12
  229.1 11.8 %collective-permute-done.8 = bf16[2304,256]{1,0:T(8,128)(2,1)S(1)} collective-permute-done((bf16[2304,256]{1,0:T(8,128)(2,1)}, bf16[2304,256]{1,0:T(8,128)(2,1)S(1)}, u32[]{:S(2)}, u32[]{:S(2)}) %collective-permute-start.8) | collective-permute-done | bytes 1179680 | tf_op jit(solution)/shard_map/ppermute | solution.py:12
  247.2 7.8 fusion.164
  260.9 8.1 collective-permute-done.6
  277.9 9.8 %broadcast_add_fusion = (f32[384,512]{1,0:T(8,128)}, f32[384,512]{1,0:T(8,128)}, f32[384,512]{1,0:T(8,128)}) fusion(f32[512]{0:T(512)S(1)} %bitcast.142, f32[384,512]{1,0:T(8,128)} %fusion.164, f32[384,512]{1,0:T(8,128)S(1)} %copy-done.66, bf16[384,9216]{1,0:T(8,128)(2,1)} %get-tuple-element.205, bf16[9216,256]{1,0:T(8,128)(2,1)} %get-tuple-element.200, ...), kind=kOutput, calls=%fused_computation.191 | convolution fusion | flops 3643342848 | bytes 20449280 | tf_op jit(solution)/shard_map/dot_general | solution.py:183
  309.7 37.6 %collective-permute-done.10 = bf16[192,9216]{1,0:T(8,128)(2,1)S(1)} collective-permute-done((bf16[192,9216]{1,0:T(8,128)(2,1)}, bf16[192,9216]{1,0:T(8,128)(2,1)S(1)}, u32[]{:S(2)}, u32[]{:S(2)}) %collective-permute-start.10) | collective-permute-done | bytes 3538976 | tf_op jit(solution)/shard_map/ppermute | solution.py:12
  364.7 10.1 %collective-permute-done.15 = bf16[2304,256]{1,0:T(8,128)(2,1)S(1)} collective-permute-done((bf16[2304,256]{1,0:T(8,128)(2,1)}, bf16[2304,256]{1,0:T(8,128)(2,1)S(1)}, u32[]{:S(2)}, u32[]{:S(2)}) %collective-permute-start.15) | collective-permute-done | bytes 1179680 | tf_op jit(solution)/shard_map/ppermute | solution.py:12
  374.8 21.1 %collective-permute-done.13 = bf16[1024,512]{1,0:T(8,128)(2,1)} collective-permute-done((bf16[1024,512]{1,0:T(8,128)(2,1)}, bf16[1024,512]{1,0:T(8,128)(2,1)}, u32[]{:S(2)}, u32[]{:S(2)}) %collective-permute-start.13) | collective-permute-done | bytes 1048608 | tf_op jit(solution)/shard_map/ppermute | solution.py:12
  451.5 9.3 %fusion.40 = bf16[2304,512]{1,0:T(8,128)(2,1)} fusion(bf16[1536,9216]{1,0:T(8,128)(2,1)} %constant_dynamic-update-slice_fusion.12, bf16[1536,1024]{1,0:T(8,128)(2,1)S(1)} %get-tuple-element.181), kind=kOutput, calls=%fused_computation.52 | convolution fusion | flops 3625058304 | bytes 11010048 | tf_op jit(solution)/shard_map/dot_general | solution.py:262
  460.8 8.3 fusion.37
  486.0 8.3 fusion.46
  498.7 8.3 fusion.43
  507.7 12.3 %collective-permute-done.20 = bf16[384,2304]{1,0:T(8,128)(2,1)} collective-permute-done((bf16[384,2304]{1,0:T(8,128)(2,1)}, bf16[384,2304]{1,0:T(8,128)(2,1)}, u32[]{:S(2)}, u32[]{:S(2)}) %collective-permute-start.20) | collective-permute-done | bytes 1769504 | tf_op jit(solution)/shard_map/ppermute | solution.py:12
  525.6 9.0 collective-permute-done.23
  536.5 23.7 %collective-permute-done.22 = bf16[384,2304]{1,0:T(8,128)(2,1)S(1)} collective-permute-done((bf16[384,2304]{1,0:T(8,128)(2,1)}, bf16[384,2304]{1,0:T(8,128)(2,1)S(1)}, u32[]{:S(2)}, u32[]{:S(2)}) %collective-permute-start.22) | collective-permute-done | bytes 1769504 | tf_op jit(solution)/shard_map/ppermute | solution.py:12
  578.7 20.5 %collective-permute-done.24 = bf16[384,2304]{1,0:T(8,128)(2,1)S(1)} collective-permute-done((bf16[384,2304]{1,0:T(8,128)(2,1)S(1)}, bf16[384,2304]{1,0:T(8,128)(2,1)S(1)}, u32[]{:S(2)}, u32[]{:S(2)}) %collective-permute-start.24) | collective-permute-done | bytes 1769504 | tf_op jit(solution)/shard_map/ppermute | solution.py:12
  599.2 30.0 %collective-permute-done.21 = bf16[1536,512]{1,0:T(8,128)(2,1)S(1)} collective-permute-done((bf16[1536,512]{1,0:T(8,128)(2,1)S(1)}, bf16[1536,512]{1,0:T(8,128)(2,1)S(1)}, u32[]{:S(2)}, u32[]{:S(2)}) %collective-permute-start.21) | collective-permute-done | bytes 1572896 | tf_op jit(solution)/shard_map/ppermute | solution.py:12
  639.4 15.1 %collective-permute-done.26 = bf16[2304,256]{1,0:T(8,128)(2,1)} collective-permute-done((bf16[2304,256]{1,0:T(8,128)(2,1)}, bf16[2304,256]{1,0:T(8,128)(2,1)}, u32[]{:S(2)}, u32[]{:S(2)}) %collective-permute-start.26) | collective-permute-done | bytes 1179680 | tf_op jit(solution)/shard_map/ppermute | solution.py:12
  656.2 7.8 fusion.28
  664.1 9.3 %collective-permute-done.25 = bf16[384,2304]{1,0:T(8,128)(2,1)} collective-permute-done((bf16[384,2304]{1,0:T(8,128)(2,1)}, bf16[384,2304]{1,0:T(8,128)(2,1)}, u32[]{:S(2)}, u32[]{:S(2)}) %collective-permute-start.25) | collective-permute-done | bytes 1769504 | tf_op jit(solution)/shard_map/ppermute | solution.py:12
  689.5 18.2 %collective-permute-done.32 = bf16[2304,512]{1,0:T(8,128)(2,1)S(1)} collective-permute-done((bf16[2304,512]{1,0:T(8,128)(2,1)S(1)}, bf16[2304,512]{1,0:T(8,128)(2,1)S(1)}, u32[]{:S(2)}, u32[]{:S(2)}) %collective-permute-start.32) | collective-permute-done | bytes 2359328 | tf_op jit(solution)/shard_map/ppermute | solution.py:12
  709.4 24.9 %collective-permute-done.31 = bf16[2304,256]{1,0:T(8,128)(2,1)S(1)} collective-permute-done((bf16[2304,256]{1,0:T(8,128)(2,1)S(1)}, bf16[2304,256]{1,0:T(8,128)(2,1)S(1)}, u32[]{:S(2)}, u32[]{:S(2)}) %collective-permute-start.31) | collective-permute-done | bytes 1179680 | tf_op jit(solution)/shard_map/ppermute | solution.py:12
  736.6 7.8 fusion.31
  761.8 7.8 fusion.34
  769.6 25.9 %collective-permute-done.37 = bf16[2304,256]{1,0:T(8,128)(2,1)S(1)} collective-permute-done((bf16[2304,256]{1,0:T(8,128)(2,1)S(1)}, bf16[2304,256]{1,0:T(8,128)(2,1)S(1)}, u32[]{:S(2)}, u32[]{:S(2)}) %collective-permute-start.37) | collective-permute-done | bytes 1179680 | tf_op jit(solution)/shard_map/ppermute | solution.py:12
  795.5 12.7 %collective-permute-done.36 = bf16[384,2304]{1,0:T(8,128)(2,1)} collective-permute-done((bf16[384,2304]{1,0:T(8,128)(2,1)}, bf16[384,2304]{1,0:T(8,128)(2,1)}, u32[]{:S(2)}, u32[]{:S(2)}) %collective-permute-start.36) | collective-permute-done | bytes 1769504 | tf_op jit(solution)/shard_map/ppermute | solution.py:12
  823.0 15.3 %collective-permute-done.39 = bf16[2304,256]{1,0:T(8,128)(2,1)} collective-permute-done((bf16[2304,256]{1,0:T(8,128)(2,1)}, bf16[2304,256]{1,0:T(8,128)(2,1)}, u32[]{:S(2)}, u32[]{:S(2)}) %collective-permute-start.39) | collective-permute-done | bytes 1179680 | tf_op jit(solution)/shard_map/ppermute | solution.py:12
  842.3 11.9 %collective-permute-done.38 = bf16[384,2304]{1,0:T(8,128)(2,1)} collective-permute-done((bf16[384,2304]{1,0:T(8,128)(2,1)}, bf16[384,2304]{1,0:T(8,128)(2,1)}, u32[]{:S(2)}, u32[]{:S(2)}) %collective-permute-start.38) | collective-permute-done | bytes 1769504 | tf_op jit(solution)/shard_map/ppermute | solution.py:12
  872.3 16.4 %collective-permute-done.40 = bf16[384,2304]{1,0:T(8,128)(2,1)} collective-permute-done((bf16[384,2304]{1,0:T(8,128)(2,1)}, bf16[384,2304]{1,0:T(8,128)(2,1)}, u32[]{:S(2)}, u32[]{:S(2)}) %collective-permute-start.40) | collective-permute-done | bytes 1769504 | tf_op jit(solution)/shard_map/ppermute | solution.py:12
  902.3 18.3 %maximum_bitcast_fusion = f32[1,9216,512]{2,1,0:T(8,128)} fusion(f32[2304,512]{1,0:T(8,128)S(1)} %maximum_select_fusion.3, f32[2304,512]{1,0:T(8,128)S(1)} %maximum_select_fusion.2, f32[2304,512]{1,0:T(8,128)S(1)} %maximum_select_fusion.1, f32[2304,512]{1,0:T(8,128)S(1)} %maximum_select_fusion), kind=kLoop, calls=%fused_computation.1 | loop fusion | flops 14155776 | bytes 37748736 | tf_op jit(solution)/shard_map/broadcast_in_dim | solution.py:379
  (367 shorter events, 337.2 us)
Async XLA Ops:
  7.1 79.8 %collective-permute-start.1 = (bf16[192,9216]{1,0:T(8,128)(2,1)}, bf16[192,9216]{1,0:T(8,128)(2,1)}, u32[]{:S(2)}, u32[]{:S(2)}) collective-permute-start(bf16[192,9216]{1,0:T(8,128)(2,1)} %get-tuple-element.202), channel_id=1, source_target_pairs={{0,1},{1,0},{2,3},{3,2},{4,5},{5,4},{6,7},{7,6},{8,9},{9,8},{10,11... | collective-permute-start | bytes 10616840 | tf_op jit(solution)/shard_map/ppermute | solution.py:12
  10.1 103.6 %collective-permute-start.5 = (bf16[192,9216]{1,0:T(8,128)(2,1)}, bf16[192,9216]{1,0:T(8,128)(2,1)}, u32[]{:S(2)}, u32[]{:S(2)}) collective-permute-start(bf16[192,9216]{1,0:T(8,128)(2,1)} %get-tuple-element.202), channel_id=1, source_target_pairs={{0,2},{1,3},{2,0},{3,1},{4,6},{5,7},{6,4},{7,5},{8,10},{9,11},{10,... | collective-permute-start | bytes 10616840 | tf_op jit(solution)/shard_map/ppermute | solution.py:12
  19.2 104.5 %collective-permute-start.4 = (bf16[2304,256]{1,0:T(8,128)(2,1)}, bf16[2304,256]{1,0:T(8,128)(2,1)}, u32[]{:S(2)}, u32[]{:S(2)}) collective-permute-start(bf16[2304,256]{1,0:T(8,128)(2,1)} %get-tuple-element.196), channel_id=1, source_target_pairs={{0,4},{1,5},{2,6},{3,7},{4,0},{5,1},{6,2},{7,3},{8,12},{9,13},{10,... | collective-permute-start | bytes 3538952 | tf_op jit(solution)/shard_map/ppermute | solution.py:12
  21.8 94.4 %collective-permute-start = (f32[512]{0:T(512)S(1)}, f32[512]{0:T(512)S(1)}, u32[]{:S(2)}, u32[]{:S(2)}) collective-permute-start(f32[512]{0:T(512)S(1)} %bitcast.140), channel_id=1, source_target_pairs={{0,16},{16,0},{1,17},{17,1},{2,18},{18,2},{3,19},{19,3},{4,20},{20... | collective-permute-start | bytes 6152 | tf_op jit(solution)/shard_map/ppermute | solution.py:12
  26.8 95.4 %collective-permute-start.18 = (bf16[1536,512]{1,0:T(8,128)(2,1)}, bf16[1536,512]{1,0:T(8,128)(2,1)}, u32[]{:S(2)}, u32[]{:S(2)}) collective-permute-start(bf16[1536,512]{1,0:T(8,128)(2,1)} %fusion.54), channel_id=1, source_target_pairs={{0,16},{16,0},{1,17},{17,1},{2,18},{18,2},{3,19},{19,3},{4,20},{20... | collective-permute-start | bytes 4718600 | tf_op jit(solution)/shard_map/ppermute | solution.py:12
  113.7 115.4 %collective-permute-start.2 = (bf16[192,9216]{1,0:T(8,128)(2,1)}, bf16[192,9216]{1,0:T(8,128)(2,1)}, u32[]{:S(2)}, u32[]{:S(2)}) collective-permute-start(bf16[192,9216]{1,0:T(8,128)(2,1)} %get-tuple-element.90), channel_id=1, source_target_pairs={{0,1},{1,0},{2,3},{3,2},{4,5},{5,4},{6,7},{7,6},{8,9},{9,8},{10,11... | collective-permute-start | bytes 10616840 | tf_op jit(solution)/shard_map/ppermute | solution.py:12
  114.1 126.8 %collective-permute-start.7 = (bf16[192,9216]{1,0:T(8,128)(2,1)}, bf16[192,9216]{1,0:T(8,128)(2,1)}, u32[]{:S(2)}, u32[]{:S(2)}) collective-permute-start(bf16[192,9216]{1,0:T(8,128)(2,1)} %get-tuple-element.90), channel_id=1, source_target_pairs={{0,2},{1,3},{2,0},{3,1},{4,6},{5,7},{6,4},{7,5},{8,10},{9,11},{10,... | collective-permute-start | bytes 10616840 | tf_op jit(solution)/shard_map/ppermute | solution.py:12
  116.2 98.4 %collective-permute-start.3 = (bf16[2304,256]{1,0:T(8,128)(2,1)}, bf16[2304,256]{1,0:T(8,128)(2,1)}, u32[]{:S(2)}, u32[]{:S(2)}) collective-permute-start(bf16[2304,256]{1,0:T(8,128)(2,1)} %get-tuple-element.197), channel_id=1, source_target_pairs={{0,4},{1,5},{2,6},{3,7},{4,0},{5,1},{6,2},{7,3},{8,12},{9,13},{10,... | collective-permute-start | bytes 3538952 | tf_op jit(solution)/shard_map/ppermute | solution.py:12
  216.0 53.0 %collective-permute-start.6 = (bf16[2304,256]{1,0:T(8,128)(2,1)S(1)}, bf16[2304,256]{1,0:T(8,128)(2,1)S(1)}, u32[]{:S(2)}, u32[]{:S(2)}) collective-permute-start(bf16[2304,256]{1,0:T(8,128)(2,1)S(1)} %copy-done.12), channel_id=1, source_target_pairs={{0,4},{1,5},{2,6},{3,7},{4,0},{5,1},{6,2},{7,3},{8,12},{9,13},{10,... | collective-permute-start | bytes 3538952 | tf_op jit(solution)/shard_map/ppermute | solution.py:12
  270.5 76.8 %collective-permute-start.10 = (bf16[192,9216]{1,0:T(8,128)(2,1)}, bf16[192,9216]{1,0:T(8,128)(2,1)S(1)}, u32[]{:S(2)}, u32[]{:S(2)}) collective-permute-start(bf16[192,9216]{1,0:T(8,128)(2,1)} %collective-permute-done.5), channel_id=1, source_target_pairs={{0,1},{1,0},{2,3},{3,2},{4,5},{5,4},{6,7},{7,6},{8,9},{9,8},{10,11... | collective-permute-start | bytes 10616840 | tf_op jit(solution)/shard_map/ppermute | solution.py:12
  272.0 75.3 %collective-permute-start.9 = (bf16[2304,256]{1,0:T(8,128)(2,1)S(1)}, bf16[2304,256]{1,0:T(8,128)(2,1)}, u32[]{:S(2)}, u32[]{:S(2)}) collective-permute-start(bf16[2304,256]{1,0:T(8,128)(2,1)S(1)} %copy-done.7), channel_id=1, source_target_pairs={{0,4},{1,5},{2,6},{3,7},{4,0},{5,1},{6,2},{7,3},{8,12},{9,13},{10,... | collective-permute-start | bytes 3538952 | tf_op jit(solution)/shard_map/ppermute | solution.py:12
  295.3 54.0 %collective-permute-start.14 = (bf16[2304,256]{1,0:T(8,128)(2,1)S(1)}, bf16[2304,256]{1,0:T(8,128)(2,1)S(1)}, u32[]{:S(2)}, u32[]{:S(2)}) collective-permute-start(bf16[2304,256]{1,0:T(8,128)(2,1)S(1)} %collective-permute-done.6), channel_id=1, source_target_pairs={{0,8},{8,0},{1,9},{9,1},{2,10},{10,2},{3,11},{11,3},{4,12},{12,4},... | collective-permute-start | bytes 3538952 | tf_op jit(solution)/shard_map/ppermute | solution.py:12
  349.8 46.1 %collective-permute-start.13 = (bf16[1024,512]{1,0:T(8,128)(2,1)}, bf16[1024,512]{1,0:T(8,128)(2,1)}, u32[]{:S(2)}, u32[]{:S(2)}) collective-permute-start(bf16[1024,512]{1,0:T(8,128)(2,1)} %pad_maximum_fusion.11), channel_id=1, source_target_pairs={{0,4},{1,5},{2,6},{3,7},{4,0},{5,1},{6,2},{7,3},{8,12},{9,13},{10,... | collective-permute-start | bytes 3145736 | tf_op jit(solution)/shard_map/ppermute | solution.py:12
  349.9 46.1 %collective-permute-start.12 = (f32[4,512]{1,0:T(4,128)S(1)}, f32[4,512]{1,0:T(4,128)S(1)}, u32[]{:S(2)}, u32[]{:S(2)}) collective-permute-start(f32[4,512]{1,0:T(4,128)S(1)} %pad_maximum_fusion.16), channel_id=1, source_target_pairs={{0,4},{1,5},{2,6},{3,7},{4,0},{5,1},{6,2},{7,3},{8,12},{9,13},{10,... | collective-permute-start | bytes 24584 | tf_op jit(solution)/shard_map/ppermute | solution.py:12
  354.8 84.5 %collective-permute-start.16 = (bf16[192,9216]{1,0:T(8,128)(2,1)}, bf16[192,9216]{1,0:T(8,128)(2,1)S(1)}, u32[]{:S(2)}, u32[]{:S(2)}) collective-permute-start(bf16[192,9216]{1,0:T(8,128)(2,1)} %collective-permute-done.7), channel_id=1, source_target_pairs={{0,1},{1,0},{2,3},{3,2},{4,5},{5,4},{6,7},{7,6},{8,9},{9,8},{10,11... | collective-permute-start | bytes 10616840 | tf_op jit(solution)/shard_map/ppermute | solution.py:12
  480.7 53.9 %collective-permute-start.23 = (bf16[2304,512]{1,0:T(8,128)(2,1)}, bf16[2304,512]{1,0:T(8,128)(2,1)S(1)}, u32[]{:S(2)}, u32[]{:S(2)}) collective-permute-start(bf16[2304,512]{1,0:T(8,128)(2,1)} %fusion.37), channel_id=1, source_target_pairs={{0,8},{8,0},{1,9},{9,1},{2,10},{10,2},{3,11},{11,3},{4,12},{12,4},... | collective-permute-start | bytes 7077896 | tf_op jit(solution)/shard_map/ppermute | solution.py:12
  534.6 94.6 %collective-permute-start.21 = (bf16[1536,512]{1,0:T(8,128)(2,1)S(1)}, bf16[1536,512]{1,0:T(8,128)(2,1)S(1)}, u32[]{:S(2)}, u32[]{:S(2)}) collective-permute-start(bf16[1536,512]{1,0:T(8,128)(2,1)S(1)} %pad_maximum_fusion.10), channel_id=1, source_target_pairs={{0,4},{1,5},{2,6},{3,7},{4,0},{5,1},{6,2},{7,3},{8,12},{9,13},{10,... | collective-permute-start | bytes 4718600 | tf_op jit(solution)/shard_map/ppermute | solution.py:12
  568.0 71.3 %collective-permute-start.27 = (bf16[2304,512]{1,0:T(8,128)(2,1)}, bf16[2304,512]{1,0:T(8,128)(2,1)}, u32[]{:S(2)}, u32[]{:S(2)}) collective-permute-start(bf16[2304,512]{1,0:T(8,128)(2,1)} %fusion.40), channel_id=1, source_target_pairs={{0,8},{8,0},{1,9},{9,1},{2,10},{10,2},{3,11},{11,3},{4,12},{12,4},... | collective-permute-start | bytes 7077896 | tf_op jit(solution)/shard_map/ppermute | solution.py:12
  571.0 83.5 %collective-permute-start.26 = (bf16[2304,256]{1,0:T(8,128)(2,1)}, bf16[2304,256]{1,0:T(8,128)(2,1)}, u32[]{:S(2)}, u32[]{:S(2)}) collective-permute-start(bf16[2304,256]{1,0:T(8,128)(2,1)} %slice.701), channel_id=1, source_target_pairs={{0,4},{1,5},{2,6},{3,7},{4,0},{5,1},{6,2},{7,3},{8,12},{9,13},{10,... | collective-permute-start | bytes 3538952 | tf_op jit(solution)/shard_map/ppermute | solution.py:12
  576.9 96.5 %collective-permute-start.25 = (bf16[384,2304]{1,0:T(8,128)(2,1)}, bf16[384,2304]{1,0:T(8,128)(2,1)}, u32[]{:S(2)}, u32[]{:S(2)}) collective-permute-start(bf16[384,2304]{1,0:T(8,128)(2,1)} %add_convert_fusion.7), channel_id=1, source_target_pairs={{0,2},{1,3},{2,0},{3,1},{4,6},{5,7},{6,4},{7,5},{8,10},{9,11},{10,... | collective-permute-start | bytes 5308424 | tf_op jit(solution)/shard_map/ppermute | solution.py:12
  629.2 55.3 %collective-permute-start.28 = (bf16[384,2304]{1,0:T(8,128)(2,1)}, bf16[384,2304]{1,0:T(8,128)(2,1)}, u32[]{:S(2)}, u32[]{:S(2)}) collective-permute-start(bf16[384,2304]{1,0:T(8,128)(2,1)} %convolution_convert_fusion.2), channel_id=1, source_target_pairs={{0,1},{1,0},{2,3},{3,2},{4,5},{5,4},{6,7},{7,6},{8,9},{9,8},{10,11... | collective-permute-start | bytes 5308424 | tf_op jit(solution)/shard_map/ppermute | solution.py:12
  654.5 53.1 %collective-permute-start.32 = (bf16[2304,512]{1,0:T(8,128)(2,1)S(1)}, bf16[2304,512]{1,0:T(8,128)(2,1)S(1)}, u32[]{:S(2)}, u32[]{:S(2)}) collective-permute-start(bf16[2304,512]{1,0:T(8,128)(2,1)S(1)} %copy-done.59), channel_id=1, source_target_pairs={{0,8},{8,0},{1,9},{9,1},{2,10},{10,2},{3,11},{11,3},{4,12},{12,4},... | collective-permute-start | bytes 7077896 | tf_op jit(solution)/shard_map/ppermute | solution.py:12
  673.4 63.2 %collective-permute-start.30 = (bf16[384,2304]{1,0:T(8,128)(2,1)}, bf16[384,2304]{1,0:T(8,128)(2,1)}, u32[]{:S(2)}, u32[]{:S(2)}) collective-permute-start(bf16[384,2304]{1,0:T(8,128)(2,1)} %add_convert_fusion.5), channel_id=1, source_target_pairs={{0,2},{1,3},{2,0},{3,1},{4,6},{5,7},{6,4},{7,5},{8,10},{9,11},{10,... | collective-permute-start | bytes 5308424 | tf_op jit(solution)/shard_map/ppermute | solution.py:12
  676.0 58.3 %collective-permute-start.31 = (bf16[2304,256]{1,0:T(8,128)(2,1)S(1)}, bf16[2304,256]{1,0:T(8,128)(2,1)S(1)}, u32[]{:S(2)}, u32[]{:S(2)}) collective-permute-start(bf16[2304,256]{1,0:T(8,128)(2,1)S(1)} %slice.700), channel_id=1, source_target_pairs={{0,4},{1,5},{2,6},{3,7},{4,0},{5,1},{6,2},{7,3},{8,12},{9,13},{10,... | collective-permute-start | bytes 3538952 | tf_op jit(solution)/shard_map/ppermute | solution.py:12
  684.5 64.5 %collective-permute-start.29 = (bf16[384,2304]{1,0:T(8,128)(2,1)}, bf16[384,2304]{1,0:T(8,128)(2,1)}, u32[]{:S(2)}, u32[]{:S(2)}) collective-permute-start(bf16[384,2304]{1,0:T(8,128)(2,1)} %convolution_convert_fusion.3), channel_id=1, source_target_pairs={{0,1},{1,0},{2,3},{3,2},{4,5},{5,4},{6,7},{7,6},{8,9},{9,8},{10,11... | collective-permute-start | bytes 5308424 | tf_op jit(solution)/shard_map/ppermute | solution.py:12
  707.6 52.5 %collective-permute-start.34 = (bf16[2304,512]{1,0:T(8,128)(2,1)S(1)}, bf16[2304,512]{1,0:T(8,128)(2,1)}, u32[]{:S(2)}, u32[]{:S(2)}) collective-permute-start(bf16[2304,512]{1,0:T(8,128)(2,1)S(1)} %copy-done.58), channel_id=1, source_target_pairs={{0,8},{8,0},{1,9},{9,1},{2,10},{10,2},{3,11},{11,3},{4,12},{12,4},... | collective-permute-start | bytes 7077896 | tf_op jit(solution)/shard_map/ppermute | solution.py:12
  744.6 51.0 %collective-permute-start.37 = (bf16[2304,256]{1,0:T(8,128)(2,1)S(1)}, bf16[2304,256]{1,0:T(8,128)(2,1)S(1)}, u32[]{:S(2)}, u32[]{:S(2)}) collective-permute-start(bf16[2304,256]{1,0:T(8,128)(2,1)S(1)} %slice.699), channel_id=1, source_target_pairs={{0,4},{1,5},{2,6},{3,7},{4,0},{5,1},{6,2},{7,3},{8,12},{9,13},{10,... | collective-permute-start | bytes 3538952 | tf_op jit(solution)/shard_map/ppermute | solution.py:12
  745.7 62.5 %collective-permute-start.36 = (bf16[384,2304]{1,0:T(8,128)(2,1)}, bf16[384,2304]{1,0:T(8,128)(2,1)}, u32[]{:S(2)}, u32[]{:S(2)}) collective-permute-start(bf16[384,2304]{1,0:T(8,128)(2,1)} %add_convert_fusion.4), channel_id=1, source_target_pairs={{0,2},{1,3},{2,0},{3,1},{4,6},{5,7},{6,4},{7,5},{8,10},{9,11},{10,... | collective-permute-start | bytes 5308424 | tf_op jit(solution)/shard_map/ppermute | solution.py:12
  754.2 59.5 %collective-permute-start.33 = (bf16[384,2304]{1,0:T(8,128)(2,1)}, bf16[384,2304]{1,0:T(8,128)(2,1)}, u32[]{:S(2)}, u32[]{:S(2)}) collective-permute-start(bf16[384,2304]{1,0:T(8,128)(2,1)} %convolution_convert_fusion.4), channel_id=1, source_target_pairs={{0,1},{1,0},{2,3},{3,2},{4,5},{5,4},{6,7},{7,6},{8,9},{9,8},{10,11... | collective-permute-start | bytes 5308424 | tf_op jit(solution)/shard_map/ppermute | solution.py:12
  760.1 53.4 %collective-permute-start.35 = (bf16[2304,256]{1,0:T(8,128)(2,1)S(1)}, bf16[2304,256]{1,0:T(8,128)(2,1)S(1)}, u32[]{:S(2)}, u32[]{:S(2)}) collective-permute-start(bf16[2304,256]{1,0:T(8,128)(2,1)S(1)} %get-tuple-element.143), channel_id=1, source_target_pairs={{0,8},{8,0},{1,9},{9,1},{2,10},{10,2},{3,11},{11,3},{4,12},{12,4},... | collective-permute-start | bytes 3538952 | tf_op jit(solution)/shard_map/ppermute | solution.py:12
  809.4 50.8 %collective-permute-start.43 = (bf16[2304,256]{1,0:T(8,128)(2,1)}, bf16[2304,256]{1,0:T(8,128)(2,1)}, u32[]{:S(2)}, u32[]{:S(2)}) collective-permute-start(bf16[2304,256]{1,0:T(8,128)(2,1)} %slice.698), channel_id=1, source_target_pairs={{0,4},{1,5},{2,6},{3,7},{4,0},{5,1},{6,2},{7,3},{8,12},{9,13},{10,... | collective-permute-start | bytes 3538952 | tf_op jit(solution)/shard_map/ppermute | solution.py:12
  810.4 61.2 %collective-permute-start.41 = (bf16[384,2304]{1,0:T(8,128)(2,1)}, bf16[384,2304]{1,0:T(8,128)(2,1)}, u32[]{:S(2)}, u32[]{:S(2)}) collective-permute-start(bf16[384,2304]{1,0:T(8,128)(2,1)} %add_convert_fusion.1), channel_id=1, source_target_pairs={{0,2},{1,3},{2,0},{3,1},{4,6},{5,7},{6,4},{7,5},{8,10},{9,11},{10,... | collective-permute-start | bytes 5308424 | tf_op jit(solution)/shard_map/ppermute | solution.py:12
  (94 other events, 1681.4 us)

commit v2 on v0

--- a/solution.py
+++ b/solution.py
@@ -1,20 +1,22 @@
+import functools
+
 import jax
 import jax.numpy as jnp
 from jax import lax
+from jax.experimental import pallas as pl
+from jax.experimental.pallas import tpu as pltpu
 from jax.sharding import PartitionSpec as P
 
-
-def swapped(block, axis, bit):
+BF = jnp.bfloat16
+F32 = jnp.float32
+
+
+def swapped(block, axis, mask):
     count = lax.axis_size(axis)
-    route = []
-    for low in range(count):
-        high = low | 1 << bit
-        if high != low and high < count:
-            route += [(low, high), (high, low)]
-    return lax.ppermute(block, axis, route)
-
-
-def per_device(acts, fc_weight, fc_bias, stitch, image_grad, crop_counts, row_image, row_live):
+    return lax.ppermute(block, axis, [(i, i ^ mask) for i in range(count)])
+
+
+def general(acts, fc_weight, fc_bias, stitch, image_grad, crop_counts, row_image, row_live):
     feature_rows = acts[0]
     weight_matrix = fc_weight[0]
     layer_bias = fc_bias[0].astype(jnp.float32)
@@ -29,7 +31,7 @@
     tower = lax.axis_index("tower")
     self_coefficient = jnp.where(tower == 0, coefs[0], coefs[1])
     other_coef = jnp.where(tower == 0, coefs[1], coefs[0])
-    partner = swapped(hidden, "tower", 0)
+    partner = swapped(hidden, "tower", 1)
     hidden_wide = hidden.astype(jnp.float32)
     partner_wide = partner.astype(jnp.float32)
     stitched = self_coefficient[None, :] * hidden_wide + other_coef[None, :] * partner_wide
@@ -43,7 +45,7 @@
     picked = jnp.dot(match.astype(jnp.bfloat16), grads_img, preferred_element_type=jnp.float32)
     out_grad = (picked * row_weighting_scale[:, None]).astype(jnp.bfloat16)
     out_wide = out_grad.astype(jnp.float32)
-    returned = swapped(other_coef[None, :] * out_wide, "tower", 0)
+    returned = swapped(other_coef[None, :] * out_wide, "tower", 1)
     hidden_grad = (self_coefficient[None, :] * out_wide + returned).astype(jnp.bfloat16)
     pre_grad = jnp.where(active, hidden_grad, jnp.zeros_like(hidden_grad))
     own_stitch = jnp.sum(out_wide * hidden_wide, axis=0)
@@ -69,6 +71,540 @@
         input_grad.astype(jnp.bfloat16)[None],
         weight_grad[None],
         bias_grad[None],
+        stitch_grad[None],
+    )
+
+STEPS = (
+    "+y0", "+z0", "z0", "+z1", "+p0", "+d0", "+o", "+a", "z1", "+z2", "+d1", "p0",
+    "+x0", "+p1", "o", "a", "y0", "d0", "x0", "F01", "p1", "+x1", "+p2", "z2",
+    "+d2", "p2", "+x2", "+g", "+m", "x1", "F12", "d1", "D02", "x2", "F23", "D23",
+    "g", "m", "+b", "d2", "E03", "b", "hg",
+)
+
+NT = (((1,), (1,)), ((), ()))
+TN = (((0,), (0,)), ((), ()))
+LIGHT = pl.CostEstimate(flops=1000, bytes_accessed=1000, transcendentals=0)
+
+
+def forward_body(n_x, starts, has_acc, *refs):
+    xs, rest = refs[:n_x], list(refs[n_x:])
+    w_m, w_o = rest.pop(0), rest.pop(0)
+    n_q = len(starts) - 1
+    ps = [rest.pop(0) for _ in range(n_q)]
+    gs = [rest.pop(0) for _ in range(n_q)]
+    acc_in = rest.pop(0) if has_acc else None
+    out = rest[0]
+    i = pl.program_id(0)
+    half = w_m.shape[1]
+
+    @pl.when(i == 0)
+    def _():
+        if has_acc:
+            out[...] = acc_in[...]
+        else:
+            out[...] = jnp.zeros_like(out)
+
+    for q in range(n_q):
+
+        @pl.when((i >= starts[q]) & (i < starts[q + 1]))
+        def _():
+            lo = 0
+            for x in xs:
+                rows = x.shape[0]
+                for j, w in enumerate((w_m, ps[q], w_o, gs[q])):
+                    out[lo : lo + rows, j * half : (j + 1) * half] += jnp.dot(
+                        x[...], w[...], preferred_element_type=F32
+                    )
+                lo += rows
+
+
+def forward(xs, w_m, w_o, ps, gs, lo, block, acc=None):
+    starts = [0]
+    for p in ps:
+        starts.append(starts[-1] + p.shape[0] // block)
+    rows = sum(x.shape[0] for x in xs)
+    half = w_m.shape[1]
+    operands = [*xs, w_m, w_o, *ps, *gs]
+    specs = [pl.BlockSpec((x.shape[0], block), lambda i: (0, lo + i)) for x in xs]
+    specs += [pl.BlockSpec((block, half), lambda i: (lo + i, 0))] * 2
+    for a, e in [*zip(starts, starts[1:])] * 2:
+        specs.append(
+            pl.BlockSpec((block, half), lambda i, a=a, e=e: (jnp.clip(i - a, 0, e - a - 1), 0))
+        )
+    wide = pl.BlockSpec((rows, 4 * half), lambda i: (0, 0))
+    if acc is not None:
+        operands.append(acc)
+        specs.append(wide)
+    return pl.pallas_call(
+        functools.partial(forward_body, len(xs), starts, acc is not None),
+        out_shape=jax.ShapeDtypeStruct((rows, 4 * half), F32),
+        grid=(starts[-1],),
+        in_specs=specs,
+        out_specs=wide,
+        cost_estimate=LIGHT,
+    )(*operands)
+
+
+def activate_body(bounds, *refs):
+    accs, rest = refs[: len(bounds)], refs[len(bounds) :]
+    bias, hg, hid, pre_grad = rest
+    i = pl.program_id(0)
+    for acc, (lo, hi) in zip(accs, bounds):
+
+        @pl.when((i >= lo) & (i < hi))
+        def _():
+            pre = acc[...] + bias[...]
+            hid[...] = jnp.maximum(pre, 0.0).astype(BF)
+            pre_grad[...] = jnp.where(pre > 0, hg[...], jnp.zeros_like(hg))
+
+
+def activate(accs, bias, hg, rows):
+    wide = hg.shape[1]
+    bounds, lo = [], 0
+    for acc in accs:
+        bounds.append((lo, lo + acc.shape[0] // rows))
+        lo = bounds[-1][1]
+    specs = [
+        pl.BlockSpec((rows, wide), lambda i, lo=lo, hi=hi: (jnp.clip(i - lo, 0, hi - lo - 1), 0))
+        for lo, hi in bounds
+    ]
+    at = pl.BlockSpec((rows, wide), lambda i: (i, 0))
+    return pl.pallas_call(
+        functools.partial(activate_body, bounds),
+        out_shape=(jax.ShapeDtypeStruct(hg.shape, BF),) * 2,
+        grid=(bounds[-1][1],),
+        in_specs=[*specs, pl.BlockSpec((1, wide), lambda i: (0, 0)), at],
+        out_specs=[at, at],
+        cost_estimate=LIGHT,
+    )(*accs, bias, hg)
+
+
+def nt_body(n_p, n_w, n_add, *refs):
+    ps, ws = refs[:n_p], refs[n_p : n_p + n_w]
+    adds, out = refs[n_p + n_w : n_p + n_w + n_add], refs[-1]
+    weights = jnp.concatenate([w[...] for w in ws], 1)
+    rows = ps[0].shape[0]
+    for j, p in enumerate(ps):
+        r = lax.dot_general(p[...], weights, NT, preferred_element_type=F32)
+        for a in adds:
+            r = r + a[...].astype(F32)
+        out[j * rows : (j + 1) * rows, :] = r.astype(BF)
+
+
+def nt_product(pre_grad, picks, ws, adds, rows, width, block, into=None):
+    steps = width // block
+    operands, specs = [], []
+    for o in picks:
+        operands.append(pre_grad)
+        specs.append(pl.BlockSpec((rows, pre_grad.shape[1]), lambda i, o=o: (o, 0)))
+    for w, lo in ws:
+        operands.append(w)
+        specs.append(pl.BlockSpec((block, w.shape[1]), lambda i, lo=lo: (lo + i, 0)))
+    for a, r, lo in adds:
+        operands.append(a)
+        specs.append(pl.BlockSpec((rows, block), lambda i, r=r, lo=lo: (r, lo + i)))
+    body = functools.partial(nt_body, len(picks), len(ws), len(adds))
+    height = rows * len(picks)
+    shape, first, alias = (height, width), 0, {}
+    if into is not None:
+        held, shape, first = into
+        if held is not None:
+            alias = {len(operands): 0}
+            operands.append(held)
+            specs.append(pl.BlockSpec(memory_space=pl.ANY))
+            inner = body
+
+            def body(*refs):
+                inner(*refs[:-2], refs[-1])
+
+    return pl.pallas_call(
+        body,
+        out_shape=jax.ShapeDtypeStruct(shape, BF),
+        grid=(steps,),
+        in_specs=specs,
+        out_specs=pl.BlockSpec((height, block), lambda i: (0, first + i)),
+        input_output_aliases=alias,
+        cost_estimate=LIGHT,
+    )(*operands)
+
+
+def sent_body(n_x, *refs):
+    block = jnp.concatenate([x[...] for x in refs[:n_x]], 0)
+    p, out = refs[n_x], refs[n_x + 1]
+    out[...] = lax.dot_general(block, p[...], TN, preferred_element_type=F32).astype(BF)
+
+
+def kept_body(n_x, *refs):
+    block = jnp.concatenate([x[...] for x in refs[:n_x]], 0)
+    p, got, near, far = refs[n_x:]
+    r = lax.dot_general(block, p[...], TN, preferred_element_type=F32) + got[...].astype(F32)
+    half = near.shape[1]
+    near[...] = r[:, :half]
+    far[...] = r[:, half:].astype(BF)
+
+
+def tn_product(xs, pre_grad, side, lo, width, block, got=None):
+    cols = pre_grad.shape[1] // 2
+    steps = width // block
+    operands = [*xs, pre_grad]
+    specs = [pl.BlockSpec((x.shape[0], block), lambda i: (0, lo + i)) for x in xs]
+    specs.append(pl.BlockSpec((pre_grad.shape[0], cols), lambda i: (0, side)))
+    if got is None:
+        body = functools.partial(sent_body, len(xs))
+        outs = jax.ShapeDtypeStruct((width, cols), BF)
+        out_specs = pl.BlockSpec((block, cols), lambda i: (i, 0))
+    else:
+        body = functools.partial(kept_body, len(xs))
+        operands.append(got)
+        specs.append(pl.BlockSpec((block, cols), lambda i: (i, 0)))
+        half = cols // 2
+        outs = (
+            jax.ShapeDtypeStruct((width, half), F32),
+            jax.ShapeDtypeStruct((width, half), BF),
+        )
+        out_specs = [pl.BlockSpec((block, half), lambda i: (i, 0))] * 2
+    return pl.pallas_call(
+        body,
+        out_shape=outs,
+        grid=(steps,),
+        in_specs=specs,
+        out_specs=out_specs,
+        cost_estimate=LIGHT,
+    )(*operands)
+
+
+def add_body(near, got, out):
+    out[...] = (near[...] + got[...].astype(F32)).astype(BF)
+
+
+def finished(near, got):
+    width, half = near.shape
+    spec = pl.BlockSpec((width // 2, half), lambda i: (i, 0))
+    return pl.pallas_call(
+        add_body,
+        out_shape=jax.ShapeDtypeStruct((width, half), BF),
+        grid=(2,),
+        in_specs=[spec, spec],
+        out_specs=spec,
+        cost_estimate=LIGHT,
+    )(near, got)
+
+
+def place_body(b, near, got, other, *rest):
+    out = rest[-1]
+    half = near.shape[1]
+    total = near[...] + got[...].astype(F32)
+    wide = other[...].astype(F32)
+    first = b[0] == 0
+    out[:, :half] = jnp.where(first, total, wide)
+    out[:, half:] = jnp.where(first, wide, total)
+
+
+def place(b, near, got, other, held, depth, at):
+    width, half = near.shape
+    spec = pl.BlockSpec((width // 2, half), lambda i, b: (i, 0))
+    operands, specs, alias = [near, got, other], [spec] * 3, {}
+    if held is not None:
+        alias = {4: 0}
+        operands.append(held)
+        specs.append(pl.BlockSpec(memory_space=pl.ANY))
+    return pl.pallas_call(
+        place_body,
+        out_shape=jax.ShapeDtypeStruct((depth, 2 * half), F32),
+        grid_spec=pltpu.PrefetchScalarGridSpec(
+            num_scalar_prefetch=1,
+            grid=(2,),
+            in_specs=specs,
+            out_specs=pl.BlockSpec((width // 2, 2 * half), lambda i, b: (2 * at + i, 0)),
+        ),
+        input_output_aliases=alias,
+        cost_estimate=LIGHT,
+    )(b, *operands)
+
+
+def squares(acts, fc_weight, fc_bias, stitch, image_grad, crop_counts, row_image, row_live):
+    x = acts[0]
+    w = fc_weight[0]
+    rows, depth = x.shape
+    cols = w.shape[1]
+    half = cols // 2
+    me = lax.axis_index("mp")
+    b = lax.axis_index("batch")
+    tower = lax.axis_index("tower")
+    nk = 6
+    dk = depth // nk
+    wat = [0, 3, 5, 6]
+    nw = len(wat) - 1
+    block = 512 if dk % 512 == 0 else dk
+
+    token = []
+
+    def tie(v, *deps):
+        deps = [d for d in (*deps, *token) if d is not None]
+        return lax.optimization_barrier((v, *deps))[0] if deps else v
+
+    def wait(v):
+        v = tie(v)
+        token[:] = [v]
+        return v
+
+    def lane(axis, mask):
+        return lambda v, *deps: swapped(tie(v, *deps), axis, mask)
+
+    sy = lane("mp", 1)
+    sz = lane("mp", 2)
+    sp = lane("mp", 4)
+    sx = lane("batch", 1)
+    st = lane("tower", 1)
+
+    def mine(v):
+        return lax.dynamic_slice_in_dim(v, b * half, half, v.ndim - 1)
+
+    def other(v):
+        return lax.dynamic_slice_in_dim(v, (1 - b) * half, half, v.ndim - 1)
+
+    def natural(m, o):
+        return jnp.where(b == 0, jnp.concatenate([m, o], -1), jnp.concatenate([o, m], -1))
+
+    def four(a, c):
+        return jnp.concatenate([a[..., :half], c[..., :half], a[..., half:], c[..., half:]], -1)
+
+    def third(v, q):
+        return v[wat[q] * dk : wat[q + 1] * dk]
+
+    w_m = mine(w)
+    w_o = other(w)
+    coefs = stitch[0]
+    self_c = jnp.where(tower == 0, coefs[0], coefs[1])
+    other_c = jnp.where(tower == 0, coefs[1], coefs[0])
+    grads = image_grad[0]
+    grads = jnp.concatenate([mine(grads), other(grads)], 1)
+
+    def square_rows(v):
+        v = v.reshape(-1, rows)
+        return jnp.concatenate(
+            [lax.dynamic_index_in_dim(v, me ^ o, 0, keepdims=False) for o in range(4)], 0
+        )
+
+    live = square_rows(row_live).astype(F32)
+    img_dev = crop_counts.shape[0]
+    local_img = square_rows(row_image) - b * img_dev
+    match = local_img[:, None] == jnp.arange(img_dev, dtype=jnp.int32)[None, :]
+    per_row = jnp.sum(jnp.where(match, crop_counts[None, :].astype(F32), 0.0), axis=1)
+    scale = live / per_row
+
+    def out_grad_of(g):
+        picked = jnp.dot(match.astype(BF), g, preferred_element_type=F32)
+        return (picked * scale[:, None]).astype(BF)
+
+    nz = 3
+    rz = rows // nz
+    V = {"X": x, "G": grads, "oc0": other_c}
+    for q in range(nw):
+        V[f"W{q}"] = third(w_m, q)
+    fb = dk
+    send = {"z": (sz, "Z"), "y": (sy, "X"), "d": (sy, "z"), "p": (sp, "W"), "x": (sx, "p")}
+    once = {"g": (sp, "G"), "m": (sp, "small"), "o": (st, "oc0"), "a": (st, "oga"), "b": (st, "ogb")}
+
+    def known():
+        return [x, V["y0"], *(V[f"z{i}"] for i in range(nz - 1))]
+
+    def weight_parts(q0, q1):
+        ps = [V[f"p{q}"] for q in range(q0, q1)]
+        return ps, [V[f"x{q}"] for q in range(q0, q1)], wat[q0], fb
+
+    for step in STEPS:
+        if step[0] == "+":
+            key = step[1:]
+            if key == "y0":
+                V[key] = sy(x)
+                continue
+            if key in once:
+                if key == "m":
+                    small = jnp.stack([self_c, other_c, V["o"], fc_bias[0].astype(F32)])
+                    V["small"] = jnp.concatenate([mine(small), other(small)], 1)
+                elif key == "a":
+                    V["oga"] = out_grad_of(grads)
+                elif key == "b":
+                    V["ogb"] = out_grad_of(V["g"])
+                f, src = once[key]
+                V[key] = f(V[src])
+            else:
+                f, src = send[key[0]]
+                if src == "Z":
+                    i = int(key[1:])
+                    V[src + key[1:]] = tie(x)[i * rz : (i + 1) * rz]
+                V[key] = f(V[src + key[1:]])
+        elif step[0] == "F":
+            q0, q1 = int(step[1]), int(step[2])
+            xs = known()
+            xs[0] = tie(xs[0])
+            V["F"] = forward(xs, w_m, w_o, *weight_parts(q0, q1), V.get("F"))
+            token[:] = [V["F"]]
+        elif step[0] in "DE":
+            q0, q1 = int(step[1]), int(step[2])
+            rest = [V[f"d{nz - 1}"]]
+            if step[0] == "D":
+                rest = [V[f"z{nz - 1}"], *(V[f"d{i}"] for i in range(nz - 1))]
+            rest[0] = tie(rest[0])
+            V[step[0]] = forward(rest, w_m, w_o, *weight_parts(q0, q1), V.get(step[0]))
+            token[:] = [V[step[0]]]
+        elif step == "hg":
+            vec = four(V["small"], V["m"])
+            self4, other4, cross4 = vec[0], vec[1], vec[2]
+            out_wide = four(V["oga"], V["ogb"]).astype(F32)
+            theirs = four(V["a"], V["b"]).astype(F32)
+            hidden_grad = (self4[None] * out_wide + cross4[None] * theirs).astype(BF)
+            bias4 = vec[3][None]
+            V["hg"] = wait(hidden_grad)
+        else:
+            V[step] = wait(V[step])
+    p = [V[f"p{q}"] for q in range(nw)]
+    xg = [V[f"x{q}"] for q in range(nw)]
+    hidden, pre_grad = activate([V["F"], V["D"], V["E"]], bias4, V["hg"], rz)
+    features = [*known(), V[f"z{nz - 1}"], *(V[f"d{i}"] for i in range(nz))]
+    per = dk // block
+
+    def weights(c):
+        q = max(i for i in range(nw) if wat[i] <= c)
+        lo = (c - wat[q]) * per
+        return [(w_m, c * per), (p[q], lo), (w_o, c * per), (xg[q], lo)]
+
+    def only(v, *deps):
+        return lax.optimization_barrier((v, *deps))[0] if deps else v
+
+    def y_part(c, *deps):
+        return nt_product(only(pre_grad, *deps), (1, 3), weights(c), (), rows, dk, block)
+
+    def z_part(c, *deps):
+        g = only(pre_grad, *deps)
+        return nt_product(g, (2,), weights(c), [(yy[c], 1, 0)], rows, dk, block)
+
+    def own_part(c, held):
+        into = (held, (rows, depth), c * per)
+        return nt_product(
+            pre_grad, (0,), weights(c), [(yy[c], 0, 0), (zz[c], 0, 0)], rows, dk, block, into
+        )
+
+    def dw_sent(c, *deps):
+        return tn_product(features, only(pre_grad, *deps), 1, c * per, dk, block)
+
+    def dw_kept(c):
+        return tn_product(features, pre_grad, 0, c * per, dk, block, s[c])
+
+    token.clear()
+    bvec = jnp.full((1,), b, jnp.int32)
+
+    s, k, a, t, k_got = ([None] * nk for _ in range(5))
+    yy, zz, own, put = ([None] * nk for _ in range(4))
+
+    hid_other = None
+    later = {}
+
+    def do_sums():
+        hw, how = hidden.astype(F32), hid_other.astype(F32)
+        sums = jnp.stack(
+            [
+                jnp.sum(out_wide * hw, axis=0),
+                jnp.sum(out_wide * how, axis=0),
+                jnp.sum(pre_grad.astype(F32), axis=0),
+            ]
+        )
+        later["a"] = jnp.concatenate([sums[:, :half], sums[:, cols : cols + half]], 1)
+        s_b = jnp.concatenate([sums[:, half:cols], sums[:, cols + half :]], 1)
+        later["p"] = sp(s_b)
+
+    def do_st():
+        hw, how = hidden.astype(F32), hid_other.astype(F32)
+        stitched = ((self4[None] * hw + other4[None] * how) * live[:, None]).astype(BF)
+        later["st_a"] = jnp.concatenate([stitched[:, :half], stitched[:, cols : cols + half]], 1)
+        st_b = jnp.concatenate([stitched[:, half:cols], stitched[:, cols + half :]], 1)
+        later["st"] = sp(st_b)
+
+    def do_sumx():
+        s_a = later["a"] + later["p"]
+        s_a = natural(s_a[:, :half], s_a[:, half:])
+        later["s"] = s_a + sx(s_a)
+
+    def lump(n, *extra):
+        places = [(v, c) for v, c in ((yy, n), (s, n), (zz, n - 1), (k_got, n - 1), (a, n - 2))
+                  if 0 <= c < nk and v[c] is not None]
+        outs = lax.optimization_barrier((*(v[c] for v, c in places), *extra))
+        for (v, c), o in zip(places, outs):
+            v[c] = o
+        held = [v[c] for v, c in ((own, n - 2), (put, n - 3)) if 0 <= c < nk]
+        token[:] = [*outs, *held]
+        return outs[len(places):]
+
+    def st_piece(half_rows):
+        lo, hi = half_rows
+        hw, how = hidden[lo:hi].astype(F32), hid_other[lo:hi].astype(F32)
+        stitched = (self4[None] * hw + other4[None] * how) * live[lo:hi, None]
+        stitched = stitched.astype(BF)
+        kept = jnp.concatenate([stitched[:, :half], stitched[:, cols : cols + half]], 1)
+        sent = jnp.concatenate([stitched[:, half:cols], stitched[:, cols + half :]], 1)
+        return kept, sp(sent)
+
+    y_next, s_next = y_part(0), None
+    cut = 960 * rows // 384
+    for n in range(nk + 2):
+        if n < nk:
+            yy[n] = sy(y_next, s_next)
+            if n == 0:
+                s_next = dw_sent(0, y_next)
+            s[n] = sx(s_next)
+        extra = []
+        if n == 0:
+            hid_other = st(only(hidden, y_next))
+            do_sums()
+            st_a0, st_g0 = st_piece((0, cut))
+            extra = [later["p"], st_g0]
+        if 0 < n <= nk:
+            zz[n - 1] = sz(z_part(n - 1))
+            t[n - 1], k[n - 1] = dw_kept(n - 1)
+            k_got[n - 1] = sp(k[n - 1])
+        if n == nk + 1 and cut < 4 * rows:
+            st_a1, st_g1 = st_piece((cut, 4 * rows))
+        if n == 1:
+            do_sumx()
+            extra = [later["s"]]
+        if 1 < n:
+            a[n - 2] = sx(finished(t[n - 2], k_got[n - 2]))
+            own[n - 2] = own_part(n - 2, own[n - 3] if n > 2 else None)
+        if 2 < n:
+            put[n - 3] = place(
+                bvec, t[n - 3], k_got[n - 3], a[n - 3], put[n - 4] if n > 3 else None, depth, n - 3
+            )
+        if n + 1 < nk:
+            y_next, s_next = y_part(n + 1), dw_sent(n + 1)
+        outs = lump(n, *extra)
+        if n == 0:
+            later["p"], st_g0 = outs
+        if n == 1:
+            (later["s"],) = outs
+    token.clear()
+    put[-1] = place(bvec, t[-1], k_got[-1], a[-1], put[-2], depth, nk - 1)
+    later["st_a"], later["st"] = st_a0, st_g0
+    if cut < 4 * rows:
+        later["st_a"] = jnp.concatenate([st_a0, st_a1], 0)
+        later["st"] = jnp.concatenate([st_g0, st_g1], 0)
+    held_x, held_w = own[-1], put[-1]
+    st_a, st_got, s_a = later["st_a"], later["st"], later["s"]
+    acts_grad, weight_grad = held_x, held_w
+
+    st_all = jnp.concatenate([st_a, st_got], 0)
+    st_all = natural(st_all[:, :half], st_all[:, half:])
+    st_all = st_all.reshape(8, rows, cols)
+    order = jnp.arange(8) ^ me
+    stitched_out = st_all[order].reshape(8 * rows, cols)
+
+    own_s, other_s = s_a[0], s_a[1]
+    stitch_grad = jnp.where(tower == 0, jnp.stack([own_s, other_s]), jnp.stack([other_s, own_s]))
+    return (
+        stitched_out[None],
+        acts_grad[None],
+        weight_grad[None],
+        s_a[2][None],
         stitch_grad[None],
     )
 
@@ -84,6 +620,7 @@
         P("batch"),
         P("batch"),
     )
+    per_device = squares if mesh.shape["mp"] == 8 and mesh.shape["batch"] == 2 else general
     return jax.shard_map(
         per_device,
         mesh=mesh,

time: 3320 us -> 798 us (0.24)
  waiting for transfers between devices: 3130 us -> 344 us
  Pallas kernels: 0 us -> 297 us
  matrix products: 132 us -> 7.85 us
  starting transfers between devices: 0.68 us -> 64.7 us
    reduce_scatter x1 -> x0, waiting for transfers between devices: 1700 us -> none  [per_device(): lax.psum_scatter(lax.dot_general(pre_grad, weight_matrix, (((1,), (1,)),...]
    all_gather x1 -> x0, waiting for transfers between devices: 1060 us -> none  [per_device(): gathered = lax.all_gather(feature_rows, 'mp', axis=0, tiled=True)]
    psum x1 -> x0, waiting for transfers between devices: 359 us -> none  [per_device(): lax.psum((weight_grad, bias_grad, stitch_grad), 'batch')]
    ppermute x2 -> x53, waiting for transfers between devices: 15.2 us -> 344 us  [swapped(): return lax.ppermute(block, axis, [(i, i ^ mask) for i in range(count)])]
    pallas_call x0 -> x49, Pallas kernels: none -> 297 us  [the longest x18 102 us: nt_product(): pl.pallas_call(body, out_shape=jax.ShapeDtypeStruct(shape, BF), grid=(ste...]
    dot_general x4 -> x2, matrix products: 132 us -> 7.85 us  [out_grad_of(): picked = jnp.dot(match.astype(BF), g, preferred_element_type=F32)]
    ppermute x2 -> x53, starting transfers between devices: 0.56 us -> 64.7 us  [swapped(): return lax.ppermute(block, axis, [(i, i ^ mask) for i in range(count)])]
  transfers between devices with their start and end apart: 5 -> 53, of which waited for: 5 -> 25; matrix products, arithmetic and copies ran while one was open for 2% -> 9% of each run, Pallas kernels for 0% -> 35%
where the time goes in v2:
time: 798 us; the launch traced here: 787 us
  waiting for transfers between devices  344 us (43%)
  Pallas kernels  297 us (37%)
  starting transfers between devices  64.7 us (8%)
  local copies, waits for them, and re-layouts  42.6 us (5%)
  other arithmetic  29.4 us (4%)
    ppermute x53, waiting for transfers between devices, swapped(): return lax.ppermute(block, axis, [(i, i ^ mask) for i in range(count)])  344 us
    pallas_call x18, Pallas kernels, nt_product(): pl.pallas_call(body, out_shape=jax.ShapeDtypeStruct(shape, BF), grid=(ste...  102 us
    pallas_call x12, Pallas kernels, tn_product(): pl.pallas_call(body, out_shape=outs, grid=(steps,), in_specs=specs, out_s...  83.2 us
    pallas_call x6, Pallas kernels, forward(): pl.pallas_call(functools.partial(forward_body, len(xs), starts, acc is no...  67.7 us
    ppermute x53, starting transfers between devices, swapped(): return lax.ppermute(block, axis, [(i, i ^ mask) for i in range(count)])  64.7 us
    pallas_call x6, Pallas kernels, place(): pl.pallas_call(place_body, out_shape=jax.ShapeDtypeStruct((depth, 2 * hal...  19.4 us
  transfers between devices with their start and end apart: 53, of which 25 were waited for; matrix products, arithmetic and copies ran while one was open for 9% of the time, Pallas kernels for 35%

profile of v2, /device:TPU:0, one launch (start us, length us, event | category | flops | bytes accessed | tf_op | source)
XLA Modules:
  0.0 786.9 jit_solution(13353192431518129621)
XLA Ops:
  11.8 48.1 %collective-permute-done.refs_2_ = bf16[128,9216]{1,0:T(8,128)(2,1)S(1)} collective-permute-done((bf16[128,9216]{1,0:T(8,128)(2,1)}, bf16[128,9216]{1,0:T(8,128)(2,1)S(1)}, u32[]{:S(2)}, u32[]{:S(2)}) %collective-permute-start) | collective-permute-done | bytes 2359328 | tf_op jit(solution)/shard_map/ppermute | solution.py:16
  73.7 93.0 %collective-permute-done.3.refs_3_ = bf16[128,9216]{1,0:T(8,128)(2,1)} collective-permute-done((bf16[128,9216]{1,0:T(8,128)(2,1)}, bf16[128,9216]{1,0:T(8,128)(2,1)}, u32[]{:S(2)}, u32[]{:S(2)}) %collective-permute-start.3) | collective-permute-done | bytes 2359328 | tf_op jit(solution)/shard_map/ppermute | solution.py:16
  186.6 21.2 %collective-permute-done.6.refs_1_.refs_5_ = bf16[128,9216]{1,0:T(8,128)(2,1)} collective-permute-done((bf16[128,9216]{1,0:T(8,128)(2,1)S(1)}, bf16[128,9216]{1,0:T(8,128)(2,1)}, u32[]{:S(2)}, u32[]{:S(2)}) %collective-permute-start.6) | collective-permute-done | bytes 2359328 | tf_op jit(solution)/shard_map/ppermute | solution.py:16
  207.8 10.3 %collective-permute-done.5.refs_7_.refs_6_.refs_5_.refs_4_ = bf16[4608,256]{1,0:T(8,128)(2,1)} collective-permute-done((bf16[4608,256]{1,0:T(8,128)(2,1)}, bf16[4608,256]{1,0:T(8,128)(2,1)}, u32[]{:S(2)}, u32[]{:S(2)}) %collective-permute-start.5) | collective-permute-done | bytes 2359328 | tf_op jit(solution)/shard_map/ppermute | solution.py:16
  218.1 15.5 %shard_map.119.refs_8_ = f32[1024,1024]{1,0:T(8,128)} custom-call(bf16[384,9216]{1,0:T(8,128)(2,1)} %bitcast.43, bf16[384,9216]{1,0:T(8,128)(2,1)} %collective-permute-done.7.refs_1_, bf16[128,9216]{1,0:T(8,128)(2,1)} %copy-done.1, bf16[128,9216]{1,0:T(8,128)(2,1)} %collective-permute-done.3.refs_3_, ...), custom_call_target="tpu_custom_call" | custom-call | flops 1000 | bytes 1000 | tf_op jit(solution)/shard_map/pallas_call | solution.py:138
  233.6 11.3 %collective-permute-done.4.refs_6_.refs_4_.refs_3_.refs_2_ = bf16[3072,256]{1,0:T(8,128)(2,1)} collective-permute-done((bf16[3072,256]{1,0:T(8,128)(2,1)}, bf16[3072,256]{1,0:T(8,128)(2,1)}, u32[]{:S(2)}, u32[]{:S(2)}) %collective-permute-start.4) | collective-permute-done | bytes 1572896 | tf_op jit(solution)/shard_map/ppermute | solution.py:16
  247.8 29.0 %collective-permute-done.10.refs_0_.refs_4_ = bf16[128,9216]{1,0:T(8,128)(2,1)} collective-permute-done((bf16[128,9216]{1,0:T(8,128)(2,1)}, bf16[128,9216]{1,0:T(8,128)(2,1)}, u32[]{:S(2)}, u32[]{:S(2)}) %collective-permute-start.10) | collective-permute-done | bytes 2359328 | tf_op jit(solution)/shard_map/ppermute | solution.py:16
  276.8 6.9 collective-permute-done.9.refs_6_.refs_5_.refs_3_.refs_2_
  291.4 14.0 %shard_map.120.refs_8_ = f32[1024,1024]{1,0:T(8,128)} custom-call(bf16[384,9216]{1,0:T(8,128)(2,1)} %bitcast.44, bf16[384,9216]{1,0:T(8,128)(2,1)} %collective-permute-done.7.refs_1_, bf16[128,9216]{1,0:T(8,128)(2,1)} %copy-done.1, bf16[128,9216]{1,0:T(8,128)(2,1)} %collective-permute-done.3.refs_3_, ...), custom_call_target="tpu_custom_call" | custom-call | flops 1000 | bytes 1000 | tf_op jit(solution)/shard_map/pallas_call | solution.py:138
  305.4 13.1 %shard_map.121.refs_7_ = f32[384,1024]{1,0:T(8,128)} custom-call(bf16[128,9216]{1,0:T(8,128)(2,1)} %collective-permute-done.10.refs_0_.refs_4_, bf16[128,9216]{1,0:T(8,128)(2,1)} %collective-permute-done.6.refs_1_.refs_5_, bf16[128,9216]{1,0:T(8,128)(2,1)} %collective-permute-done.14.refs_2_.refs_6_, ...), custom_call_target="tpu_custom_call" | custom-call | flops 1000 | bytes 1000 | tf_op jit(solution)/shard_map/pallas_call | solution.py:138
  318.5 9.5 %shard_map.122.refs_0_ = f32[1024,1024]{1,0:T(8,128)} custom-call(bf16[384,9216]{1,0:T(8,128)(2,1)} %bitcast.45, bf16[384,9216]{1,0:T(8,128)(2,1)} %collective-permute-done.7.refs_1_, bf16[128,9216]{1,0:T(8,128)(2,1)} %copy-done.1, bf16[128,9216]{1,0:T(8,128)(2,1)} %collective-permute-done.3.refs_3_, ...), custom_call_target="tpu_custom_call" | custom-call | flops 1000 | bytes 1000 | tf_op jit(solution)/shard_map/pallas_call | solution.py:138
  344.9 10.3 %shard_map.124.refs_2_ = f32[128,1024]{1,0:T(8,128)} custom-call(bf16[128,9216]{1,0:T(8,128)(2,1)} %copy-done.2, bf16[9216,256]{1,0:T(8,128)(2,1)} %get-tuple-element.256.refs_4_.refs_3_.refs_1_.refs_2_, bf16[9216,256]{1,0:T(8,128)(2,1)} %get-tuple-element.255.refs_5_.refs_4_.refs_2_.refs_3_, ...), custom_call_target="tpu_custom_call" | custom-call | flops 1000 | bytes 1000 | tf_op jit(solution)/shard_map/pallas_call | solution.py:138
  361.3 10.2 %shard_map.125 = (bf16[1536,1024]{1,0:T(8,128)(2,1)}, bf16[1536,1024]{1,0:T(8,128)(2,1)}) custom-call(f32[1024,1024]{1,0:T(8,128)} %shard_map.122.refs_0_, f32[384,1024]{1,0:T(8,128)} %shard_map.123.refs_1_, f32[128,1024]{1,0:T(8,128)} %shard_map.124.refs_2_, f32[1,1024]{1,0:T(1,128)} %get-tuple-element.283.refs_3_, bf16[1536,1024]{1,0:T(8,128)(2,1)} %fusion.1.refs_4_), custom_call_target="tpu_custom_call" | custom-call | flops 1000 | bytes 1000 | tf_op jit(solution)/shard_map/pallas_call | solution.py:172
  379.8 7.0 shard_map.127
  411.8 11.5 %collective-permute-done.20.refs_9_ = bf16[1536,512]{1,0:T(8,128)(2,1)} collective-permute-done((bf16[1536,512]{1,0:T(8,128)(2,1)}, bf16[1536,512]{1,0:T(8,128)(2,1)}, u32[]{:S(2)}, u32[]{:S(2)}) %collective-permute-start.20) | collective-permute-done | bytes 1572896 | tf_op jit(solution)/shard_map/ppermute | solution.py:16
  423.2 8.6 %collective-permute-done.19.refs_5_ = bf16[768,1536]{1,0:T(8,128)(2,1)} collective-permute-done((bf16[768,1536]{1,0:T(8,128)(2,1)}, bf16[768,1536]{1,0:T(8,128)(2,1)}, u32[]{:S(2)}, u32[]{:S(2)}) %collective-permute-start.19) | collective-permute-done | bytes 2359328 | tf_op jit(solution)/shard_map/ppermute | solution.py:16
  443.7 7.2 shard_map.139
  460.8 6.5 shard_map.135
  474.1 12.0 %collective-permute-done.26.got = bf16[1536,256]{1,0:T(8,128)(2,1)S(1)} collective-permute-done((bf16[1536,256]{1,0:T(8,128)(2,1)}, bf16[1536,256]{1,0:T(8,128)(2,1)S(1)}, u32[]{:S(2)}, u32[]{:S(2)}) %collective-permute-start.26) | collective-permute-done | bytes 786464 | tf_op jit(solution)/shard_map/ppermute | solution.py:16
  497.2 7.2 shard_map.141
  516.9 6.6 shard_map.133
  529.3 9.5 %collective-permute-done.31.got = bf16[1536,256]{1,0:T(8,128)(2,1)S(1)} collective-permute-done((bf16[1536,256]{1,0:T(8,128)(2,1)}, bf16[1536,256]{1,0:T(8,128)(2,1)S(1)}, u32[]{:S(2)}, u32[]{:S(2)}) %collective-permute-start.31) | collective-permute-done | bytes 786464 | tf_op jit(solution)/shard_map/ppermute | solution.py:16
  551.4 7.3 shard_map.145
  570.9 6.6 shard_map.131
  603.1 7.2 shard_map.150
  622.7 6.6 shard_map.129
  655.8 7.3 shard_map.155
  677.4 15.7 %collective-permute-done.46.got = bf16[1536,256]{1,0:T(8,128)(2,1)S(1)} collective-permute-done((bf16[1536,256]{1,0:T(8,128)(2,1)}, bf16[1536,256]{1,0:T(8,128)(2,1)S(1)}, u32[]{:S(2)}, u32[]{:S(2)}) %collective-permute-start.46) | collective-permute-done | bytes 786464 | tf_op jit(solution)/shard_map/ppermute | solution.py:16
  703.5 7.2 shard_map.160
  729.7 13.5 %collective-permute-done.49.got = bf16[1536,256]{1,0:T(8,128)(2,1)S(1)} collective-permute-done((bf16[1536,256]{1,0:T(8,128)(2,1)}, bf16[1536,256]{1,0:T(8,128)(2,1)S(1)}, u32[]{:S(2)}, u32[]{:S(2)}) %collective-permute-start.49) | collective-permute-done | bytes 786464 | tf_op jit(solution)/shard_map/ppermute | solution.py:16
  760.3 8.8 %collective-permute-done.51 = bf16[576,512]{1,0:T(8,128)(2,1)} collective-permute-done((bf16[576,512]{1,0:T(8,128)(2,1)}, bf16[576,512]{1,0:T(8,128)(2,1)}, u32[]{:S(2)}, u32[]{:S(2)}) %collective-permute-start.51) | collective-permute-done | bytes 589856 | tf_op jit(solution)/shard_map/ppermute | solution.py:16
  769.1 10.5 %pad_maximum_fusion.1 = bf16[3072,512]{1,0:T(8,128)(2,1)S(1)} fusion(bf16[576,512]{1,0:T(8,128)(2,1)} %collective-permute-done.51, bf16[960,512]{1,0:T(8,128)(2,1)} %collective-permute-done.22, bf16[576,256]{1,0:T(8,128)(2,1)S(1)} %get-tuple-element.274, bf16[576,256]{1,0:T(8,128)(2,1)S(1)} %get-tuple-element.271, bf16[960,256]{1,0:T(8,128)(2,1)S(1)} %copy-done.27, ...), kind=kLoop, calls=%fused_computation.19 | loop fusion | flops 18874368 | bytes 6291456 | tf_op jit(solution)/shard_map/concatenate | solution.py:595
  (269 shorter events, 326.0 us)
Async XLA Ops:
  0.6 178.9 %collective-permute-start.7 = (bf16[384,9216]{1,0:T(8,128)(2,1)}, bf16[384,9216]{1,0:T(8,128)(2,1)}, u32[]{:S(2)}, u32[]{:S(2)}) collective-permute-start(bf16[384,9216]{1,0:T(8,128)(2,1)} %bitcast.40), channel_id=1, source_target_pairs={{0,1},{1,0},{2,3},{3,2},{4,5},{5,4},{6,7},{7,6},{8,9},{9,8},{10,11... | collective-permute-start | bytes 21233672 | tf_op jit(solution)/shard_map/ppermute | solution.py:16
  6.9 52.9 %collective-permute-start = (bf16[128,9216]{1,0:T(8,128)(2,1)}, bf16[128,9216]{1,0:T(8,128)(2,1)S(1)}, u32[]{:S(2)}, u32[]{:S(2)}) collective-permute-start(bf16[128,9216]{1,0:T(8,128)(2,1)} %slice_bitcast_fusion), channel_id=1, source_target_pairs={{0,2},{1,3},{2,0},{3,1},{4,6},{5,7},{6,4},{7,5},{8,10},{9,11},{10,... | collective-permute-start | bytes 7077896 | tf_op jit(solution)/shard_map/ppermute | solution.py:16
  63.9 102.7 %collective-permute-start.3 = (bf16[128,9216]{1,0:T(8,128)(2,1)}, bf16[128,9216]{1,0:T(8,128)(2,1)}, u32[]{:S(2)}, u32[]{:S(2)}) collective-permute-start(bf16[128,9216]{1,0:T(8,128)(2,1)} %slice.166), channel_id=1, source_target_pairs={{0,2},{1,3},{2,0},{3,1},{4,6},{5,7},{6,4},{7,5},{8,10},{9,11},{10,... | collective-permute-start | bytes 7077896 | tf_op jit(solution)/shard_map/ppermute | solution.py:16
  65.5 103.5 %collective-permute-start.2 = (bf16[4608,256]{1,0:T(8,128)(2,1)}, bf16[4608,256]{1,0:T(8,128)(2,1)}, u32[]{:S(2)}, u32[]{:S(2)}) collective-permute-start(bf16[4608,256]{1,0:T(8,128)(2,1)} %dynamic-slice_bitcast_fusion.2), channel_id=1, source_target_pairs={{0,4},{1,5},{2,6},{3,7},{4,0},{5,1},{6,2},{7,3},{8,12},{9,13},{10,... | collective-permute-start | bytes 7077896 | tf_op jit(solution)/shard_map/ppermute | solution.py:16
  73.1 103.7 %collective-permute-start.8 = (bf16[1536,512]{1,0:T(8,128)(2,1)}, bf16[1536,512]{1,0:T(8,128)(2,1)}, u32[]{:S(2)}, u32[]{:S(2)}) collective-permute-start(bf16[1536,512]{1,0:T(8,128)(2,1)} %fusion.11), channel_id=1, source_target_pairs={{0,16},{16,0},{1,17},{17,1},{2,18},{18,2},{3,19},{19,3},{4,20},{20... | collective-permute-start | bytes 4718600 | tf_op jit(solution)/shard_map/ppermute | solution.py:16
  73.1 134.7 %collective-permute-start.6 = (bf16[128,9216]{1,0:T(8,128)(2,1)S(1)}, bf16[128,9216]{1,0:T(8,128)(2,1)}, u32[]{:S(2)}, u32[]{:S(2)}) collective-permute-start(bf16[128,9216]{1,0:T(8,128)(2,1)S(1)} %collective-permute-done.refs_2_), channel_id=1, source_target_pairs={{0,1},{1,0},{2,3},{3,2},{4,5},{5,4},{6,7},{7,6},{8,9},{9,8},{10,11... | collective-permute-start | bytes 7077896 | tf_op jit(solution)/shard_map/ppermute | solution.py:16
  169.0 49.1 %collective-permute-start.5 = (bf16[4608,256]{1,0:T(8,128)(2,1)}, bf16[4608,256]{1,0:T(8,128)(2,1)}, u32[]{:S(2)}, u32[]{:S(2)}) collective-permute-start(bf16[4608,256]{1,0:T(8,128)(2,1)} %collective-permute-done.2.refs_6_.refs_5_.refs_3_.refs_2_), channel_id=1, source_target_pairs={{0,8},{8,0},{1,9},{9,1},{2,10},{10,2},{3,11},{11,3},{4,12},{12,4},... | collective-permute-start | bytes 7077896 | tf_op jit(solution)/shard_map/ppermute | solution.py:16
  173.3 71.7 %collective-permute-start.4 = (bf16[3072,256]{1,0:T(8,128)(2,1)}, bf16[3072,256]{1,0:T(8,128)(2,1)}, u32[]{:S(2)}, u32[]{:S(2)}) collective-permute-start(bf16[3072,256]{1,0:T(8,128)(2,1)} %dynamic-slice_bitcast_fusion.3), channel_id=1, source_target_pairs={{0,4},{1,5},{2,6},{3,7},{4,0},{5,1},{6,2},{7,3},{8,12},{9,13},{10,... | collective-permute-start | bytes 4718600 | tf_op jit(solution)/shard_map/ppermute | solution.py:16
  176.8 100.0 %collective-permute-start.10 = (bf16[128,9216]{1,0:T(8,128)(2,1)}, bf16[128,9216]{1,0:T(8,128)(2,1)}, u32[]{:S(2)}, u32[]{:S(2)}) collective-permute-start(bf16[128,9216]{1,0:T(8,128)(2,1)} %slice.171), channel_id=1, source_target_pairs={{0,2},{1,3},{2,0},{3,1},{4,6},{5,7},{6,4},{7,5},{8,10},{9,11},{10,... | collective-permute-start | bytes 7077896 | tf_op jit(solution)/shard_map/ppermute | solution.py:16
  179.5 125.9 %collective-permute-start.14 = (bf16[128,9216]{1,0:T(8,128)(2,1)}, bf16[128,9216]{1,0:T(8,128)(2,1)}, u32[]{:S(2)}, u32[]{:S(2)}) collective-permute-start(bf16[128,9216]{1,0:T(8,128)(2,1)} %collective-permute-done.3.refs_3_), channel_id=1, source_target_pairs={{0,1},{1,0},{2,3},{3,2},{4,5},{5,4},{6,7},{7,6},{8,9},{9,8},{10,11... | collective-permute-start | bytes 7077896 | tf_op jit(solution)/shard_map/ppermute | solution.py:16
  245.0 41.0 %collective-permute-start.15 = (bf16[3072,256]{1,0:T(8,128)(2,1)}, bf16[3072,256]{1,0:T(8,128)(2,1)}, u32[]{:S(2)}, u32[]{:S(2)}) collective-permute-start(bf16[3072,256]{1,0:T(8,128)(2,1)} %collective-permute-done.4.refs_6_.refs_4_.refs_3_.refs_2_), channel_id=1, source_target_pairs={{0,8},{8,0},{1,9},{9,1},{2,10},{10,2},{3,11},{11,3},{4,12},{12,4},... | collective-permute-start | bytes 4718600 | tf_op jit(solution)/shard_map/ppermute | solution.py:16
  283.7 49.6 %collective-permute-start.12 = (bf16[1024,512]{1,0:T(8,128)(2,1)}, bf16[1024,512]{1,0:T(8,128)(2,1)}, u32[]{:S(2)}, u32[]{:S(2)}) collective-permute-start(bf16[1024,512]{1,0:T(8,128)(2,1)} %pad_maximum_fusion.2), channel_id=1, source_target_pairs={{0,4},{1,5},{2,6},{3,7},{4,0},{5,1},{6,2},{7,3},{8,12},{9,13},{10,... | collective-permute-start | bytes 3145736 | tf_op jit(solution)/shard_map/ppermute | solution.py:16
  285.4 58.1 %collective-permute-start.16 = (bf16[128,9216]{1,0:T(8,128)(2,1)}, bf16[128,9216]{1,0:T(8,128)(2,1)S(1)}, u32[]{:S(2)}, u32[]{:S(2)}) collective-permute-start(bf16[128,9216]{1,0:T(8,128)(2,1)} %collective-permute-done.10.refs_0_.refs_4_), channel_id=1, source_target_pairs={{0,1},{1,0},{2,3},{3,2},{4,5},{5,4},{6,7},{7,6},{8,9},{9,8},{10,11... | collective-permute-start | bytes 7077896 | tf_op jit(solution)/shard_map/ppermute | solution.py:16
  285.9 47.4 %collective-permute-start.11 = (f32[4,512]{1,0:T(4,128)S(1)}, f32[4,512]{1,0:T(4,128)S(1)}, u32[]{:S(2)}, u32[]{:S(2)}) collective-permute-start(f32[4,512]{1,0:T(4,128)S(1)} %pad_maximum_fusion.8), channel_id=1, source_target_pairs={{0,4},{1,5},{2,6},{3,7},{4,0},{5,1},{6,2},{7,3},{8,12},{9,13},{10,... | collective-permute-start | bytes 24584 | tf_op jit(solution)/shard_map/ppermute | solution.py:16
  378.3 53.5 %collective-permute-start.19 = (bf16[768,1536]{1,0:T(8,128)(2,1)}, bf16[768,1536]{1,0:T(8,128)(2,1)}, u32[]{:S(2)}, u32[]{:S(2)}) collective-permute-start(bf16[768,1536]{1,0:T(8,128)(2,1)} %shard_map.126), channel_id=1, source_target_pairs={{0,1},{1,0},{2,3},{3,2},{4,5},{5,4},{6,7},{7,6},{8,9},{9,8},{10,11... | collective-permute-start | bytes 7077896 | tf_op jit(solution)/shard_map/ppermute | solution.py:16
  392.2 44.3 %collective-permute-start.22 = (bf16[960,512]{1,0:T(8,128)(2,1)S(1)}, bf16[960,512]{1,0:T(8,128)(2,1)}, u32[]{:S(2)}, u32[]{:S(2)}) collective-permute-start(bf16[960,512]{1,0:T(8,128)(2,1)S(1)} %pad_maximum_fusion.3), channel_id=1, source_target_pairs={{0,4},{1,5},{2,6},{3,7},{4,0},{5,1},{6,2},{7,3},{8,12},{9,13},{10,... | collective-permute-start | bytes 2949128 | tf_op jit(solution)/shard_map/ppermute | solution.py:16
  436.5 53.5 %collective-permute-start.23 = (bf16[768,1536]{1,0:T(8,128)(2,1)}, bf16[768,1536]{1,0:T(8,128)(2,1)S(1)}, u32[]{:S(2)}, u32[]{:S(2)}) collective-permute-start(bf16[768,1536]{1,0:T(8,128)(2,1)} %shard_map.136), channel_id=1, source_target_pairs={{0,1},{1,0},{2,3},{3,2},{4,5},{5,4},{6,7},{7,6},{8,9},{9,8},{10,11... | collective-permute-start | bytes 7077896 | tf_op jit(solution)/shard_map/ppermute | solution.py:16
  437.0 51.3 %collective-permute-start.24 = (bf16[1536,512]{1,0:T(8,128)(2,1)}, bf16[1536,512]{1,0:T(8,128)(2,1)}, u32[]{:S(2)}, u32[]{:S(2)}) collective-permute-start(bf16[1536,512]{1,0:T(8,128)(2,1)} %shard_map.137), channel_id=1, source_target_pairs={{0,8},{8,0},{1,9},{9,1},{2,10},{10,2},{3,11},{11,3},{4,12},{12,4},... | collective-permute-start | bytes 4718600 | tf_op jit(solution)/shard_map/ppermute | solution.py:16
  443.7 44.6 %collective-permute-start.25 = (bf16[384,1536]{1,0:T(8,128)(2,1)}, bf16[384,1536]{1,0:T(8,128)(2,1)}, u32[]{:S(2)}, u32[]{:S(2)}) collective-permute-start(bf16[384,1536]{1,0:T(8,128)(2,1)} %shard_map.138), channel_id=1, source_target_pairs={{0,2},{1,3},{2,0},{3,1},{4,6},{5,7},{6,4},{7,5},{8,10},{9,11},{10,... | collective-permute-start | bytes 3538952 | tf_op jit(solution)/shard_map/ppermute | solution.py:16
  490.0 53.1 %collective-permute-start.28 = (bf16[768,1536]{1,0:T(8,128)(2,1)}, bf16[768,1536]{1,0:T(8,128)(2,1)}, u32[]{:S(2)}, u32[]{:S(2)}) collective-permute-start(bf16[768,1536]{1,0:T(8,128)(2,1)} %shard_map.134), channel_id=1, source_target_pairs={{0,1},{1,0},{2,3},{3,2},{4,5},{5,4},{6,7},{7,6},{8,9},{9,8},{10,11... | collective-permute-start | bytes 7077896 | tf_op jit(solution)/shard_map/ppermute | solution.py:16
  490.5 52.5 %collective-permute-start.29 = (bf16[1536,512]{1,0:T(8,128)(2,1)}, bf16[1536,512]{1,0:T(8,128)(2,1)}, u32[]{:S(2)}, u32[]{:S(2)}) collective-permute-start(bf16[1536,512]{1,0:T(8,128)(2,1)} %shard_map.135), channel_id=1, source_target_pairs={{0,8},{8,0},{1,9},{9,1},{2,10},{10,2},{3,11},{11,3},{4,12},{12,4},... | collective-permute-start | bytes 4718600 | tf_op jit(solution)/shard_map/ppermute | solution.py:16
  497.2 45.8 %collective-permute-start.30 = (bf16[384,1536]{1,0:T(8,128)(2,1)}, bf16[384,1536]{1,0:T(8,128)(2,1)}, u32[]{:S(2)}, u32[]{:S(2)}) collective-permute-start(bf16[384,1536]{1,0:T(8,128)(2,1)} %shard_map.140), channel_id=1, source_target_pairs={{0,2},{1,3},{2,0},{3,1},{4,6},{5,7},{6,4},{7,5},{8,10},{9,11},{10,... | collective-permute-start | bytes 3538952 | tf_op jit(solution)/shard_map/ppermute | solution.py:16
  543.0 52.8 %collective-permute-start.33 = (bf16[768,1536]{1,0:T(8,128)(2,1)S(1)}, bf16[768,1536]{1,0:T(8,128)(2,1)}, u32[]{:S(2)}, u32[]{:S(2)}) collective-permute-start(bf16[768,1536]{1,0:T(8,128)(2,1)S(1)} %copy-done.21), channel_id=1, source_target_pairs={{0,1},{1,0},{2,3},{3,2},{4,5},{5,4},{6,7},{7,6},{8,9},{9,8},{10,11... | collective-permute-start | bytes 7077896 | tf_op jit(solution)/shard_map/ppermute | solution.py:16
  544.5 51.3 %collective-permute-start.34 = (bf16[1536,512]{1,0:T(8,128)(2,1)}, bf16[1536,512]{1,0:T(8,128)(2,1)}, u32[]{:S(2)}, u32[]{:S(2)}) collective-permute-start(bf16[1536,512]{1,0:T(8,128)(2,1)} %shard_map.133), channel_id=1, source_target_pairs={{0,8},{8,0},{1,9},{9,1},{2,10},{10,2},{3,11},{11,3},{4,12},{12,4},... | collective-permute-start | bytes 4718600 | tf_op jit(solution)/shard_map/ppermute | solution.py:16
  551.4 44.4 %collective-permute-start.35 = (bf16[384,1536]{1,0:T(8,128)(2,1)}, bf16[384,1536]{1,0:T(8,128)(2,1)}, u32[]{:S(2)}, u32[]{:S(2)}) collective-permute-start(bf16[384,1536]{1,0:T(8,128)(2,1)} %shard_map.144), channel_id=1, source_target_pairs={{0,2},{1,3},{2,0},{3,1},{4,6},{5,7},{6,4},{7,5},{8,10},{9,11},{10,... | collective-permute-start | bytes 3538952 | tf_op jit(solution)/shard_map/ppermute | solution.py:16
  595.8 51.3 %collective-permute-start.38 = (bf16[768,1536]{1,0:T(8,128)(2,1)}, bf16[768,1536]{1,0:T(8,128)(2,1)S(1)}, u32[]{:S(2)}, u32[]{:S(2)}) collective-permute-start(bf16[768,1536]{1,0:T(8,128)(2,1)} %shard_map.130), channel_id=1, source_target_pairs={{0,1},{1,0},{2,3},{3,2},{4,5},{5,4},{6,7},{7,6},{8,9},{9,8},{10,11... | collective-permute-start | bytes 7077896 | tf_op jit(solution)/shard_map/ppermute | solution.py:16
  596.6 50.5 %collective-permute-start.39 = (bf16[1536,512]{1,0:T(8,128)(2,1)}, bf16[1536,512]{1,0:T(8,128)(2,1)}, u32[]{:S(2)}, u32[]{:S(2)}) collective-permute-start(bf16[1536,512]{1,0:T(8,128)(2,1)} %shard_map.131), channel_id=1, source_target_pairs={{0,8},{8,0},{1,9},{9,1},{2,10},{10,2},{3,11},{11,3},{4,12},{12,4},... | collective-permute-start | bytes 4718600 | tf_op jit(solution)/shard_map/ppermute | solution.py:16
  603.1 44.0 %collective-permute-start.40 = (bf16[384,1536]{1,0:T(8,128)(2,1)}, bf16[384,1536]{1,0:T(8,128)(2,1)}, u32[]{:S(2)}, u32[]{:S(2)}) collective-permute-start(bf16[384,1536]{1,0:T(8,128)(2,1)} %shard_map.149), channel_id=1, source_target_pairs={{0,2},{1,3},{2,0},{3,1},{4,6},{5,7},{6,4},{7,5},{8,10},{9,11},{10,... | collective-permute-start | bytes 3538952 | tf_op jit(solution)/shard_map/ppermute | solution.py:16
  647.1 50.2 %collective-permute-start.43 = (bf16[768,1536]{1,0:T(8,128)(2,1)}, bf16[768,1536]{1,0:T(8,128)(2,1)}, u32[]{:S(2)}, u32[]{:S(2)}) collective-permute-start(bf16[768,1536]{1,0:T(8,128)(2,1)} %shard_map.128), channel_id=1, source_target_pairs={{0,1},{1,0},{2,3},{3,2},{4,5},{5,4},{6,7},{7,6},{8,9},{9,8},{10,11... | collective-permute-start | bytes 7077896 | tf_op jit(solution)/shard_map/ppermute | solution.py:16
  648.7 48.7 %collective-permute-start.44 = (bf16[1536,512]{1,0:T(8,128)(2,1)}, bf16[1536,512]{1,0:T(8,128)(2,1)}, u32[]{:S(2)}, u32[]{:S(2)}) collective-permute-start(bf16[1536,512]{1,0:T(8,128)(2,1)} %shard_map.129), channel_id=1, source_target_pairs={{0,8},{8,0},{1,9},{9,1},{2,10},{10,2},{3,11},{11,3},{4,12},{12,4},... | collective-permute-start | bytes 4718600 | tf_op jit(solution)/shard_map/ppermute | solution.py:16
  655.8 41.5 %collective-permute-start.45 = (bf16[384,1536]{1,0:T(8,128)(2,1)}, bf16[384,1536]{1,0:T(8,128)(2,1)S(1)}, u32[]{:S(2)}, u32[]{:S(2)}) collective-permute-start(bf16[384,1536]{1,0:T(8,128)(2,1)} %shard_map.154), channel_id=1, source_target_pairs={{0,2},{1,3},{2,0},{3,1},{4,6},{5,7},{6,4},{7,5},{8,10},{9,11},{10,... | collective-permute-start | bytes 3538952 | tf_op jit(solution)/shard_map/ppermute | solution.py:16
  703.4 39.7 %collective-permute-start.48 = (bf16[384,1536]{1,0:T(8,128)(2,1)}, bf16[384,1536]{1,0:T(8,128)(2,1)S(1)}, u32[]{:S(2)}, u32[]{:S(2)}) collective-permute-start(bf16[384,1536]{1,0:T(8,128)(2,1)} %shard_map.157), channel_id=1, source_target_pairs={{0,2},{1,3},{2,0},{3,1},{4,6},{5,7},{6,4},{7,5},{8,10},{9,11},{10,... | collective-permute-start | bytes 3538952 | tf_op jit(solution)/shard_map/ppermute | solution.py:16
  (66 other events, 1374.1 us)

commit v3 on v2

--- a/solution.py
+++ b/solution.py
@@ -75,14 +75,15 @@
     )
 
 STEPS = (
-    "+y0", "+z0", "z0", "+z1", "+p0", "+d0", "+o", "+a", "z1", "+z2", "+d1", "p0",
-    "+x0", "+p1", "o", "a", "y0", "d0", "x0", "F01", "p1", "+x1", "+p2", "z2",
-    "+d2", "p2", "+x2", "+g", "+m", "x1", "F12", "d1", "D02", "x2", "F23", "D23",
-    "g", "m", "+b", "d2", "E03", "b", "hg",
+    "+y0", "+z0", "+o", "o", "z0", "+z1", "+p0", "+d0", "+a", "z1", "+z2", "+d1",
+    "p0", "+x0", "+p1", "a", "y0", "d0", "x0", "F01", "p1", "+x1", "+p2", "z2",
+    "+d2", "p2", "+x2", "+g", "+m", "x1", "d1", "D02", "x2", "F13", "D23", "d2",
+    "g", "m", "+b", "E03", "b",
 )
 
 NT = (((1,), (1,)), ((), ()))
 TN = (((0,), (0,)), ((), ()))
+HEAVY = pl.CostEstimate(flops=1000, bytes_accessed=60000000, transcendentals=0)
 LIGHT = pl.CostEstimate(flops=1000, bytes_accessed=1000, transcendentals=0)
 
 
@@ -146,20 +147,26 @@
 
 
 def activate_body(bounds, *refs):
-    accs, rest = refs[: len(bounds)], refs[len(bounds) :]
-    bias, hg, hid, pre_grad = rest
+    accs, (vec, og_a, og_b, oo_a, oo_b, hid, pre_grad) = refs[: len(bounds)], refs[len(bounds) :]
     i = pl.program_id(0)
+    half = og_a.shape[1] // 2
     for acc, (lo, hi) in zip(accs, bounds):
 
         @pl.when((i >= lo) & (i < hi))
         def _():
-            pre = acc[...] + bias[...]
-            hid[...] = jnp.maximum(pre, 0.0).astype(BF)
-            pre_grad[...] = jnp.where(pre > 0, hg[...], jnp.zeros_like(hg))
-
-
-def activate(accs, bias, hg, rows):
-    wide = hg.shape[1]
+            for j in range(4):
+                at = slice(j * half, (j + 1) * half)
+                part = slice(j // 2 * half, (j // 2 + 1) * half)
+                og, oo = (og_b, oo_b) if j % 2 else (og_a, oo_a)
+                pre = acc[:, at] + vec[3:4, at]
+                hg = vec[0:1, at] * og[:, part].astype(F32) + vec[2:3, at] * oo[:, part].astype(F32)
+                hid[:, at] = jnp.maximum(pre, 0.0).astype(BF)
+                pre_grad[:, at] = jnp.where(pre > 0, hg.astype(BF), jnp.zeros(hg.shape, BF))
+
+
+def activate(accs, vec, ogs, rows):
+    wide = vec.shape[1]
+    total = ogs[0].shape[0]
     bounds, lo = [], 0
     for acc in accs:
         bounds.append((lo, lo + acc.shape[0] // rows))
@@ -168,15 +175,17 @@
         pl.BlockSpec((rows, wide), lambda i, lo=lo, hi=hi: (jnp.clip(i - lo, 0, hi - lo - 1), 0))
         for lo, hi in bounds
     ]
+    specs.append(pl.BlockSpec(vec.shape, lambda i: (0, 0)))
+    specs += [pl.BlockSpec((rows, wide // 2), lambda i: (i, 0))] * 4
     at = pl.BlockSpec((rows, wide), lambda i: (i, 0))
     return pl.pallas_call(
         functools.partial(activate_body, bounds),
-        out_shape=(jax.ShapeDtypeStruct(hg.shape, BF),) * 2,
+        out_shape=(jax.ShapeDtypeStruct((total, wide), BF),) * 2,
         grid=(bounds[-1][1],),
-        in_specs=[*specs, pl.BlockSpec((1, wide), lambda i: (0, 0)), at],
+        in_specs=specs,
         out_specs=[at, at],
         cost_estimate=LIGHT,
-    )(*accs, bias, hg)
+    )(*accs, vec, *ogs)
 
 
 def nt_body(n_p, n_w, n_add, *refs):
@@ -191,7 +200,7 @@
         out[j * rows : (j + 1) * rows, :] = r.astype(BF)
 
 
-def nt_product(pre_grad, picks, ws, adds, rows, width, block, into=None):
+def nt_product(pre_grad, picks, ws, adds, rows, width, block, into=None, cost=LIGHT):
     steps = width // block
     operands, specs = [], []
     for o in picks:
@@ -224,7 +233,7 @@
         in_specs=specs,
         out_specs=pl.BlockSpec((height, block), lambda i: (0, first + i)),
         input_output_aliases=alias,
-        cost_estimate=LIGHT,
+        cost_estimate=cost,
     )(*operands)
 
 
@@ -300,7 +309,7 @@
     out[:, half:] = jnp.where(first, wide, total)
 
 
-def place(b, near, got, other, held, depth, at):
+def place(b, near, got, other, held, depth, at, cost=LIGHT):
     width, half = near.shape
     spec = pl.BlockSpec((width // 2, half), lambda i, b: (i, 0))
     operands, specs, alias = [near, got, other], [spec] * 3, {}
@@ -318,8 +327,52 @@
             out_specs=pl.BlockSpec((width // 2, 2 * half), lambda i, b: (2 * at + i, 0)),
         ),
         input_output_aliases=alias,
-        cost_estimate=LIGHT,
+        cost_estimate=cost,
     )(b, *operands)
+
+
+def lay(where, pieces, held, height, rows):
+    width = pieces[0].shape[1]
+    operands, specs, bounds, lo = [], [], [], 0
+    for v in pieces:
+        n = v.shape[0] // rows
+        operands.append(v)
+        specs.append(
+            pl.BlockSpec((rows, width), lambda i, at, lo=lo, n=n: (jnp.clip(i - lo, 0, n - 1), 0))
+        )
+        bounds.append((lo, lo + n))
+        lo += n
+    alias = {}
+    if held is not None:
+        alias = {len(operands) + 1: 0}
+        operands.append(held)
+        specs.append(pl.BlockSpec(memory_space=pl.ANY))
+
+    def body(at, *refs):
+        out = refs[-1]
+        half = width // 2
+        i = pl.program_id(0)
+        for ref, (a, e) in zip(refs, bounds):
+
+            @pl.when((i >= a) & (i < e))
+            def _():
+                m, o = ref[:, :half].astype(F32), ref[:, half:].astype(F32)
+                first = at[0] == 0
+                out[:, :half] = jnp.where(first, m, o).astype(BF)
+                out[:, half:] = jnp.where(first, o, m).astype(BF)
+
+    return pl.pallas_call(
+        body,
+        out_shape=jax.ShapeDtypeStruct((height, width), BF),
+        grid_spec=pltpu.PrefetchScalarGridSpec(
+            num_scalar_prefetch=1,
+            grid=(lo,),
+            in_specs=specs,
+            out_specs=pl.BlockSpec((rows, width), lambda i, at: (at[i + 1], 0)),
+        ),
+        input_output_aliases=alias,
+        cost_estimate=HEAVY,
+    )(where, *operands)
 
 
 def squares(acts, fc_weight, fc_bias, stitch, image_grad, crop_counts, row_image, row_live):
@@ -333,7 +386,7 @@
     tower = lax.axis_index("tower")
     nk = 6
     dk = depth // nk
-    wat = [0, 3, 5, 6]
+    wat = (0, 3, 5, 6)
     nw = len(wat) - 1
     block = 512 if dk % 512 == 0 else dk
 
@@ -341,6 +394,9 @@
 
     def tie(v, *deps):
         deps = [d for d in (*deps, *token) if d is not None]
+        return lax.optimization_barrier((v, *deps))[0] if deps else v
+
+    def only(v, *deps):
         return lax.optimization_barrier((v, *deps))[0] if deps else v
 
     def wait(v):
@@ -397,9 +453,14 @@
         picked = jnp.dot(match.astype(BF), g, preferred_element_type=F32)
         return (picked * scale[:, None]).astype(BF)
 
-    nz = 3
-    rz = rows // nz
+    zat = [c * rows // 384 for c in (0, 128, 256, 384)]
+    nz = len(zat) - 1
+    rz = rows - zat[-2]
+    first = x[: zat[1]]
+    late = lax.optimization_barrier((x, first))[0]
     V = {"X": x, "G": grads, "oc0": other_c}
+    for i in range(nz):
+        V[f"Z{i}"] = first if i == 0 else late[zat[i] : zat[i + 1]]
     for q in range(nw):
         V[f"W{q}"] = third(w_m, q)
     fb = dk
@@ -420,7 +481,11 @@
                 V[key] = sy(x)
                 continue
             if key in once:
-                if key == "m":
+                if key == "o":
+                    names = [n for n in V if n[0] in "ZW" and n != "Z0"]
+                    cut = lax.optimization_barrier((other_c, *(V[n] for n in names)))
+                    V.update(zip(["oc0", *names], cut))
+                elif key == "m":
                     small = jnp.stack([self_c, other_c, V["o"], fc_bias[0].astype(F32)])
                     V["small"] = jnp.concatenate([mine(small), other(small)], 1)
                 elif key == "a":
@@ -431,9 +496,6 @@
                 V[key] = f(V[src])
             else:
                 f, src = send[key[0]]
-                if src == "Z":
-                    i = int(key[1:])
-                    V[src + key[1:]] = tie(x)[i * rz : (i + 1) * rz]
                 V[key] = f(V[src + key[1:]])
         elif step[0] == "F":
             q0, q1 = int(step[1]), int(step[2])
@@ -449,19 +511,14 @@
             rest[0] = tie(rest[0])
             V[step[0]] = forward(rest, w_m, w_o, *weight_parts(q0, q1), V.get(step[0]))
             token[:] = [V[step[0]]]
-        elif step == "hg":
-            vec = four(V["small"], V["m"])
-            self4, other4, cross4 = vec[0], vec[1], vec[2]
-            out_wide = four(V["oga"], V["ogb"]).astype(F32)
-            theirs = four(V["a"], V["b"]).astype(F32)
-            hidden_grad = (self4[None] * out_wide + cross4[None] * theirs).astype(BF)
-            bias4 = vec[3][None]
-            V["hg"] = wait(hidden_grad)
         else:
             V[step] = wait(V[step])
     p = [V[f"p{q}"] for q in range(nw)]
     xg = [V[f"x{q}"] for q in range(nw)]
-    hidden, pre_grad = activate([V["F"], V["D"], V["E"]], bias4, V["hg"], rz)
+    vec = four(V["small"], V["m"])
+    self4, other4 = vec[0], vec[1]
+    ogs = [V[n] for n in ("oga", "ogb", "a", "b")]
+    hidden, pre_grad = activate([V["F"], V["D"], V["E"]], vec, ogs, rz)
     features = [*known(), V[f"z{nz - 1}"], *(V[f"d{i}"] for i in range(nz))]
     per = dk // block
 
@@ -470,9 +527,6 @@
         lo = (c - wat[q]) * per
         return [(w_m, c * per), (p[q], lo), (w_o, c * per), (xg[q], lo)]
 
-    def only(v, *deps):
-        return lax.optimization_barrier((v, *deps))[0] if deps else v
-
     def y_part(c, *deps):
         return nt_product(only(pre_grad, *deps), (1, 3), weights(c), (), rows, dk, block)
 
@@ -480,10 +534,12 @@
         g = only(pre_grad, *deps)
         return nt_product(g, (2,), weights(c), [(yy[c], 1, 0)], rows, dk, block)
 
-    def own_part(c, held):
+    def own_part(c, held, *deps):
         into = (held, (rows, depth), c * per)
+        g = only(pre_grad, *deps)
         return nt_product(
-            pre_grad, (0,), weights(c), [(yy[c], 0, 0), (zz[c], 0, 0)], rows, dk, block, into
+            g, (0,), weights(c), [(yy[c], 0, 0), (zz[c], 0, 0)], rows, dk, block, into,
+            HEAVY if c == nk - 1 else LIGHT,
         )
 
     def dw_sent(c, *deps):
@@ -546,7 +602,8 @@
         return kept, sp(sent)
 
     y_next, s_next = y_part(0), None
-    cut = 960 * rows // 384
+    cuts = [c * rows // 384 for c in (0, 960, 1536)]
+    st_kept, st_got = [], []
     for n in range(nk + 2):
         if n < nk:
             yy[n] = sy(y_next, s_next)
@@ -556,15 +613,22 @@
         extra = []
         if n == 0:
             hid_other = st(only(hidden, y_next))
+            out_wide = four(only(V["oga"], s_next), V["ogb"]).astype(F32)
             do_sums()
-            st_a0, st_g0 = st_piece((0, cut))
-            extra = [later["p"], st_g0]
+        if n in (0, 7):
+            piece = (0, 7).index(n)
+            kept, got_st = st_piece((cuts[piece], cuts[piece + 1]))
+            st_kept.append(kept)
+            if n == nk + 1:
+                st_got.append(got_st)
+            else:
+                extra.append(got_st)
         if 0 < n <= nk:
             zz[n - 1] = sz(z_part(n - 1))
             t[n - 1], k[n - 1] = dw_kept(n - 1)
             k_got[n - 1] = sp(k[n - 1])
-        if n == nk + 1 and cut < 4 * rows:
-            st_a1, st_g1 = st_piece((cut, 4 * rows))
+        if n == 0:
+            extra = [later["p"], *extra]
         if n == 1:
             do_sumx()
             extra = [later["s"]]
@@ -573,31 +637,34 @@
             own[n - 2] = own_part(n - 2, own[n - 3] if n > 2 else None)
         if 2 < n:
             put[n - 3] = place(
-                bvec, t[n - 3], k_got[n - 3], a[n - 3], put[n - 4] if n > 3 else None, depth, n - 3
+                bvec, t[n - 3], k_got[n - 3], a[n - 3], put[n - 4] if n > 3 else None, depth, n - 3,
+                HEAVY if n == nk + 1 else LIGHT,
             )
         if n + 1 < nk:
             y_next, s_next = y_part(n + 1), dw_sent(n + 1)
         outs = lump(n, *extra)
         if n == 0:
-            later["p"], st_g0 = outs
+            later["p"], *outs = outs
         if n == 1:
-            (later["s"],) = outs
+            later["s"], *outs = outs
+        st_got += outs
     token.clear()
     put[-1] = place(bvec, t[-1], k_got[-1], a[-1], put[-2], depth, nk - 1)
-    later["st_a"], later["st"] = st_a0, st_g0
-    if cut < 4 * rows:
-        later["st_a"] = jnp.concatenate([st_a0, st_a1], 0)
-        later["st"] = jnp.concatenate([st_g0, st_g1], 0)
     held_x, held_w = own[-1], put[-1]
-    st_a, st_got, s_a = later["st_a"], later["st"], later["s"]
+    s_a = later["s"]
     acts_grad, weight_grad = held_x, held_w
 
-    st_all = jnp.concatenate([st_a, st_got], 0)
-    st_all = natural(st_all[:, :half], st_all[:, half:])
-    st_all = st_all.reshape(8, rows, cols)
-    order = jnp.arange(8) ^ me
-    stitched_out = st_all[order].reshape(8 * rows, cols)
-
+    piece = rows // 2
+    tops = [lo // piece for lo in cuts]
+    spots = [2 * (me ^ (i // 2)) + i % 2 for i in range(16)]
+    ahead = [*range(8), *(8 + i for i in range(tops[-2]))]
+    last = [8 + i for i in range(tops[-2], tops[-1])]
+    stitched_out = lay(
+        jnp.stack([b, *(spots[i] for i in ahead)]), [*st_kept, *st_got[:-1]], None, 8 * rows, piece
+    )
+    stitched_out = lay(
+        jnp.stack([b, *(spots[i] for i in last)]), st_got[-1:], stitched_out, 8 * rows, piece
+    )
     own_s, other_s = s_a[0], s_a[1]
     stitch_grad = jnp.where(tower == 0, jnp.stack([own_s, other_s]), jnp.stack([other_s, own_s]))
     return (

time: 798 us -> 785 us (0.984)
  other arithmetic: 29.4 us -> 18.2 us
  Pallas kernels: 297 us -> 306 us
    pallas_call x0 -> x2, Pallas kernels: none -> 12.9 us  [lay(): pl.pallas_call(body, out_shape=jax.ShapeDtypeStruct((height, width), BF),...]
    concatenate x1 -> x2, other arithmetic: 10.5 us -> 1.93 us  [st_piece(): jnp.concatenate([stitched[:, :half], stitched[:, cols:cols + half]], 1)]
    pallas_call x6 -> x5, Pallas kernels: 67.7 us -> 62.1 us  [forward(): pl.pallas_call(functools.partial(forward_body, len(xs), starts, acc is no...]
  transfers between devices with their start and end apart: 53 -> 53, of which waited for: 25 -> 29; matrix products, arithmetic and copies ran while one was open for 9% -> 7% of each run, Pallas kernels for 35% -> 35%
where the time goes in v3:
time: 785 us; the launch traced here: 775 us
  waiting for transfers between devices  341 us (43%)
  Pallas kernels  306 us (39%)
  starting transfers between devices  64.4 us (8%)
  local copies, waits for them, and re-layouts  37.1 us (5%)
  other arithmetic  18.2 us (2%)
    ppermute x53, waiting for transfers between devices, swapped(): return lax.ppermute(block, axis, [(i, i ^ mask) for i in range(count)])  341 us
    pallas_call x18, Pallas kernels, nt_product(): pl.pallas_call(body, out_shape=jax.ShapeDtypeStruct(shape, BF), grid=(ste...  102 us
    pallas_call x12, Pallas kernels, tn_product(): pl.pallas_call(body, out_shape=outs, grid=(steps,), in_specs=specs, out_s...  83.4 us
    ppermute x53, starting transfers between devices, swapped(): return lax.ppermute(block, axis, [(i, i ^ mask) for i in range(count)])  64.4 us
    pallas_call x5, Pallas kernels, forward(): pl.pallas_call(functools.partial(forward_body, len(xs), starts, acc is no...  62.1 us
    pallas_call x6, Pallas kernels, place(): pl.pallas_call(place_body, out_shape=jax.ShapeDtypeStruct((depth, 2 * hal...  19.3 us
  transfers between devices with their start and end apart: 53, of which 29 were waited for; matrix products, arithmetic and copies ran while one was open for 7% of the time, Pallas kernels for 35%

profile of v3, /device:TPU:0, one launch (start us, length us, event | category | flops | bytes accessed | tf_op | source)
XLA Modules:
  0.0 774.5 jit_solution(2870556280451596054)
XLA Ops:
  22.6 35.7 %collective-permute-done.1.refs_2_ = bf16[128,9216]{1,0:T(8,128)(2,1)S(1)} collective-permute-done((bf16[128,9216]{1,0:T(8,128)(2,1)}, bf16[128,9216]{1,0:T(8,128)(2,1)S(1)}, u32[]{:S(2)}, u32[]{:S(2)}) %collective-permute-start.1) | collective-permute-done | bytes 2359328 | tf_op jit(solution)/shard_map/ppermute | solution.py:16
  67.9 93.7 %collective-permute-done.3.refs_3_ = bf16[128,9216]{1,0:T(8,128)(2,1)} collective-permute-done((bf16[128,9216]{1,0:T(8,128)(2,1)}, bf16[128,9216]{1,0:T(8,128)(2,1)}, u32[]{:S(2)}, u32[]{:S(2)}) %collective-permute-start.3) | collective-permute-done | bytes 2359328 | tf_op jit(solution)/shard_map/ppermute | solution.py:16
  169.6 6.5 dynamic-slice_bitcast_fusion
  177.6 35.3 %collective-permute-done.6.refs_1_.refs_5_ = bf16[128,9216]{1,0:T(8,128)(2,1)S(1)} collective-permute-done((bf16[128,9216]{1,0:T(8,128)(2,1)S(1)}, bf16[128,9216]{1,0:T(8,128)(2,1)S(1)}, u32[]{:S(2)}, u32[]{:S(2)}) %collective-permute-start.6) | collective-permute-done | bytes 2359328 | tf_op jit(solution)/shard_map/ppermute | solution.py:16
  215.7 15.4 %shard_map.119.refs_10_ = f32[1024,1024]{1,0:T(8,128)} custom-call(bf16[384,9216]{1,0:T(8,128)(2,1)} %bitcast.52, bf16[384,9216]{1,0:T(8,128)(2,1)} %collective-permute-done.7.refs_1_, bf16[128,9216]{1,0:T(8,128)(2,1)} %copy-done.1, bf16[128,9216]{1,0:T(8,128)(2,1)} %collective-permute-done.3.refs_3_, ...), custom_call_target="tpu_custom_call" | custom-call | flops 1000 | bytes 1000 | tf_op jit(solution)/shard_map/pallas_call | solution.py:139
  231.1 17.3 %collective-permute-done.4.refs_6_.refs_4_.refs_3_.refs_2_ = bf16[3072,256]{1,0:T(8,128)(2,1)} collective-permute-done((bf16[3072,256]{1,0:T(8,128)(2,1)}, bf16[3072,256]{1,0:T(8,128)(2,1)}, u32[]{:S(2)}, u32[]{:S(2)}) %collective-permute-start.4) | collective-permute-done | bytes 1572896 | tf_op jit(solution)/shard_map/ppermute | solution.py:16
  256.1 28.8 %collective-permute-done.9.refs_7_.refs_5_.refs_3_.refs_2_ = bf16[1536,256]{1,0:T(8,128)(2,1)S(1)} collective-permute-done((bf16[1536,256]{1,0:T(8,128)(2,1)}, bf16[1536,256]{1,0:T(8,128)(2,1)S(1)}, u32[]{:S(2)}, u32[]{:S(2)}) %collective-permute-start.9) | collective-permute-done | bytes 786464 | tf_op jit(solution)/shard_map/ppermute | solution.py:16
  288.4 12.6 %shard_map.120.refs_7_ = f32[384,1024]{1,0:T(8,128)} custom-call(bf16[128,9216]{1,0:T(8,128)(2,1)} %collective-permute-done.10.refs_0_.refs_4_, bf16[128,9216]{1,0:T(8,128)(2,1)} %copy-done.2, bf16[128,9216]{1,0:T(8,128)(2,1)} %collective-permute-done.15.refs_2_.refs_6_, bf16[9216,256]{1,0:T(8,128)(2,1)} %get-tuple-element.262.refs_4_.refs_3_.refs_1_.refs_2_, ...), custom_call_target="tpu_custom_call" | custom-call | flops 1000 | bytes 1000 | tf_op jit(solution)/shard_map/pallas_call | solution.py:139
  304.1 18.4 %shard_map.121.refs_0_ = f32[1024,1024]{1,0:T(8,128)} custom-call(bf16[384,9216]{1,0:T(8,128)(2,1)} %bitcast.53, bf16[384,9216]{1,0:T(8,128)(2,1)} %collective-permute-done.7.refs_1_, bf16[128,9216]{1,0:T(8,128)(2,1)} %copy-done.1, bf16[128,9216]{1,0:T(8,128)(2,1)} %collective-permute-done.3.refs_3_, ...), custom_call_target="tpu_custom_call" | custom-call | flops 1000 | bytes 1000 | tf_op jit(solution)/shard_map/pallas_call | solution.py:139
  337.2 10.4 %shard_map.123.refs_2_ = f32[128,1024]{1,0:T(8,128)} custom-call(bf16[128,9216]{1,0:T(8,128)(2,1)} %copy-done.3, bf16[9216,256]{1,0:T(8,128)(2,1)} %get-tuple-element.262.refs_4_.refs_3_.refs_1_.refs_2_, bf16[9216,256]{1,0:T(8,128)(2,1)} %get-tuple-element.261.refs_5_.refs_4_.refs_2_.refs_3_, ...), custom_call_target="tpu_custom_call" | custom-call | flops 1000 | bytes 1000 | tf_op jit(solution)/shard_map/pallas_call | solution.py:139
  349.4 11.5 %shard_map.124 = (bf16[1536,1024]{1,0:T(8,128)(2,1)}, bf16[1536,1024]{1,0:T(8,128)(2,1)}) custom-call(f32[1024,1024]{1,0:T(8,128)} %shard_map.121.refs_0_, f32[384,1024]{1,0:T(8,128)} %shard_map.122.refs_1_, f32[128,1024]{1,0:T(8,128)} %shard_map.123.refs_2_, f32[4,1024]{1,0:T(4,128)} %pad_maximum_fusion.6.refs_3_, bf16[1536,512]{1,0:T(8,128)(2,1)} %copy-done.9, ...), custom_call_target="tpu_custom_call" | custom-call | flops 1000 | bytes 1000 | tf_op jit(solution)/shard_map/pallas_call | solution.py:181
  370.8 6.8 shard_map.136
  398.2 6.5 shard_map.135
  404.7 9.4 %collective-permute-done.20.refs_9_ = bf16[1536,512]{1,0:T(8,128)(2,1)} collective-permute-done((bf16[1536,512]{1,0:T(8,128)(2,1)}, bf16[1536,512]{1,0:T(8,128)(2,1)}, u32[]{:S(2)}, u32[]{:S(2)}) %collective-permute-start.20) | collective-permute-done | bytes 1572896 | tf_op jit(solution)/shard_map/ppermute | solution.py:16
  414.1 9.7 %collective-permute-done.19.refs_5_ = bf16[768,1536]{1,0:T(8,128)(2,1)} collective-permute-done((bf16[768,1536]{1,0:T(8,128)(2,1)}, bf16[768,1536]{1,0:T(8,128)(2,1)}, u32[]{:S(2)}, u32[]{:S(2)}) %collective-permute-start.19) | collective-permute-done | bytes 2359328 | tf_op jit(solution)/shard_map/ppermute | solution.py:16
  423.8 6.8 collective-permute-done.21
  438.2 7.2 shard_map.138
  455.5 6.6 shard_map.133
  462.1 6.6 collective-permute-done.27
  469.2 11.4 %collective-permute-done.26.got = bf16[1536,256]{1,0:T(8,128)(2,1)S(1)} collective-permute-done((bf16[1536,256]{1,0:T(8,128)(2,1)}, bf16[1536,256]{1,0:T(8,128)(2,1)S(1)}, u32[]{:S(2)}, u32[]{:S(2)}) %collective-permute-start.26) | collective-permute-done | bytes 786464 | tf_op jit(solution)/shard_map/ppermute | solution.py:16
  491.7 7.3 shard_map.140
  511.3 6.6 shard_map.131
  523.7 9.6 %collective-permute-done.31.got = bf16[1536,256]{1,0:T(8,128)(2,1)S(1)} collective-permute-done((bf16[1536,256]{1,0:T(8,128)(2,1)}, bf16[1536,256]{1,0:T(8,128)(2,1)S(1)}, u32[]{:S(2)}, u32[]{:S(2)}) %collective-permute-start.31) | collective-permute-done | bytes 786464 | tf_op jit(solution)/shard_map/ppermute | solution.py:16
  544.8 7.5 shard_map.144
  564.6 6.6 shard_map.129
  597.7 7.3 shard_map.149
  617.3 6.6 shard_map.127
  649.2 7.2 shard_map.154
  671.4 15.6 %collective-permute-done.46.got = bf16[1536,256]{1,0:T(8,128)(2,1)S(1)} collective-permute-done((bf16[1536,256]{1,0:T(8,128)(2,1)}, bf16[1536,256]{1,0:T(8,128)(2,1)S(1)}, u32[]{:S(2)}, u32[]{:S(2)}) %collective-permute-start.46) | collective-permute-done | bytes 786464 | tf_op jit(solution)/shard_map/ppermute | solution.py:16
  698.7 7.3 shard_map.159
  725.2 11.6 %collective-permute-done.49.got = bf16[1536,256]{1,0:T(8,128)(2,1)S(1)} collective-permute-done((bf16[1536,256]{1,0:T(8,128)(2,1)}, bf16[1536,256]{1,0:T(8,128)(2,1)S(1)}, u32[]{:S(2)}, u32[]{:S(2)}) %collective-permute-start.49) | collective-permute-done | bytes 786464 | tf_op jit(solution)/shard_map/ppermute | solution.py:16
  746.7 9.5 %shard_map.163.refs_1_ = bf16[3072,512]{1,0:T(8,128)(2,1)} custom-call(s32[14]{0:T(128)} %stack.109.at, bf16[960,512]{1,0:T(8,128)(2,1)} %pad_maximum_fusion.3.refs_0_, bf16[576,512]{1,0:T(8,128)(2,1)} %pad_maximum_fusion.5.refs_1_, bf16[960,512]{1,0:T(8,128)(2,1)} %collective-permute-done.22.refs_2_), custom_call_target="tpu_custom_call" | custom-call | flops 1000 | bytes 60000000 | tf_op jit(solution)/shard_map/pallas_call | solution.py:364
  (264 shorter events, 313.9 us)
Async XLA Ops:
  3.9 54.5 %collective-permute-start.1 = (bf16[128,9216]{1,0:T(8,128)(2,1)}, bf16[128,9216]{1,0:T(8,128)(2,1)S(1)}, u32[]{:S(2)}, u32[]{:S(2)}) collective-permute-start(bf16[128,9216]{1,0:T(8,128)(2,1)} %slice_bitcast_fusion), channel_id=1, source_target_pairs={{0,2},{1,3},{2,0},{3,1},{4,6},{5,7},{6,4},{7,5},{8,10},{9,11},{10,... | collective-permute-start | bytes 7077896 | tf_op jit(solution)/shard_map/ppermute | solution.py:16
  6.9 169.2 %collective-permute-start.7 = (bf16[384,9216]{1,0:T(8,128)(2,1)}, bf16[384,9216]{1,0:T(8,128)(2,1)}, u32[]{:S(2)}, u32[]{:S(2)}) collective-permute-start(bf16[384,9216]{1,0:T(8,128)(2,1)} %bitcast.50), channel_id=1, source_target_pairs={{0,1},{1,0},{2,3},{3,2},{4,5},{5,4},{6,7},{7,6},{8,9},{9,8},{10,11... | collective-permute-start | bytes 21233672 | tf_op jit(solution)/shard_map/ppermute | solution.py:16
  58.4 103.3 %collective-permute-start.3 = (bf16[128,9216]{1,0:T(8,128)(2,1)}, bf16[128,9216]{1,0:T(8,128)(2,1)}, u32[]{:S(2)}, u32[]{:S(2)}) collective-permute-start(bf16[128,9216]{1,0:T(8,128)(2,1)} %get-tuple-element.136), channel_id=1, source_target_pairs={{0,2},{1,3},{2,0},{3,1},{4,6},{5,7},{6,4},{7,5},{8,10},{9,11},{10,... | collective-permute-start | bytes 7077896 | tf_op jit(solution)/shard_map/ppermute | solution.py:16
  60.1 103.8 %collective-permute-start.2 = (bf16[4608,256]{1,0:T(8,128)(2,1)}, bf16[4608,256]{1,0:T(8,128)(2,1)}, u32[]{:S(2)}, u32[]{:S(2)}) collective-permute-start(bf16[4608,256]{1,0:T(8,128)(2,1)} %dynamic-slice_bitcast_fusion.2), channel_id=1, source_target_pairs={{0,4},{1,5},{2,6},{3,7},{4,0},{5,1},{6,2},{7,3},{8,12},{9,13},{10,... | collective-permute-start | bytes 7077896 | tf_op jit(solution)/shard_map/ppermute | solution.py:16
  66.3 99.6 %collective-permute-start.8 = (bf16[1536,512]{1,0:T(8,128)(2,1)S(1)}, bf16[1536,512]{1,0:T(8,128)(2,1)S(1)}, u32[]{:S(2)}, u32[]{:S(2)}) collective-permute-start(bf16[1536,512]{1,0:T(8,128)(2,1)S(1)} %fusion.9.refs_4_), channel_id=1, source_target_pairs={{0,16},{16,0},{1,17},{17,1},{2,18},{18,2},{3,19},{19,3},{4,20},{20... | collective-permute-start | bytes 4718600 | tf_op jit(solution)/shard_map/ppermute | solution.py:16
  66.4 146.5 %collective-permute-start.6 = (bf16[128,9216]{1,0:T(8,128)(2,1)S(1)}, bf16[128,9216]{1,0:T(8,128)(2,1)S(1)}, u32[]{:S(2)}, u32[]{:S(2)}) collective-permute-start(bf16[128,9216]{1,0:T(8,128)(2,1)S(1)} %collective-permute-done.1.refs_2_), channel_id=1, source_target_pairs={{0,1},{1,0},{2,3},{3,2},{4,5},{5,4},{6,7},{7,6},{8,9},{9,8},{10,11... | collective-permute-start | bytes 7077896 | tf_op jit(solution)/shard_map/ppermute | solution.py:16
  163.9 50.4 %collective-permute-start.5 = (bf16[4608,256]{1,0:T(8,128)(2,1)}, bf16[4608,256]{1,0:T(8,128)(2,1)S(1)}, u32[]{:S(2)}, u32[]{:S(2)}) collective-permute-start(bf16[4608,256]{1,0:T(8,128)(2,1)} %collective-permute-done.2.refs_6_.refs_5_.refs_3_.refs_2_), channel_id=1, source_target_pairs={{0,8},{8,0},{1,9},{9,1},{2,10},{10,2},{3,11},{11,3},{4,12},{12,4},... | collective-permute-start | bytes 7077896 | tf_op jit(solution)/shard_map/ppermute | solution.py:16
  165.4 83.8 %collective-permute-start.10 = (bf16[128,9216]{1,0:T(8,128)(2,1)}, bf16[128,9216]{1,0:T(8,128)(2,1)}, u32[]{:S(2)}, u32[]{:S(2)}) collective-permute-start(bf16[128,9216]{1,0:T(8,128)(2,1)} %get-tuple-element.151), channel_id=1, source_target_pairs={{0,2},{1,3},{2,0},{3,1},{4,6},{5,7},{6,4},{7,5},{8,10},{9,11},{10,... | collective-permute-start | bytes 7077896 | tf_op jit(solution)/shard_map/ppermute | solution.py:16
  167.0 81.4 %collective-permute-start.4 = (bf16[3072,256]{1,0:T(8,128)(2,1)}, bf16[3072,256]{1,0:T(8,128)(2,1)}, u32[]{:S(2)}, u32[]{:S(2)}) collective-permute-start(bf16[3072,256]{1,0:T(8,128)(2,1)} %dynamic-slice_bitcast_fusion.3), channel_id=1, source_target_pairs={{0,4},{1,5},{2,6},{3,7},{4,0},{5,1},{6,2},{7,3},{8,12},{9,13},{10,... | collective-permute-start | bytes 4718600 | tf_op jit(solution)/shard_map/ppermute | solution.py:16
  176.1 112.3 %collective-permute-start.15 = (bf16[128,9216]{1,0:T(8,128)(2,1)}, bf16[128,9216]{1,0:T(8,128)(2,1)}, u32[]{:S(2)}, u32[]{:S(2)}) collective-permute-start(bf16[128,9216]{1,0:T(8,128)(2,1)} %collective-permute-done.3.refs_3_), channel_id=1, source_target_pairs={{0,1},{1,0},{2,3},{3,2},{4,5},{5,4},{6,7},{7,6},{8,9},{9,8},{10,11... | collective-permute-start | bytes 7077896 | tf_op jit(solution)/shard_map/ppermute | solution.py:16
  249.2 78.6 %collective-permute-start.13 = (bf16[128,9216]{1,0:T(8,128)(2,1)}, bf16[128,9216]{1,0:T(8,128)(2,1)S(1)}, u32[]{:S(2)}, u32[]{:S(2)}) collective-permute-start(bf16[128,9216]{1,0:T(8,128)(2,1)} %collective-permute-done.10.refs_0_.refs_4_), channel_id=1, source_target_pairs={{0,1},{1,0},{2,3},{3,2},{4,5},{5,4},{6,7},{7,6},{8,9},{9,8},{10,11... | collective-permute-start | bytes 7077896 | tf_op jit(solution)/shard_map/ppermute | solution.py:16
  284.8 47.8 %collective-permute-start.12 = (bf16[1024,512]{1,0:T(8,128)(2,1)}, bf16[1024,512]{1,0:T(8,128)(2,1)}, u32[]{:S(2)}, u32[]{:S(2)}) collective-permute-start(bf16[1024,512]{1,0:T(8,128)(2,1)} %pad_maximum_fusion.1), channel_id=1, source_target_pairs={{0,4},{1,5},{2,6},{3,7},{4,0},{5,1},{6,2},{7,3},{8,12},{9,13},{10,... | collective-permute-start | bytes 3145736 | tf_op jit(solution)/shard_map/ppermute | solution.py:16
  286.4 50.8 %collective-permute-start.11 = (f32[4,512]{1,0:T(4,128)S(1)}, f32[4,512]{1,0:T(4,128)S(1)}, u32[]{:S(2)}, u32[]{:S(2)}) collective-permute-start(f32[4,512]{1,0:T(4,128)S(1)} %pad_maximum_fusion.9), channel_id=1, source_target_pairs={{0,4},{1,5},{2,6},{3,7},{4,0},{5,1},{6,2},{7,3},{8,12},{9,13},{10,... | collective-permute-start | bytes 24584 | tf_op jit(solution)/shard_map/ppermute | solution.py:16
  370.3 53.5 %collective-permute-start.19 = (bf16[768,1536]{1,0:T(8,128)(2,1)}, bf16[768,1536]{1,0:T(8,128)(2,1)}, u32[]{:S(2)}, u32[]{:S(2)}) collective-permute-start(bf16[768,1536]{1,0:T(8,128)(2,1)} %shard_map.125), channel_id=1, source_target_pairs={{0,1},{1,0},{2,3},{3,2},{4,5},{5,4},{6,7},{7,6},{8,9},{9,8},{10,11... | collective-permute-start | bytes 7077896 | tf_op jit(solution)/shard_map/ppermute | solution.py:16
  385.8 44.8 %collective-permute-start.22 = (bf16[960,512]{1,0:T(8,128)(2,1)}, bf16[960,512]{1,0:T(8,128)(2,1)}, u32[]{:S(2)}, u32[]{:S(2)}) collective-permute-start(bf16[960,512]{1,0:T(8,128)(2,1)} %pad_maximum_fusion.2), channel_id=1, source_target_pairs={{0,4},{1,5},{2,6},{3,7},{4,0},{5,1},{6,2},{7,3},{8,12},{9,13},{10,... | collective-permute-start | bytes 2949128 | tf_op jit(solution)/shard_map/ppermute | solution.py:16
  389.0 41.6 %collective-permute-start.21 = (f32[3,512]{1,0:T(4,128)S(1)}, f32[3,512]{1,0:T(4,128)S(1)}, u32[]{:S(2)}, u32[]{:S(2)}) collective-permute-start(f32[3,512]{1,0:T(4,128)S(1)} %pad_maximum_fusion.10), channel_id=1, source_target_pairs={{0,4},{1,5},{2,6},{3,7},{4,0},{5,1},{6,2},{7,3},{8,12},{9,13},{10,... | collective-permute-start | bytes 18440 | tf_op jit(solution)/shard_map/ppermute | solution.py:16
  430.6 53.5 %collective-permute-start.23 = (bf16[768,1536]{1,0:T(8,128)(2,1)}, bf16[768,1536]{1,0:T(8,128)(2,1)S(1)}, u32[]{:S(2)}, u32[]{:S(2)}) collective-permute-start(bf16[768,1536]{1,0:T(8,128)(2,1)} %shard_map.134), channel_id=1, source_target_pairs={{0,1},{1,0},{2,3},{3,2},{4,5},{5,4},{6,7},{7,6},{8,9},{9,8},{10,11... | collective-permute-start | bytes 7077896 | tf_op jit(solution)/shard_map/ppermute | solution.py:16
  432.1 50.7 %collective-permute-start.24 = (bf16[1536,512]{1,0:T(8,128)(2,1)}, bf16[1536,512]{1,0:T(8,128)(2,1)}, u32[]{:S(2)}, u32[]{:S(2)}) collective-permute-start(bf16[1536,512]{1,0:T(8,128)(2,1)} %shard_map.135), channel_id=1, source_target_pairs={{0,8},{8,0},{1,9},{9,1},{2,10},{10,2},{3,11},{11,3},{4,12},{12,4},... | collective-permute-start | bytes 4718600 | tf_op jit(solution)/shard_map/ppermute | solution.py:16
  438.2 44.6 %collective-permute-start.25 = (bf16[384,1536]{1,0:T(8,128)(2,1)}, bf16[384,1536]{1,0:T(8,128)(2,1)}, u32[]{:S(2)}, u32[]{:S(2)}) collective-permute-start(bf16[384,1536]{1,0:T(8,128)(2,1)} %shard_map.137), channel_id=1, source_target_pairs={{0,2},{1,3},{2,0},{3,1},{4,6},{5,7},{6,4},{7,5},{8,10},{9,11},{10,... | collective-permute-start | bytes 3538952 | tf_op jit(solution)/shard_map/ppermute | solution.py:16
  484.1 54.0 %collective-permute-start.28 = (bf16[768,1536]{1,0:T(8,128)(2,1)}, bf16[768,1536]{1,0:T(8,128)(2,1)}, u32[]{:S(2)}, u32[]{:S(2)}) collective-permute-start(bf16[768,1536]{1,0:T(8,128)(2,1)} %shard_map.132), channel_id=1, source_target_pairs={{0,1},{1,0},{2,3},{3,2},{4,5},{5,4},{6,7},{7,6},{8,9},{9,8},{10,11... | collective-permute-start | bytes 7077896 | tf_op jit(solution)/shard_map/ppermute | solution.py:16
  485.6 52.4 %collective-permute-start.29 = (bf16[1536,512]{1,0:T(8,128)(2,1)}, bf16[1536,512]{1,0:T(8,128)(2,1)}, u32[]{:S(2)}, u32[]{:S(2)}) collective-permute-start(bf16[1536,512]{1,0:T(8,128)(2,1)} %shard_map.133), channel_id=1, source_target_pairs={{0,8},{8,0},{1,9},{9,1},{2,10},{10,2},{3,11},{11,3},{4,12},{12,4},... | collective-permute-start | bytes 4718600 | tf_op jit(solution)/shard_map/ppermute | solution.py:16
  491.7 46.3 %collective-permute-start.30 = (bf16[384,1536]{1,0:T(8,128)(2,1)}, bf16[384,1536]{1,0:T(8,128)(2,1)}, u32[]{:S(2)}, u32[]{:S(2)}) collective-permute-start(bf16[384,1536]{1,0:T(8,128)(2,1)} %shard_map.139), channel_id=1, source_target_pairs={{0,2},{1,3},{2,0},{3,1},{4,6},{5,7},{6,4},{7,5},{8,10},{9,11},{10,... | collective-permute-start | bytes 3538952 | tf_op jit(solution)/shard_map/ppermute | solution.py:16
  538.0 51.9 %collective-permute-start.33 = (bf16[768,1536]{1,0:T(8,128)(2,1)S(1)}, bf16[768,1536]{1,0:T(8,128)(2,1)}, u32[]{:S(2)}, u32[]{:S(2)}) collective-permute-start(bf16[768,1536]{1,0:T(8,128)(2,1)S(1)} %copy-done.18), channel_id=1, source_target_pairs={{0,1},{1,0},{2,3},{3,2},{4,5},{5,4},{6,7},{7,6},{8,9},{9,8},{10,11... | collective-permute-start | bytes 7077896 | tf_op jit(solution)/shard_map/ppermute | solution.py:16
  538.6 51.3 %collective-permute-start.34 = (bf16[1536,512]{1,0:T(8,128)(2,1)}, bf16[1536,512]{1,0:T(8,128)(2,1)}, u32[]{:S(2)}, u32[]{:S(2)}) collective-permute-start(bf16[1536,512]{1,0:T(8,128)(2,1)} %shard_map.131), channel_id=1, source_target_pairs={{0,8},{8,0},{1,9},{9,1},{2,10},{10,2},{3,11},{11,3},{4,12},{12,4},... | collective-permute-start | bytes 4718600 | tf_op jit(solution)/shard_map/ppermute | solution.py:16
  544.8 45.2 %collective-permute-start.35 = (bf16[384,1536]{1,0:T(8,128)(2,1)}, bf16[384,1536]{1,0:T(8,128)(2,1)}, u32[]{:S(2)}, u32[]{:S(2)}) collective-permute-start(bf16[384,1536]{1,0:T(8,128)(2,1)} %shard_map.143), channel_id=1, source_target_pairs={{0,2},{1,3},{2,0},{3,1},{4,6},{5,7},{6,4},{7,5},{8,10},{9,11},{10,... | collective-permute-start | bytes 3538952 | tf_op jit(solution)/shard_map/ppermute | solution.py:16
  589.9 52.7 %collective-permute-start.38 = (bf16[768,1536]{1,0:T(8,128)(2,1)}, bf16[768,1536]{1,0:T(8,128)(2,1)S(1)}, u32[]{:S(2)}, u32[]{:S(2)}) collective-permute-start(bf16[768,1536]{1,0:T(8,128)(2,1)} %shard_map.128), channel_id=1, source_target_pairs={{0,1},{1,0},{2,3},{3,2},{4,5},{5,4},{6,7},{7,6},{8,9},{9,8},{10,11... | collective-permute-start | bytes 7077896 | tf_op jit(solution)/shard_map/ppermute | solution.py:16
  591.5 51.1 %collective-permute-start.39 = (bf16[1536,512]{1,0:T(8,128)(2,1)}, bf16[1536,512]{1,0:T(8,128)(2,1)}, u32[]{:S(2)}, u32[]{:S(2)}) collective-permute-start(bf16[1536,512]{1,0:T(8,128)(2,1)} %shard_map.129), channel_id=1, source_target_pairs={{0,8},{8,0},{1,9},{9,1},{2,10},{10,2},{3,11},{11,3},{4,12},{12,4},... | collective-permute-start | bytes 4718600 | tf_op jit(solution)/shard_map/ppermute | solution.py:16
  597.7 44.9 %collective-permute-start.40 = (bf16[384,1536]{1,0:T(8,128)(2,1)}, bf16[384,1536]{1,0:T(8,128)(2,1)}, u32[]{:S(2)}, u32[]{:S(2)}) collective-permute-start(bf16[384,1536]{1,0:T(8,128)(2,1)} %shard_map.148), channel_id=1, source_target_pairs={{0,2},{1,3},{2,0},{3,1},{4,6},{5,7},{6,4},{7,5},{8,10},{9,11},{10,... | collective-permute-start | bytes 3538952 | tf_op jit(solution)/shard_map/ppermute | solution.py:16
  642.6 49.5 %collective-permute-start.43 = (bf16[768,1536]{1,0:T(8,128)(2,1)}, bf16[768,1536]{1,0:T(8,128)(2,1)}, u32[]{:S(2)}, u32[]{:S(2)}) collective-permute-start(bf16[768,1536]{1,0:T(8,128)(2,1)} %shard_map.126), channel_id=1, source_target_pairs={{0,1},{1,0},{2,3},{3,2},{4,5},{5,4},{6,7},{7,6},{8,9},{9,8},{10,11... | collective-permute-start | bytes 7077896 | tf_op jit(solution)/shard_map/ppermute | solution.py:16
  642.8 49.4 %collective-permute-start.44 = (bf16[1536,512]{1,0:T(8,128)(2,1)}, bf16[1536,512]{1,0:T(8,128)(2,1)}, u32[]{:S(2)}, u32[]{:S(2)}) collective-permute-start(bf16[1536,512]{1,0:T(8,128)(2,1)} %shard_map.127), channel_id=1, source_target_pairs={{0,8},{8,0},{1,9},{9,1},{2,10},{10,2},{3,11},{11,3},{4,12},{12,4},... | collective-permute-start | bytes 4718600 | tf_op jit(solution)/shard_map/ppermute | solution.py:16
  649.2 42.9 %collective-permute-start.45 = (bf16[384,1536]{1,0:T(8,128)(2,1)}, bf16[384,1536]{1,0:T(8,128)(2,1)S(1)}, u32[]{:S(2)}, u32[]{:S(2)}) collective-permute-start(bf16[384,1536]{1,0:T(8,128)(2,1)} %shard_map.153), channel_id=1, source_target_pairs={{0,2},{1,3},{2,0},{3,1},{4,6},{5,7},{6,4},{7,5},{8,10},{9,11},{10,... | collective-permute-start | bytes 3538952 | tf_op jit(solution)/shard_map/ppermute | solution.py:16
  698.7 40.2 %collective-permute-start.48 = (bf16[384,1536]{1,0:T(8,128)(2,1)}, bf16[384,1536]{1,0:T(8,128)(2,1)S(1)}, u32[]{:S(2)}, u32[]{:S(2)}) collective-permute-start(bf16[384,1536]{1,0:T(8,128)(2,1)} %shard_map.156), channel_id=1, source_target_pairs={{0,2},{1,3},{2,0},{3,1},{4,6},{5,7},{6,4},{7,5},{8,10},{9,11},{10,... | collective-permute-start | bytes 3538952 | tf_op jit(solution)/shard_map/ppermute | solution.py:16
  (66 other events, 1158.3 us)

commit v4 on v3

--- a/solution.py
+++ b/solution.py
@@ -94,7 +94,7 @@
     ps = [rest.pop(0) for _ in range(n_q)]
     gs = [rest.pop(0) for _ in range(n_q)]
     acc_in = rest.pop(0) if has_acc else None
-    out = rest[0]
+    out, features, weights = rest
     i = pl.program_id(0)
     half = w_m.shape[1]
 
@@ -105,18 +105,20 @@
         else:
             out[...] = jnp.zeros_like(out)
 
+    lo = 0
+    for x in xs:
+        features[lo : lo + x.shape[0], :] = x[...]
+        lo += x.shape[0]
+    weights[:, :half] = w_m[...]
+    weights[:, 2 * half : 3 * half] = w_o[...]
     for q in range(n_q):
 
         @pl.when((i >= starts[q]) & (i < starts[q + 1]))
         def _():
-            lo = 0
-            for x in xs:
-                rows = x.shape[0]
-                for j, w in enumerate((w_m, ps[q], w_o, gs[q])):
-                    out[lo : lo + rows, j * half : (j + 1) * half] += jnp.dot(
-                        x[...], w[...], preferred_element_type=F32
-                    )
-                lo += rows
+            weights[:, half : 2 * half] = ps[q][...]
+            weights[:, 3 * half :] = gs[q][...]
+
+    out[...] += jnp.dot(features[...], weights[...], preferred_element_type=F32)
 
 
 def forward(xs, w_m, w_o, ps, gs, lo, block, acc=None):
@@ -142,6 +144,7 @@
         grid=(starts[-1],),
         in_specs=specs,
         out_specs=wide,
+        scratch_shapes=[pltpu.VMEM((rows, block), BF), pltpu.VMEM((block, 4 * half), BF)],
         cost_estimate=LIGHT,
     )(*operands)
 

time: 785 us -> 788 us (level)
  transfers between devices with their start and end apart: 53 -> 53, of which waited for: 29 -> 29; matrix products, arithmetic and copies ran while one was open for 7% -> 7% of each run, Pallas kernels for 35% -> 36%
where the time goes in v4:
time: 788 us; the launch traced here: 776 us
  waiting for transfers between devices  336 us (43%)
  Pallas kernels  312 us (40%)
  starting transfers between devices  64.4 us (8%)
  local copies, waits for them, and re-layouts  37.1 us (5%)
  other arithmetic  18.2 us (2%)
    ppermute x53, waiting for transfers between devices, swapped(): return lax.ppermute(block, axis, [(i, i ^ mask) for i in range(count)])  336 us
    pallas_call x18, Pallas kernels, nt_product(): pl.pallas_call(body, out_shape=jax.ShapeDtypeStruct(shape, BF), grid=(ste...  102 us
    pallas_call x12, Pallas kernels, tn_product(): pl.pallas_call(body, out_shape=outs, grid=(steps,), in_specs=specs, out_s...  83.2 us
    pallas_call x5, Pallas kernels, forward(): pl.pallas_call(functools.partial(forward_body, len(xs), starts, acc is no...  68.6 us
    ppermute x53, starting transfers between devices, swapped(): return lax.ppermute(block, axis, [(i, i ^ mask) for i in range(count)])  64.4 us
    pallas_call x6, Pallas kernels, place(): pl.pallas_call(place_body, out_shape=jax.ShapeDtypeStruct((depth, 2 * hal...  19.5 us
  transfers between devices with their start and end apart: 53, of which 29 were waited for; matrix products, arithmetic and copies ran while one was open for 7% of the time, Pallas kernels for 36%

profile of v4, /device:TPU:0, one launch (start us, length us, event | category | flops | bytes accessed | tf_op | source)
XLA Modules:
  0.0 776.2 jit_solution(10958043940580280511)
XLA Ops:
  22.6 35.7 %collective-permute-done.1.refs_2_ = bf16[128,9216]{1,0:T(8,128)(2,1)S(1)} collective-permute-done((bf16[128,9216]{1,0:T(8,128)(2,1)}, bf16[128,9216]{1,0:T(8,128)(2,1)S(1)}, u32[]{:S(2)}, u32[]{:S(2)}) %collective-permute-start.1) | collective-permute-done | bytes 2359328 | tf_op jit(solution)/shard_map/ppermute | solution.py:16
  67.9 93.7 %collective-permute-done.3.refs_3_ = bf16[128,9216]{1,0:T(8,128)(2,1)} collective-permute-done((bf16[128,9216]{1,0:T(8,128)(2,1)}, bf16[128,9216]{1,0:T(8,128)(2,1)}, u32[]{:S(2)}, u32[]{:S(2)}) %collective-permute-start.3) | collective-permute-done | bytes 2359328 | tf_op jit(solution)/shard_map/ppermute | solution.py:16
  169.6 6.5 dynamic-slice_bitcast_fusion
  177.6 35.3 %collective-permute-done.6.refs_1_.refs_5_ = bf16[128,9216]{1,0:T(8,128)(2,1)S(1)} collective-permute-done((bf16[128,9216]{1,0:T(8,128)(2,1)S(1)}, bf16[128,9216]{1,0:T(8,128)(2,1)S(1)}, u32[]{:S(2)}, u32[]{:S(2)}) %collective-permute-start.6) | collective-permute-done | bytes 2359328 | tf_op jit(solution)/shard_map/ppermute | solution.py:16
  215.7 17.4 %shard_map.119.refs_10_ = f32[1024,1024]{1,0:T(8,128)} custom-call(bf16[384,9216]{1,0:T(8,128)(2,1)} %bitcast.52, bf16[384,9216]{1,0:T(8,128)(2,1)} %collective-permute-done.7.refs_1_, bf16[128,9216]{1,0:T(8,128)(2,1)} %copy-done.1, bf16[128,9216]{1,0:T(8,128)(2,1)} %collective-permute-done.3.refs_3_, ...), custom_call_target="tpu_custom_call" | custom-call | flops 1000 | bytes 1000 | tf_op jit(solution)/shard_map/pallas_call | solution.py:141
  233.1 15.3 %collective-permute-done.4.refs_6_.refs_4_.refs_3_.refs_2_ = bf16[3072,256]{1,0:T(8,128)(2,1)} collective-permute-done((bf16[3072,256]{1,0:T(8,128)(2,1)}, bf16[3072,256]{1,0:T(8,128)(2,1)}, u32[]{:S(2)}, u32[]{:S(2)}) %collective-permute-start.4) | collective-permute-done | bytes 1572896 | tf_op jit(solution)/shard_map/ppermute | solution.py:16
  256.1 28.8 %collective-permute-done.9.refs_7_.refs_5_.refs_3_.refs_2_ = bf16[1536,256]{1,0:T(8,128)(2,1)S(1)} collective-permute-done((bf16[1536,256]{1,0:T(8,128)(2,1)}, bf16[1536,256]{1,0:T(8,128)(2,1)S(1)}, u32[]{:S(2)}, u32[]{:S(2)}) %collective-permute-start.9) | collective-permute-done | bytes 786464 | tf_op jit(solution)/shard_map/ppermute | solution.py:16
  288.4 14.1 %shard_map.120.refs_7_ = f32[384,1024]{1,0:T(8,128)} custom-call(bf16[128,9216]{1,0:T(8,128)(2,1)} %collective-permute-done.10.refs_0_.refs_4_, bf16[128,9216]{1,0:T(8,128)(2,1)} %copy-done.2, bf16[128,9216]{1,0:T(8,128)(2,1)} %collective-permute-done.15.refs_2_.refs_6_, bf16[9216,256]{1,0:T(8,128)(2,1)} %get-tuple-element.262.refs_4_.refs_3_.refs_1_.refs_2_, ...), custom_call_target="tpu_custom_call" | custom-call | flops 1000 | bytes 1000 | tf_op jit(solution)/shard_map/pallas_call | solution.py:141
  304.1 19.8 %shard_map.121.refs_0_ = f32[1024,1024]{1,0:T(8,128)} custom-call(bf16[384,9216]{1,0:T(8,128)(2,1)} %bitcast.53, bf16[384,9216]{1,0:T(8,128)(2,1)} %collective-permute-done.7.refs_1_, bf16[128,9216]{1,0:T(8,128)(2,1)} %copy-done.1, bf16[128,9216]{1,0:T(8,128)(2,1)} %collective-permute-done.3.refs_3_, ...), custom_call_target="tpu_custom_call" | custom-call | flops 1000 | bytes 1000 | tf_op jit(solution)/shard_map/pallas_call | solution.py:141
  337.6 12.1 %shard_map.123.refs_2_ = f32[128,1024]{1,0:T(8,128)} custom-call(bf16[128,9216]{1,0:T(8,128)(2,1)} %copy-done.3, bf16[9216,256]{1,0:T(8,128)(2,1)} %get-tuple-element.262.refs_4_.refs_3_.refs_1_.refs_2_, bf16[9216,256]{1,0:T(8,128)(2,1)} %get-tuple-element.261.refs_5_.refs_4_.refs_2_.refs_3_, ...), custom_call_target="tpu_custom_call" | custom-call | flops 1000 | bytes 1000 | tf_op jit(solution)/shard_map/pallas_call | solution.py:141
  351.4 11.5 %shard_map.124 = (bf16[1536,1024]{1,0:T(8,128)(2,1)}, bf16[1536,1024]{1,0:T(8,128)(2,1)}) custom-call(f32[1024,1024]{1,0:T(8,128)} %shard_map.121.refs_0_, f32[384,1024]{1,0:T(8,128)} %shard_map.122.refs_1_, f32[128,1024]{1,0:T(8,128)} %shard_map.123.refs_2_, f32[4,1024]{1,0:T(4,128)} %pad_maximum_fusion.6.refs_3_, bf16[1536,512]{1,0:T(8,128)(2,1)} %copy-done.9, ...), custom_call_target="tpu_custom_call" | custom-call | flops 1000 | bytes 1000 | tf_op jit(solution)/shard_map/pallas_call | solution.py:184
  372.9 6.7 shard_map.136
  400.0 6.5 shard_map.135
  406.6 9.4 %collective-permute-done.20.refs_9_ = bf16[1536,512]{1,0:T(8,128)(2,1)} collective-permute-done((bf16[1536,512]{1,0:T(8,128)(2,1)}, bf16[1536,512]{1,0:T(8,128)(2,1)}, u32[]{:S(2)}, u32[]{:S(2)}) %collective-permute-start.20) | collective-permute-done | bytes 1572896 | tf_op jit(solution)/shard_map/ppermute | solution.py:16
  416.0 9.9 %collective-permute-done.19.refs_5_ = bf16[768,1536]{1,0:T(8,128)(2,1)} collective-permute-done((bf16[768,1536]{1,0:T(8,128)(2,1)}, bf16[768,1536]{1,0:T(8,128)(2,1)}, u32[]{:S(2)}, u32[]{:S(2)}) %collective-permute-start.19) | collective-permute-done | bytes 2359328 | tf_op jit(solution)/shard_map/ppermute | solution.py:16
  425.8 6.6 collective-permute-done.21
  440.1 7.2 shard_map.138
  457.4 6.7 shard_map.133
  464.1 6.4 collective-permute-done.27
  471.1 11.4 %collective-permute-done.26.got = bf16[1536,256]{1,0:T(8,128)(2,1)S(1)} collective-permute-done((bf16[1536,256]{1,0:T(8,128)(2,1)}, bf16[1536,256]{1,0:T(8,128)(2,1)S(1)}, u32[]{:S(2)}, u32[]{:S(2)}) %collective-permute-start.26) | collective-permute-done | bytes 786464 | tf_op jit(solution)/shard_map/ppermute | solution.py:16
  493.6 7.3 shard_map.140
  513.2 6.6 shard_map.131
  525.6 9.6 %collective-permute-done.31.got = bf16[1536,256]{1,0:T(8,128)(2,1)S(1)} collective-permute-done((bf16[1536,256]{1,0:T(8,128)(2,1)}, bf16[1536,256]{1,0:T(8,128)(2,1)S(1)}, u32[]{:S(2)}, u32[]{:S(2)}) %collective-permute-start.31) | collective-permute-done | bytes 786464 | tf_op jit(solution)/shard_map/ppermute | solution.py:16
  546.7 7.3 shard_map.144
  566.3 6.6 shard_map.129
  599.6 7.3 shard_map.149
  619.2 6.6 shard_map.127
  651.1 7.2 shard_map.154
  673.3 15.6 %collective-permute-done.46.got = bf16[1536,256]{1,0:T(8,128)(2,1)S(1)} collective-permute-done((bf16[1536,256]{1,0:T(8,128)(2,1)}, bf16[1536,256]{1,0:T(8,128)(2,1)S(1)}, u32[]{:S(2)}, u32[]{:S(2)}) %collective-permute-start.46) | collective-permute-done | bytes 786464 | tf_op jit(solution)/shard_map/ppermute | solution.py:16
  700.6 7.3 shard_map.159
  726.8 11.9 %collective-permute-done.49.got = bf16[1536,256]{1,0:T(8,128)(2,1)S(1)} collective-permute-done((bf16[1536,256]{1,0:T(8,128)(2,1)}, bf16[1536,256]{1,0:T(8,128)(2,1)S(1)}, u32[]{:S(2)}, u32[]{:S(2)}) %collective-permute-start.49) | collective-permute-done | bytes 786464 | tf_op jit(solution)/shard_map/ppermute | solution.py:16
  748.5 9.5 %shard_map.163.refs_1_ = bf16[3072,512]{1,0:T(8,128)(2,1)} custom-call(s32[14]{0:T(128)} %stack.109.at, bf16[960,512]{1,0:T(8,128)(2,1)} %pad_maximum_fusion.3.refs_0_, bf16[576,512]{1,0:T(8,128)(2,1)} %pad_maximum_fusion.5.refs_1_, bf16[960,512]{1,0:T(8,128)(2,1)} %collective-permute-done.22.refs_2_), custom_call_target="tpu_custom_call" | custom-call | flops 1000 | bytes 60000000 | tf_op jit(solution)/shard_map/pallas_call | solution.py:367
  (264 shorter events, 311.2 us)
Async XLA Ops:
  3.9 54.5 %collective-permute-start.1 = (bf16[128,9216]{1,0:T(8,128)(2,1)}, bf16[128,9216]{1,0:T(8,128)(2,1)S(1)}, u32[]{:S(2)}, u32[]{:S(2)}) collective-permute-start(bf16[128,9216]{1,0:T(8,128)(2,1)} %slice_bitcast_fusion), channel_id=1, source_target_pairs={{0,2},{1,3},{2,0},{3,1},{4,6},{5,7},{6,4},{7,5},{8,10},{9,11},{10,... | collective-permute-start | bytes 7077896 | tf_op jit(solution)/shard_map/ppermute | solution.py:16
  6.9 169.2 %collective-permute-start.7 = (bf16[384,9216]{1,0:T(8,128)(2,1)}, bf16[384,9216]{1,0:T(8,128)(2,1)}, u32[]{:S(2)}, u32[]{:S(2)}) collective-permute-start(bf16[384,9216]{1,0:T(8,128)(2,1)} %bitcast.50), channel_id=1, source_target_pairs={{0,1},{1,0},{2,3},{3,2},{4,5},{5,4},{6,7},{7,6},{8,9},{9,8},{10,11... | collective-permute-start | bytes 21233672 | tf_op jit(solution)/shard_map/ppermute | solution.py:16
  58.4 103.3 %collective-permute-start.3 = (bf16[128,9216]{1,0:T(8,128)(2,1)}, bf16[128,9216]{1,0:T(8,128)(2,1)}, u32[]{:S(2)}, u32[]{:S(2)}) collective-permute-start(bf16[128,9216]{1,0:T(8,128)(2,1)} %get-tuple-element.136), channel_id=1, source_target_pairs={{0,2},{1,3},{2,0},{3,1},{4,6},{5,7},{6,4},{7,5},{8,10},{9,11},{10,... | collective-permute-start | bytes 7077896 | tf_op jit(solution)/shard_map/ppermute | solution.py:16
  60.1 103.8 %collective-permute-start.2 = (bf16[4608,256]{1,0:T(8,128)(2,1)}, bf16[4608,256]{1,0:T(8,128)(2,1)}, u32[]{:S(2)}, u32[]{:S(2)}) collective-permute-start(bf16[4608,256]{1,0:T(8,128)(2,1)} %dynamic-slice_bitcast_fusion.2), channel_id=1, source_target_pairs={{0,4},{1,5},{2,6},{3,7},{4,0},{5,1},{6,2},{7,3},{8,12},{9,13},{10,... | collective-permute-start | bytes 7077896 | tf_op jit(solution)/shard_map/ppermute | solution.py:16
  66.3 99.6 %collective-permute-start.8 = (bf16[1536,512]{1,0:T(8,128)(2,1)S(1)}, bf16[1536,512]{1,0:T(8,128)(2,1)S(1)}, u32[]{:S(2)}, u32[]{:S(2)}) collective-permute-start(bf16[1536,512]{1,0:T(8,128)(2,1)S(1)} %fusion.9.refs_4_), channel_id=1, source_target_pairs={{0,16},{16,0},{1,17},{17,1},{2,18},{18,2},{3,19},{19,3},{4,20},{20... | collective-permute-start | bytes 4718600 | tf_op jit(solution)/shard_map/ppermute | solution.py:16
  66.4 146.6 %collective-permute-start.6 = (bf16[128,9216]{1,0:T(8,128)(2,1)S(1)}, bf16[128,9216]{1,0:T(8,128)(2,1)S(1)}, u32[]{:S(2)}, u32[]{:S(2)}) collective-permute-start(bf16[128,9216]{1,0:T(8,128)(2,1)S(1)} %collective-permute-done.1.refs_2_), channel_id=1, source_target_pairs={{0,1},{1,0},{2,3},{3,2},{4,5},{5,4},{6,7},{7,6},{8,9},{9,8},{10,11... | collective-permute-start | bytes 7077896 | tf_op jit(solution)/shard_map/ppermute | solution.py:16
  163.9 50.4 %collective-permute-start.5 = (bf16[4608,256]{1,0:T(8,128)(2,1)}, bf16[4608,256]{1,0:T(8,128)(2,1)S(1)}, u32[]{:S(2)}, u32[]{:S(2)}) collective-permute-start(bf16[4608,256]{1,0:T(8,128)(2,1)} %collective-permute-done.2.refs_6_.refs_5_.refs_3_.refs_2_), channel_id=1, source_target_pairs={{0,8},{8,0},{1,9},{9,1},{2,10},{10,2},{3,11},{11,3},{4,12},{12,4},... | collective-permute-start | bytes 7077896 | tf_op jit(solution)/shard_map/ppermute | solution.py:16
  165.4 83.8 %collective-permute-start.10 = (bf16[128,9216]{1,0:T(8,128)(2,1)}, bf16[128,9216]{1,0:T(8,128)(2,1)}, u32[]{:S(2)}, u32[]{:S(2)}) collective-permute-start(bf16[128,9216]{1,0:T(8,128)(2,1)} %get-tuple-element.151), channel_id=1, source_target_pairs={{0,2},{1,3},{2,0},{3,1},{4,6},{5,7},{6,4},{7,5},{8,10},{9,11},{10,... | collective-permute-start | bytes 7077896 | tf_op jit(solution)/shard_map/ppermute | solution.py:16
  167.0 81.4 %collective-permute-start.4 = (bf16[3072,256]{1,0:T(8,128)(2,1)}, bf16[3072,256]{1,0:T(8,128)(2,1)}, u32[]{:S(2)}, u32[]{:S(2)}) collective-permute-start(bf16[3072,256]{1,0:T(8,128)(2,1)} %dynamic-slice_bitcast_fusion.3), channel_id=1, source_target_pairs={{0,4},{1,5},{2,6},{3,7},{4,0},{5,1},{6,2},{7,3},{8,12},{9,13},{10,... | collective-permute-start | bytes 4718600 | tf_op jit(solution)/shard_map/ppermute | solution.py:16
  176.1 112.3 %collective-permute-start.15 = (bf16[128,9216]{1,0:T(8,128)(2,1)}, bf16[128,9216]{1,0:T(8,128)(2,1)}, u32[]{:S(2)}, u32[]{:S(2)}) collective-permute-start(bf16[128,9216]{1,0:T(8,128)(2,1)} %collective-permute-done.3.refs_3_), channel_id=1, source_target_pairs={{0,1},{1,0},{2,3},{3,2},{4,5},{5,4},{6,7},{7,6},{8,9},{9,8},{10,11... | collective-permute-start | bytes 7077896 | tf_op jit(solution)/shard_map/ppermute | solution.py:16
  249.2 80.0 %collective-permute-start.13 = (bf16[128,9216]{1,0:T(8,128)(2,1)}, bf16[128,9216]{1,0:T(8,128)(2,1)S(1)}, u32[]{:S(2)}, u32[]{:S(2)}) collective-permute-start(bf16[128,9216]{1,0:T(8,128)(2,1)} %collective-permute-done.10.refs_0_.refs_4_), channel_id=1, source_target_pairs={{0,1},{1,0},{2,3},{3,2},{4,5},{5,4},{6,7},{7,6},{8,9},{9,8},{10,11... | collective-permute-start | bytes 7077896 | tf_op jit(solution)/shard_map/ppermute | solution.py:16
  284.8 47.8 %collective-permute-start.12 = (bf16[1024,512]{1,0:T(8,128)(2,1)}, bf16[1024,512]{1,0:T(8,128)(2,1)}, u32[]{:S(2)}, u32[]{:S(2)}) collective-permute-start(bf16[1024,512]{1,0:T(8,128)(2,1)} %pad_maximum_fusion.1), channel_id=1, source_target_pairs={{0,4},{1,5},{2,6},{3,7},{4,0},{5,1},{6,2},{7,3},{8,12},{9,13},{10,... | collective-permute-start | bytes 3145736 | tf_op jit(solution)/shard_map/ppermute | solution.py:16
  286.4 51.1 %collective-permute-start.11 = (f32[4,512]{1,0:T(4,128)S(1)}, f32[4,512]{1,0:T(4,128)S(1)}, u32[]{:S(2)}, u32[]{:S(2)}) collective-permute-start(f32[4,512]{1,0:T(4,128)S(1)} %pad_maximum_fusion.9), channel_id=1, source_target_pairs={{0,4},{1,5},{2,6},{3,7},{4,0},{5,1},{6,2},{7,3},{8,12},{9,13},{10,... | collective-permute-start | bytes 24584 | tf_op jit(solution)/shard_map/ppermute | solution.py:16
  372.3 53.5 %collective-permute-start.19 = (bf16[768,1536]{1,0:T(8,128)(2,1)}, bf16[768,1536]{1,0:T(8,128)(2,1)}, u32[]{:S(2)}, u32[]{:S(2)}) collective-permute-start(bf16[768,1536]{1,0:T(8,128)(2,1)} %shard_map.125), channel_id=1, source_target_pairs={{0,1},{1,0},{2,3},{3,2},{4,5},{5,4},{6,7},{7,6},{8,9},{9,8},{10,11... | collective-permute-start | bytes 7077896 | tf_op jit(solution)/shard_map/ppermute | solution.py:16
  387.7 44.8 %collective-permute-start.22 = (bf16[960,512]{1,0:T(8,128)(2,1)}, bf16[960,512]{1,0:T(8,128)(2,1)}, u32[]{:S(2)}, u32[]{:S(2)}) collective-permute-start(bf16[960,512]{1,0:T(8,128)(2,1)} %pad_maximum_fusion.2), channel_id=1, source_target_pairs={{0,4},{1,5},{2,6},{3,7},{4,0},{5,1},{6,2},{7,3},{8,12},{9,13},{10,... | collective-permute-start | bytes 2949128 | tf_op jit(solution)/shard_map/ppermute | solution.py:16
  390.9 41.6 %collective-permute-start.21 = (f32[3,512]{1,0:T(4,128)S(1)}, f32[3,512]{1,0:T(4,128)S(1)}, u32[]{:S(2)}, u32[]{:S(2)}) collective-permute-start(f32[3,512]{1,0:T(4,128)S(1)} %pad_maximum_fusion.10), channel_id=1, source_target_pairs={{0,4},{1,5},{2,6},{3,7},{4,0},{5,1},{6,2},{7,3},{8,12},{9,13},{10,... | collective-permute-start | bytes 18440 | tf_op jit(solution)/shard_map/ppermute | solution.py:16
  432.5 53.5 %collective-permute-start.23 = (bf16[768,1536]{1,0:T(8,128)(2,1)}, bf16[768,1536]{1,0:T(8,128)(2,1)S(1)}, u32[]{:S(2)}, u32[]{:S(2)}) collective-permute-start(bf16[768,1536]{1,0:T(8,128)(2,1)} %shard_map.134), channel_id=1, source_target_pairs={{0,1},{1,0},{2,3},{3,2},{4,5},{5,4},{6,7},{7,6},{8,9},{9,8},{10,11... | collective-permute-start | bytes 7077896 | tf_op jit(solution)/shard_map/ppermute | solution.py:16
  434.0 50.7 %collective-permute-start.24 = (bf16[1536,512]{1,0:T(8,128)(2,1)}, bf16[1536,512]{1,0:T(8,128)(2,1)}, u32[]{:S(2)}, u32[]{:S(2)}) collective-permute-start(bf16[1536,512]{1,0:T(8,128)(2,1)} %shard_map.135), channel_id=1, source_target_pairs={{0,8},{8,0},{1,9},{9,1},{2,10},{10,2},{3,11},{11,3},{4,12},{12,4},... | collective-permute-start | bytes 4718600 | tf_op jit(solution)/shard_map/ppermute | solution.py:16
  440.1 44.6 %collective-permute-start.25 = (bf16[384,1536]{1,0:T(8,128)(2,1)}, bf16[384,1536]{1,0:T(8,128)(2,1)}, u32[]{:S(2)}, u32[]{:S(2)}) collective-permute-start(bf16[384,1536]{1,0:T(8,128)(2,1)} %shard_map.137), channel_id=1, source_target_pairs={{0,2},{1,3},{2,0},{3,1},{4,6},{5,7},{6,4},{7,5},{8,10},{9,11},{10,... | collective-permute-start | bytes 3538952 | tf_op jit(solution)/shard_map/ppermute | solution.py:16
  485.9 54.0 %collective-permute-start.28 = (bf16[768,1536]{1,0:T(8,128)(2,1)}, bf16[768,1536]{1,0:T(8,128)(2,1)}, u32[]{:S(2)}, u32[]{:S(2)}) collective-permute-start(bf16[768,1536]{1,0:T(8,128)(2,1)} %shard_map.132), channel_id=1, source_target_pairs={{0,1},{1,0},{2,3},{3,2},{4,5},{5,4},{6,7},{7,6},{8,9},{9,8},{10,11... | collective-permute-start | bytes 7077896 | tf_op jit(solution)/shard_map/ppermute | solution.py:16
  487.5 52.4 %collective-permute-start.29 = (bf16[1536,512]{1,0:T(8,128)(2,1)}, bf16[1536,512]{1,0:T(8,128)(2,1)}, u32[]{:S(2)}, u32[]{:S(2)}) collective-permute-start(bf16[1536,512]{1,0:T(8,128)(2,1)} %shard_map.133), channel_id=1, source_target_pairs={{0,8},{8,0},{1,9},{9,1},{2,10},{10,2},{3,11},{11,3},{4,12},{12,4},... | collective-permute-start | bytes 4718600 | tf_op jit(solution)/shard_map/ppermute | solution.py:16
  493.6 46.3 %collective-permute-start.30 = (bf16[384,1536]{1,0:T(8,128)(2,1)}, bf16[384,1536]{1,0:T(8,128)(2,1)}, u32[]{:S(2)}, u32[]{:S(2)}) collective-permute-start(bf16[384,1536]{1,0:T(8,128)(2,1)} %shard_map.139), channel_id=1, source_target_pairs={{0,2},{1,3},{2,0},{3,1},{4,6},{5,7},{6,4},{7,5},{8,10},{9,11},{10,... | collective-permute-start | bytes 3538952 | tf_op jit(solution)/shard_map/ppermute | solution.py:16
  539.9 51.9 %collective-permute-start.33 = (bf16[768,1536]{1,0:T(8,128)(2,1)S(1)}, bf16[768,1536]{1,0:T(8,128)(2,1)}, u32[]{:S(2)}, u32[]{:S(2)}) collective-permute-start(bf16[768,1536]{1,0:T(8,128)(2,1)S(1)} %copy-done.18), channel_id=1, source_target_pairs={{0,1},{1,0},{2,3},{3,2},{4,5},{5,4},{6,7},{7,6},{8,9},{9,8},{10,11... | collective-permute-start | bytes 7077896 | tf_op jit(solution)/shard_map/ppermute | solution.py:16
  540.5 51.3 %collective-permute-start.34 = (bf16[1536,512]{1,0:T(8,128)(2,1)}, bf16[1536,512]{1,0:T(8,128)(2,1)}, u32[]{:S(2)}, u32[]{:S(2)}) collective-permute-start(bf16[1536,512]{1,0:T(8,128)(2,1)} %shard_map.131), channel_id=1, source_target_pairs={{0,8},{8,0},{1,9},{9,1},{2,10},{10,2},{3,11},{11,3},{4,12},{12,4},... | collective-permute-start | bytes 4718600 | tf_op jit(solution)/shard_map/ppermute | solution.py:16
  546.6 45.2 %collective-permute-start.35 = (bf16[384,1536]{1,0:T(8,128)(2,1)}, bf16[384,1536]{1,0:T(8,128)(2,1)}, u32[]{:S(2)}, u32[]{:S(2)}) collective-permute-start(bf16[384,1536]{1,0:T(8,128)(2,1)} %shard_map.143), channel_id=1, source_target_pairs={{0,2},{1,3},{2,0},{3,1},{4,6},{5,7},{6,4},{7,5},{8,10},{9,11},{10,... | collective-permute-start | bytes 3538952 | tf_op jit(solution)/shard_map/ppermute | solution.py:16
  591.8 52.7 %collective-permute-start.38 = (bf16[768,1536]{1,0:T(8,128)(2,1)}, bf16[768,1536]{1,0:T(8,128)(2,1)S(1)}, u32[]{:S(2)}, u32[]{:S(2)}) collective-permute-start(bf16[768,1536]{1,0:T(8,128)(2,1)} %shard_map.128), channel_id=1, source_target_pairs={{0,1},{1,0},{2,3},{3,2},{4,5},{5,4},{6,7},{7,6},{8,9},{9,8},{10,11... | collective-permute-start | bytes 7077896 | tf_op jit(solution)/shard_map/ppermute | solution.py:16
  593.4 51.1 %collective-permute-start.39 = (bf16[1536,512]{1,0:T(8,128)(2,1)}, bf16[1536,512]{1,0:T(8,128)(2,1)}, u32[]{:S(2)}, u32[]{:S(2)}) collective-permute-start(bf16[1536,512]{1,0:T(8,128)(2,1)} %shard_map.129), channel_id=1, source_target_pairs={{0,8},{8,0},{1,9},{9,1},{2,10},{10,2},{3,11},{11,3},{4,12},{12,4},... | collective-permute-start | bytes 4718600 | tf_op jit(solution)/shard_map/ppermute | solution.py:16
  599.6 45.0 %collective-permute-start.40 = (bf16[384,1536]{1,0:T(8,128)(2,1)}, bf16[384,1536]{1,0:T(8,128)(2,1)}, u32[]{:S(2)}, u32[]{:S(2)}) collective-permute-start(bf16[384,1536]{1,0:T(8,128)(2,1)} %shard_map.148), channel_id=1, source_target_pairs={{0,2},{1,3},{2,0},{3,1},{4,6},{5,7},{6,4},{7,5},{8,10},{9,11},{10,... | collective-permute-start | bytes 3538952 | tf_op jit(solution)/shard_map/ppermute | solution.py:16
  644.6 49.5 %collective-permute-start.43 = (bf16[768,1536]{1,0:T(8,128)(2,1)}, bf16[768,1536]{1,0:T(8,128)(2,1)}, u32[]{:S(2)}, u32[]{:S(2)}) collective-permute-start(bf16[768,1536]{1,0:T(8,128)(2,1)} %shard_map.126), channel_id=1, source_target_pairs={{0,1},{1,0},{2,3},{3,2},{4,5},{5,4},{6,7},{7,6},{8,9},{9,8},{10,11... | collective-permute-start | bytes 7077896 | tf_op jit(solution)/shard_map/ppermute | solution.py:16
  644.7 49.3 %collective-permute-start.44 = (bf16[1536,512]{1,0:T(8,128)(2,1)}, bf16[1536,512]{1,0:T(8,128)(2,1)}, u32[]{:S(2)}, u32[]{:S(2)}) collective-permute-start(bf16[1536,512]{1,0:T(8,128)(2,1)} %shard_map.127), channel_id=1, source_target_pairs={{0,8},{8,0},{1,9},{9,1},{2,10},{10,2},{3,11},{11,3},{4,12},{12,4},... | collective-permute-start | bytes 4718600 | tf_op jit(solution)/shard_map/ppermute | solution.py:16
  651.1 42.9 %collective-permute-start.45 = (bf16[384,1536]{1,0:T(8,128)(2,1)}, bf16[384,1536]{1,0:T(8,128)(2,1)S(1)}, u32[]{:S(2)}, u32[]{:S(2)}) collective-permute-start(bf16[384,1536]{1,0:T(8,128)(2,1)} %shard_map.153), channel_id=1, source_target_pairs={{0,2},{1,3},{2,0},{3,1},{4,6},{5,7},{6,4},{7,5},{8,10},{9,11},{10,... | collective-permute-start | bytes 3538952 | tf_op jit(solution)/shard_map/ppermute | solution.py:16
  700.6 40.2 %collective-permute-start.48 = (bf16[384,1536]{1,0:T(8,128)(2,1)}, bf16[384,1536]{1,0:T(8,128)(2,1)S(1)}, u32[]{:S(2)}, u32[]{:S(2)}) collective-permute-start(bf16[384,1536]{1,0:T(8,128)(2,1)} %shard_map.156), channel_id=1, source_target_pairs={{0,2},{1,3},{2,0},{3,1},{4,6},{5,7},{6,4},{7,5},{8,10},{9,11},{10,... | collective-permute-start | bytes 3538952 | tf_op jit(solution)/shard_map/ppermute | solution.py:16
  (66 other events, 1160.2 us)

commit v5 on v3

--- a/solution.py
+++ b/solution.py
@@ -602,7 +602,7 @@
         return kept, sp(sent)
 
     y_next, s_next = y_part(0), None
-    cuts = [c * rows // 384 for c in (0, 960, 1536)]
+    cuts = [c * rows // 384 for c in (0, 768, 1536)]
     st_kept, st_got = [], []
     for n in range(nk + 2):
         if n < nk:

time: 785 us -> 785 us (level)
  transfers between devices with their start and end apart: 53 -> 53, of which waited for: 29 -> 28; matrix products, arithmetic and copies ran while one was open for 7% -> 6% of each run, Pallas kernels for 35% -> 36%
where the time goes in v5:
time: 785 us; the launch traced here: 774 us
  waiting for transfers between devices  340 us (43%)
  Pallas kernels  305 us (39%)
  starting transfers between devices  64.8 us (8%)
  local copies, waits for them, and re-layouts  40.2 us (5%)
  other arithmetic  16.1 us (2%)
    ppermute x53, waiting for transfers between devices, swapped(): return lax.ppermute(block, axis, [(i, i ^ mask) for i in range(count)])  340 us
    pallas_call x18, Pallas kernels, nt_product(): pl.pallas_call(body, out_shape=jax.ShapeDtypeStruct(shape, BF), grid=(ste...  102 us
    pallas_call x12, Pallas kernels, tn_product(): pl.pallas_call(body, out_shape=outs, grid=(steps,), in_specs=specs, out_s...  83.6 us
    ppermute x53, starting transfers between devices, swapped(): return lax.ppermute(block, axis, [(i, i ^ mask) for i in range(count)])  64.8 us
    pallas_call x5, Pallas kernels, forward(): pl.pallas_call(functools.partial(forward_body, len(xs), starts, acc is no...  61.8 us
    pallas_call x6, Pallas kernels, place(): pl.pallas_call(place_body, out_shape=jax.ShapeDtypeStruct((depth, 2 * hal...  19.3 us
  transfers between devices with their start and end apart: 53, of which 28 were waited for; matrix products, arithmetic and copies ran while one was open for 6% of the time, Pallas kernels for 36%

profile of v5, /device:TPU:0, one launch (start us, length us, event | category | flops | bytes accessed | tf_op | source)
XLA Modules:
  0.0 773.8 jit_solution(16826187243699696903)
XLA Ops:
  22.7 35.7 %collective-permute-done.1.refs_2_ = bf16[128,9216]{1,0:T(8,128)(2,1)S(1)} collective-permute-done((bf16[128,9216]{1,0:T(8,128)(2,1)}, bf16[128,9216]{1,0:T(8,128)(2,1)S(1)}, u32[]{:S(2)}, u32[]{:S(2)}) %collective-permute-start.1) | collective-permute-done | bytes 2359328 | tf_op jit(solution)/shard_map/ppermute | solution.py:16
  67.9 93.7 %collective-permute-done.3.refs_3_ = bf16[128,9216]{1,0:T(8,128)(2,1)} collective-permute-done((bf16[128,9216]{1,0:T(8,128)(2,1)}, bf16[128,9216]{1,0:T(8,128)(2,1)}, u32[]{:S(2)}, u32[]{:S(2)}) %collective-permute-start.3) | collective-permute-done | bytes 2359328 | tf_op jit(solution)/shard_map/ppermute | solution.py:16
  169.6 6.4 dynamic-slice_bitcast_fusion
  177.5 35.4 %collective-permute-done.6.refs_1_.refs_5_ = bf16[128,9216]{1,0:T(8,128)(2,1)S(1)} collective-permute-done((bf16[128,9216]{1,0:T(8,128)(2,1)S(1)}, bf16[128,9216]{1,0:T(8,128)(2,1)S(1)}, u32[]{:S(2)}, u32[]{:S(2)}) %collective-permute-start.6) | collective-permute-done | bytes 2359328 | tf_op jit(solution)/shard_map/ppermute | solution.py:16
  215.8 15.4 %shard_map.119.refs_10_ = f32[1024,1024]{1,0:T(8,128)} custom-call(bf16[384,9216]{1,0:T(8,128)(2,1)} %bitcast.52, bf16[384,9216]{1,0:T(8,128)(2,1)} %collective-permute-done.7.refs_1_, bf16[128,9216]{1,0:T(8,128)(2,1)} %copy-done.1, bf16[128,9216]{1,0:T(8,128)(2,1)} %collective-permute-done.3.refs_3_, ...), custom_call_target="tpu_custom_call" | custom-call | flops 1000 | bytes 1000 | tf_op jit(solution)/shard_map/pallas_call | solution.py:139
  231.2 17.2 %collective-permute-done.4.refs_6_.refs_4_.refs_3_.refs_2_ = bf16[3072,256]{1,0:T(8,128)(2,1)} collective-permute-done((bf16[3072,256]{1,0:T(8,128)(2,1)}, bf16[3072,256]{1,0:T(8,128)(2,1)}, u32[]{:S(2)}, u32[]{:S(2)}) %collective-permute-start.4) | collective-permute-done | bytes 1572896 | tf_op jit(solution)/shard_map/ppermute | solution.py:16
  256.1 28.7 %collective-permute-done.9.refs_7_.refs_5_.refs_3_.refs_2_ = bf16[1536,256]{1,0:T(8,128)(2,1)S(1)} collective-permute-done((bf16[1536,256]{1,0:T(8,128)(2,1)}, bf16[1536,256]{1,0:T(8,128)(2,1)S(1)}, u32[]{:S(2)}, u32[]{:S(2)}) %collective-permute-start.9) | collective-permute-done | bytes 786464 | tf_op jit(solution)/shard_map/ppermute | solution.py:16
  288.4 12.7 %shard_map.120.refs_7_ = f32[384,1024]{1,0:T(8,128)} custom-call(bf16[128,9216]{1,0:T(8,128)(2,1)} %collective-permute-done.10.refs_0_.refs_4_, bf16[128,9216]{1,0:T(8,128)(2,1)} %copy-done.2, bf16[128,9216]{1,0:T(8,128)(2,1)} %collective-permute-done.15.refs_2_.refs_6_, bf16[9216,256]{1,0:T(8,128)(2,1)} %get-tuple-element.262.refs_4_.refs_3_.refs_1_.refs_2_, ...), custom_call_target="tpu_custom_call" | custom-call | flops 1000 | bytes 1000 | tf_op jit(solution)/shard_map/pallas_call | solution.py:139
  304.1 18.1 %shard_map.121.refs_0_ = f32[1024,1024]{1,0:T(8,128)} custom-call(bf16[384,9216]{1,0:T(8,128)(2,1)} %bitcast.53, bf16[384,9216]{1,0:T(8,128)(2,1)} %collective-permute-done.7.refs_1_, bf16[128,9216]{1,0:T(8,128)(2,1)} %copy-done.1, bf16[128,9216]{1,0:T(8,128)(2,1)} %collective-permute-done.3.refs_3_, ...), custom_call_target="tpu_custom_call" | custom-call | flops 1000 | bytes 1000 | tf_op jit(solution)/shard_map/pallas_call | solution.py:139
  337.1 10.4 %shard_map.123.refs_2_ = f32[128,1024]{1,0:T(8,128)} custom-call(bf16[128,9216]{1,0:T(8,128)(2,1)} %copy-done.3, bf16[9216,256]{1,0:T(8,128)(2,1)} %get-tuple-element.262.refs_4_.refs_3_.refs_1_.refs_2_, bf16[9216,256]{1,0:T(8,128)(2,1)} %get-tuple-element.261.refs_5_.refs_4_.refs_2_.refs_3_, ...), custom_call_target="tpu_custom_call" | custom-call | flops 1000 | bytes 1000 | tf_op jit(solution)/shard_map/pallas_call | solution.py:139
  349.3 11.5 %shard_map.124 = (bf16[1536,1024]{1,0:T(8,128)(2,1)}, bf16[1536,1024]{1,0:T(8,128)(2,1)}) custom-call(f32[1024,1024]{1,0:T(8,128)} %shard_map.121.refs_0_, f32[384,1024]{1,0:T(8,128)} %shard_map.122.refs_1_, f32[128,1024]{1,0:T(8,128)} %shard_map.123.refs_2_, f32[4,1024]{1,0:T(4,128)} %pad_maximum_fusion.6.refs_3_, bf16[1536,512]{1,0:T(8,128)(2,1)} %copy-done.11, ...), custom_call_target="tpu_custom_call" | custom-call | flops 1000 | bytes 1000 | tf_op jit(solution)/shard_map/pallas_call | solution.py:181
  360.8 6.3 shard_map.125
  370.8 7.0 shard_map.136
  399.6 6.5 shard_map.135
  406.1 8.2 %collective-permute-done.20.refs_9_ = bf16[1536,512]{1,0:T(8,128)(2,1)} collective-permute-done((bf16[1536,512]{1,0:T(8,128)(2,1)}, bf16[1536,512]{1,0:T(8,128)(2,1)}, u32[]{:S(2)}, u32[]{:S(2)}) %collective-permute-start.20) | collective-permute-done | bytes 1572896 | tf_op jit(solution)/shard_map/ppermute | solution.py:16
  414.3 9.5 %collective-permute-done.19.refs_5_ = bf16[768,1536]{1,0:T(8,128)(2,1)} collective-permute-done((bf16[768,1536]{1,0:T(8,128)(2,1)}, bf16[768,1536]{1,0:T(8,128)(2,1)}, u32[]{:S(2)}, u32[]{:S(2)}) %collective-permute-start.19) | collective-permute-done | bytes 2359328 | tf_op jit(solution)/shard_map/ppermute | solution.py:16
  431.2 7.3 shard_map.138
  448.5 6.5 shard_map.133
  455.0 6.6 collective-permute-done.27
  462.2 11.4 %collective-permute-done.26.got = bf16[1536,256]{1,0:T(8,128)(2,1)S(1)} collective-permute-done((bf16[1536,256]{1,0:T(8,128)(2,1)}, bf16[1536,256]{1,0:T(8,128)(2,1)S(1)}, u32[]{:S(2)}, u32[]{:S(2)}) %collective-permute-start.26) | collective-permute-done | bytes 786464 | tf_op jit(solution)/shard_map/ppermute | solution.py:16
  484.7 7.3 shard_map.140
  504.3 6.6 shard_map.131
  516.5 9.7 %collective-permute-done.31.got = bf16[1536,256]{1,0:T(8,128)(2,1)S(1)} collective-permute-done((bf16[1536,256]{1,0:T(8,128)(2,1)}, bf16[1536,256]{1,0:T(8,128)(2,1)S(1)}, u32[]{:S(2)}, u32[]{:S(2)}) %collective-permute-start.31) | collective-permute-done | bytes 786464 | tf_op jit(solution)/shard_map/ppermute | solution.py:16
  538.7 7.4 shard_map.144
  558.5 6.6 shard_map.129
  591.9 7.3 shard_map.149
  611.5 6.6 shard_map.127
  643.9 7.3 shard_map.154
  666.0 16.4 %collective-permute-done.46.got = bf16[1536,256]{1,0:T(8,128)(2,1)S(1)} collective-permute-done((bf16[1536,256]{1,0:T(8,128)(2,1)}, bf16[1536,256]{1,0:T(8,128)(2,1)S(1)}, u32[]{:S(2)}, u32[]{:S(2)}) %collective-permute-start.46) | collective-permute-done | bytes 786464 | tf_op jit(solution)/shard_map/ppermute | solution.py:16
  693.8 7.3 shard_map.159
  715.7 16.0 %collective-permute-done.49.got = bf16[1536,256]{1,0:T(8,128)(2,1)S(1)} collective-permute-done((bf16[1536,256]{1,0:T(8,128)(2,1)}, bf16[1536,256]{1,0:T(8,128)(2,1)S(1)}, u32[]{:S(2)}, u32[]{:S(2)}) %collective-permute-start.49) | collective-permute-done | bytes 786464 | tf_op jit(solution)/shard_map/ppermute | solution.py:16
  742.8 8.8 %shard_map.163.refs_1_ = bf16[3072,512]{1,0:T(8,128)(2,1)} custom-call(s32[13]{0:T(128)} %stack.109.at, bf16[768,512]{1,0:T(8,128)(2,1)} %pad_maximum_fusion.4.refs_0_, bf16[768,512]{1,0:T(8,128)(2,1)} %pad_maximum_fusion.5.refs_1_, bf16[768,512]{1,0:T(8,128)(2,1)} %collective-permute-done.22.refs_2_), custom_call_target="tpu_custom_call" | custom-call | flops 1000 | bytes 60000000 | tf_op jit(solution)/shard_map/pallas_call | solution.py:364
  (253 shorter events, 310.9 us)
Async XLA Ops:
  3.9 54.5 %collective-permute-start.1 = (bf16[128,9216]{1,0:T(8,128)(2,1)}, bf16[128,9216]{1,0:T(8,128)(2,1)S(1)}, u32[]{:S(2)}, u32[]{:S(2)}) collective-permute-start(bf16[128,9216]{1,0:T(8,128)(2,1)} %slice_bitcast_fusion), channel_id=1, source_target_pairs={{0,2},{1,3},{2,0},{3,1},{4,6},{5,7},{6,4},{7,5},{8,10},{9,11},{10,... | collective-permute-start | bytes 7077896 | tf_op jit(solution)/shard_map/ppermute | solution.py:16
  6.9 169.1 %collective-permute-start.7 = (bf16[384,9216]{1,0:T(8,128)(2,1)}, bf16[384,9216]{1,0:T(8,128)(2,1)}, u32[]{:S(2)}, u32[]{:S(2)}) collective-permute-start(bf16[384,9216]{1,0:T(8,128)(2,1)} %bitcast.50), channel_id=1, source_target_pairs={{0,1},{1,0},{2,3},{3,2},{4,5},{5,4},{6,7},{7,6},{8,9},{9,8},{10,11... | collective-permute-start | bytes 21233672 | tf_op jit(solution)/shard_map/ppermute | solution.py:16
  58.4 103.3 %collective-permute-start.3 = (bf16[128,9216]{1,0:T(8,128)(2,1)}, bf16[128,9216]{1,0:T(8,128)(2,1)}, u32[]{:S(2)}, u32[]{:S(2)}) collective-permute-start(bf16[128,9216]{1,0:T(8,128)(2,1)} %get-tuple-element.136), channel_id=1, source_target_pairs={{0,2},{1,3},{2,0},{3,1},{4,6},{5,7},{6,4},{7,5},{8,10},{9,11},{10,... | collective-permute-start | bytes 7077896 | tf_op jit(solution)/shard_map/ppermute | solution.py:16
  60.1 103.8 %collective-permute-start.2 = (bf16[4608,256]{1,0:T(8,128)(2,1)}, bf16[4608,256]{1,0:T(8,128)(2,1)}, u32[]{:S(2)}, u32[]{:S(2)}) collective-permute-start(bf16[4608,256]{1,0:T(8,128)(2,1)} %dynamic-slice_bitcast_fusion.2), channel_id=1, source_target_pairs={{0,4},{1,5},{2,6},{3,7},{4,0},{5,1},{6,2},{7,3},{8,12},{9,13},{10,... | collective-permute-start | bytes 7077896 | tf_op jit(solution)/shard_map/ppermute | solution.py:16
  66.3 99.6 %collective-permute-start.8 = (bf16[1536,512]{1,0:T(8,128)(2,1)S(1)}, bf16[1536,512]{1,0:T(8,128)(2,1)S(1)}, u32[]{:S(2)}, u32[]{:S(2)}) collective-permute-start(bf16[1536,512]{1,0:T(8,128)(2,1)S(1)} %fusion.9.refs_4_), channel_id=1, source_target_pairs={{0,16},{16,0},{1,17},{17,1},{2,18},{18,2},{3,19},{19,3},{4,20},{20... | collective-permute-start | bytes 4718600 | tf_op jit(solution)/shard_map/ppermute | solution.py:16
  66.4 146.5 %collective-permute-start.6 = (bf16[128,9216]{1,0:T(8,128)(2,1)S(1)}, bf16[128,9216]{1,0:T(8,128)(2,1)S(1)}, u32[]{:S(2)}, u32[]{:S(2)}) collective-permute-start(bf16[128,9216]{1,0:T(8,128)(2,1)S(1)} %collective-permute-done.1.refs_2_), channel_id=1, source_target_pairs={{0,1},{1,0},{2,3},{3,2},{4,5},{5,4},{6,7},{7,6},{8,9},{9,8},{10,11... | collective-permute-start | bytes 7077896 | tf_op jit(solution)/shard_map/ppermute | solution.py:16
  163.9 50.4 %collective-permute-start.5 = (bf16[4608,256]{1,0:T(8,128)(2,1)}, bf16[4608,256]{1,0:T(8,128)(2,1)S(1)}, u32[]{:S(2)}, u32[]{:S(2)}) collective-permute-start(bf16[4608,256]{1,0:T(8,128)(2,1)} %collective-permute-done.2.refs_6_.refs_5_.refs_3_.refs_2_), channel_id=1, source_target_pairs={{0,8},{8,0},{1,9},{9,1},{2,10},{10,2},{3,11},{11,3},{4,12},{12,4},... | collective-permute-start | bytes 7077896 | tf_op jit(solution)/shard_map/ppermute | solution.py:16
  165.4 83.8 %collective-permute-start.10 = (bf16[128,9216]{1,0:T(8,128)(2,1)}, bf16[128,9216]{1,0:T(8,128)(2,1)}, u32[]{:S(2)}, u32[]{:S(2)}) collective-permute-start(bf16[128,9216]{1,0:T(8,128)(2,1)} %get-tuple-element.151), channel_id=1, source_target_pairs={{0,2},{1,3},{2,0},{3,1},{4,6},{5,7},{6,4},{7,5},{8,10},{9,11},{10,... | collective-permute-start | bytes 7077896 | tf_op jit(solution)/shard_map/ppermute | solution.py:16
  167.0 81.4 %collective-permute-start.4 = (bf16[3072,256]{1,0:T(8,128)(2,1)}, bf16[3072,256]{1,0:T(8,128)(2,1)}, u32[]{:S(2)}, u32[]{:S(2)}) collective-permute-start(bf16[3072,256]{1,0:T(8,128)(2,1)} %dynamic-slice_bitcast_fusion.3), channel_id=1, source_target_pairs={{0,4},{1,5},{2,6},{3,7},{4,0},{5,1},{6,2},{7,3},{8,12},{9,13},{10,... | collective-permute-start | bytes 4718600 | tf_op jit(solution)/shard_map/ppermute | solution.py:16
  176.0 112.4 %collective-permute-start.15 = (bf16[128,9216]{1,0:T(8,128)(2,1)}, bf16[128,9216]{1,0:T(8,128)(2,1)}, u32[]{:S(2)}, u32[]{:S(2)}) collective-permute-start(bf16[128,9216]{1,0:T(8,128)(2,1)} %collective-permute-done.3.refs_3_), channel_id=1, source_target_pairs={{0,1},{1,0},{2,3},{3,2},{4,5},{5,4},{6,7},{7,6},{8,9},{9,8},{10,11... | collective-permute-start | bytes 7077896 | tf_op jit(solution)/shard_map/ppermute | solution.py:16
  249.2 78.3 %collective-permute-start.13 = (bf16[128,9216]{1,0:T(8,128)(2,1)}, bf16[128,9216]{1,0:T(8,128)(2,1)S(1)}, u32[]{:S(2)}, u32[]{:S(2)}) collective-permute-start(bf16[128,9216]{1,0:T(8,128)(2,1)} %collective-permute-done.10.refs_0_.refs_4_), channel_id=1, source_target_pairs={{0,1},{1,0},{2,3},{3,2},{4,5},{5,4},{6,7},{7,6},{8,9},{9,8},{10,11... | collective-permute-start | bytes 7077896 | tf_op jit(solution)/shard_map/ppermute | solution.py:16
  284.8 47.7 %collective-permute-start.12 = (bf16[1024,512]{1,0:T(8,128)(2,1)}, bf16[1024,512]{1,0:T(8,128)(2,1)}, u32[]{:S(2)}, u32[]{:S(2)}) collective-permute-start(bf16[1024,512]{1,0:T(8,128)(2,1)} %pad_maximum_fusion.1), channel_id=1, source_target_pairs={{0,4},{1,5},{2,6},{3,7},{4,0},{5,1},{6,2},{7,3},{8,12},{9,13},{10,... | collective-permute-start | bytes 3145736 | tf_op jit(solution)/shard_map/ppermute | solution.py:16
  286.4 50.7 %collective-permute-start.11 = (f32[4,512]{1,0:T(4,128)S(1)}, f32[4,512]{1,0:T(4,128)S(1)}, u32[]{:S(2)}, u32[]{:S(2)}) collective-permute-start(f32[4,512]{1,0:T(4,128)S(1)} %pad_maximum_fusion.9), channel_id=1, source_target_pairs={{0,4},{1,5},{2,6},{3,7},{4,0},{5,1},{6,2},{7,3},{8,12},{9,13},{10,... | collective-permute-start | bytes 24584 | tf_op jit(solution)/shard_map/ppermute | solution.py:16
  370.3 53.5 %collective-permute-start.19 = (bf16[768,1536]{1,0:T(8,128)(2,1)}, bf16[768,1536]{1,0:T(8,128)(2,1)}, u32[]{:S(2)}, u32[]{:S(2)}) collective-permute-start(bf16[768,1536]{1,0:T(8,128)(2,1)} %shard_map.125), channel_id=1, source_target_pairs={{0,1},{1,0},{2,3},{3,2},{4,5},{5,4},{6,7},{7,6},{8,9},{9,8},{10,11... | collective-permute-start | bytes 7077896 | tf_op jit(solution)/shard_map/ppermute | solution.py:16
  377.9 36.4 %collective-permute-start.20 = (bf16[1536,512]{1,0:T(8,128)(2,1)}, bf16[1536,512]{1,0:T(8,128)(2,1)}, u32[]{:S(2)}, u32[]{:S(2)}) collective-permute-start(bf16[1536,512]{1,0:T(8,128)(2,1)} %shard_map.136), channel_id=1, source_target_pairs={{0,8},{8,0},{1,9},{9,1},{2,10},{10,2},{3,11},{11,3},{4,12},{12,4},... | collective-permute-start | bytes 4718600 | tf_op jit(solution)/shard_map/ppermute | solution.py:16
  387.2 36.6 %collective-permute-start.22 = (bf16[768,512]{1,0:T(8,128)(2,1)}, bf16[768,512]{1,0:T(8,128)(2,1)}, u32[]{:S(2)}, u32[]{:S(2)}) collective-permute-start(bf16[768,512]{1,0:T(8,128)(2,1)} %pad_maximum_fusion.3), channel_id=1, source_target_pairs={{0,4},{1,5},{2,6},{3,7},{4,0},{5,1},{6,2},{7,3},{8,12},{9,13},{10,... | collective-permute-start | bytes 2359304 | tf_op jit(solution)/shard_map/ppermute | solution.py:16
  423.8 53.2 %collective-permute-start.23 = (bf16[768,1536]{1,0:T(8,128)(2,1)}, bf16[768,1536]{1,0:T(8,128)(2,1)S(1)}, u32[]{:S(2)}, u32[]{:S(2)}) collective-permute-start(bf16[768,1536]{1,0:T(8,128)(2,1)} %shard_map.134), channel_id=1, source_target_pairs={{0,1},{1,0},{2,3},{3,2},{4,5},{5,4},{6,7},{7,6},{8,9},{9,8},{10,11... | collective-permute-start | bytes 7077896 | tf_op jit(solution)/shard_map/ppermute | solution.py:16
  425.1 50.7 %collective-permute-start.24 = (bf16[1536,512]{1,0:T(8,128)(2,1)}, bf16[1536,512]{1,0:T(8,128)(2,1)}, u32[]{:S(2)}, u32[]{:S(2)}) collective-permute-start(bf16[1536,512]{1,0:T(8,128)(2,1)} %shard_map.135), channel_id=1, source_target_pairs={{0,8},{8,0},{1,9},{9,1},{2,10},{10,2},{3,11},{11,3},{4,12},{12,4},... | collective-permute-start | bytes 4718600 | tf_op jit(solution)/shard_map/ppermute | solution.py:16
  431.2 44.6 %collective-permute-start.25 = (bf16[384,1536]{1,0:T(8,128)(2,1)}, bf16[384,1536]{1,0:T(8,128)(2,1)}, u32[]{:S(2)}, u32[]{:S(2)}) collective-permute-start(bf16[384,1536]{1,0:T(8,128)(2,1)} %shard_map.137), channel_id=1, source_target_pairs={{0,2},{1,3},{2,0},{3,1},{4,6},{5,7},{6,4},{7,5},{8,10},{9,11},{10,... | collective-permute-start | bytes 3538952 | tf_op jit(solution)/shard_map/ppermute | solution.py:16
  477.1 55.2 %collective-permute-start.28 = (bf16[768,1536]{1,0:T(8,128)(2,1)}, bf16[768,1536]{1,0:T(8,128)(2,1)}, u32[]{:S(2)}, u32[]{:S(2)}) collective-permute-start(bf16[768,1536]{1,0:T(8,128)(2,1)} %shard_map.132), channel_id=1, source_target_pairs={{0,1},{1,0},{2,3},{3,2},{4,5},{5,4},{6,7},{7,6},{8,9},{9,8},{10,11... | collective-permute-start | bytes 7077896 | tf_op jit(solution)/shard_map/ppermute | solution.py:16
  478.6 52.3 %collective-permute-start.29 = (bf16[1536,512]{1,0:T(8,128)(2,1)}, bf16[1536,512]{1,0:T(8,128)(2,1)}, u32[]{:S(2)}, u32[]{:S(2)}) collective-permute-start(bf16[1536,512]{1,0:T(8,128)(2,1)} %shard_map.133), channel_id=1, source_target_pairs={{0,8},{8,0},{1,9},{9,1},{2,10},{10,2},{3,11},{11,3},{4,12},{12,4},... | collective-permute-start | bytes 4718600 | tf_op jit(solution)/shard_map/ppermute | solution.py:16
  484.7 46.2 %collective-permute-start.30 = (bf16[384,1536]{1,0:T(8,128)(2,1)}, bf16[384,1536]{1,0:T(8,128)(2,1)S(1)}, u32[]{:S(2)}, u32[]{:S(2)}) collective-permute-start(bf16[384,1536]{1,0:T(8,128)(2,1)} %shard_map.139), channel_id=1, source_target_pairs={{0,2},{1,3},{2,0},{3,1},{4,6},{5,7},{6,4},{7,5},{8,10},{9,11},{10,... | collective-permute-start | bytes 3538952 | tf_op jit(solution)/shard_map/ppermute | solution.py:16
  532.2 51.7 %collective-permute-start.33 = (bf16[768,1536]{1,0:T(8,128)(2,1)}, bf16[768,1536]{1,0:T(8,128)(2,1)S(1)}, u32[]{:S(2)}, u32[]{:S(2)}) collective-permute-start(bf16[768,1536]{1,0:T(8,128)(2,1)} %shard_map.130), channel_id=1, source_target_pairs={{0,1},{1,0},{2,3},{3,2},{4,5},{5,4},{6,7},{7,6},{8,9},{9,8},{10,11... | collective-permute-start | bytes 7077896 | tf_op jit(solution)/shard_map/ppermute | solution.py:16
  532.5 51.4 %collective-permute-start.34 = (bf16[1536,512]{1,0:T(8,128)(2,1)}, bf16[1536,512]{1,0:T(8,128)(2,1)}, u32[]{:S(2)}, u32[]{:S(2)}) collective-permute-start(bf16[1536,512]{1,0:T(8,128)(2,1)} %shard_map.131), channel_id=1, source_target_pairs={{0,8},{8,0},{1,9},{9,1},{2,10},{10,2},{3,11},{11,3},{4,12},{12,4},... | collective-permute-start | bytes 4718600 | tf_op jit(solution)/shard_map/ppermute | solution.py:16
  538.6 45.3 %collective-permute-start.35 = (bf16[384,1536]{1,0:T(8,128)(2,1)}, bf16[384,1536]{1,0:T(8,128)(2,1)}, u32[]{:S(2)}, u32[]{:S(2)}) collective-permute-start(bf16[384,1536]{1,0:T(8,128)(2,1)} %shard_map.143), channel_id=1, source_target_pairs={{0,2},{1,3},{2,0},{3,1},{4,6},{5,7},{6,4},{7,5},{8,10},{9,11},{10,... | collective-permute-start | bytes 3538952 | tf_op jit(solution)/shard_map/ppermute | solution.py:16
  583.9 53.3 %collective-permute-start.38 = (bf16[768,1536]{1,0:T(8,128)(2,1)}, bf16[768,1536]{1,0:T(8,128)(2,1)}, u32[]{:S(2)}, u32[]{:S(2)}) collective-permute-start(bf16[768,1536]{1,0:T(8,128)(2,1)} %shard_map.128), channel_id=1, source_target_pairs={{0,1},{1,0},{2,3},{3,2},{4,5},{5,4},{6,7},{7,6},{8,9},{9,8},{10,11... | collective-permute-start | bytes 7077896 | tf_op jit(solution)/shard_map/ppermute | solution.py:16
  585.8 50.2 %collective-permute-start.39 = (bf16[1536,512]{1,0:T(8,128)(2,1)}, bf16[1536,512]{1,0:T(8,128)(2,1)}, u32[]{:S(2)}, u32[]{:S(2)}) collective-permute-start(bf16[1536,512]{1,0:T(8,128)(2,1)} %shard_map.129), channel_id=1, source_target_pairs={{0,8},{8,0},{1,9},{9,1},{2,10},{10,2},{3,11},{11,3},{4,12},{12,4},... | collective-permute-start | bytes 4718600 | tf_op jit(solution)/shard_map/ppermute | solution.py:16
  591.9 44.0 %collective-permute-start.40 = (bf16[384,1536]{1,0:T(8,128)(2,1)}, bf16[384,1536]{1,0:T(8,128)(2,1)S(1)}, u32[]{:S(2)}, u32[]{:S(2)}) collective-permute-start(bf16[384,1536]{1,0:T(8,128)(2,1)} %shard_map.148), channel_id=1, source_target_pairs={{0,2},{1,3},{2,0},{3,1},{4,6},{5,7},{6,4},{7,5},{8,10},{9,11},{10,... | collective-permute-start | bytes 3538952 | tf_op jit(solution)/shard_map/ppermute | solution.py:16
  637.2 49.9 %collective-permute-start.43 = (bf16[768,1536]{1,0:T(8,128)(2,1)}, bf16[768,1536]{1,0:T(8,128)(2,1)S(1)}, u32[]{:S(2)}, u32[]{:S(2)}) collective-permute-start(bf16[768,1536]{1,0:T(8,128)(2,1)} %shard_map.126), channel_id=1, source_target_pairs={{0,1},{1,0},{2,3},{3,2},{4,5},{5,4},{6,7},{7,6},{8,9},{9,8},{10,11... | collective-permute-start | bytes 7077896 | tf_op jit(solution)/shard_map/ppermute | solution.py:16
  637.7 49.4 %collective-permute-start.44 = (bf16[1536,512]{1,0:T(8,128)(2,1)}, bf16[1536,512]{1,0:T(8,128)(2,1)}, u32[]{:S(2)}, u32[]{:S(2)}) collective-permute-start(bf16[1536,512]{1,0:T(8,128)(2,1)} %shard_map.127), channel_id=1, source_target_pairs={{0,8},{8,0},{1,9},{9,1},{2,10},{10,2},{3,11},{11,3},{4,12},{12,4},... | collective-permute-start | bytes 4718600 | tf_op jit(solution)/shard_map/ppermute | solution.py:16
  643.9 43.3 %collective-permute-start.45 = (bf16[384,1536]{1,0:T(8,128)(2,1)}, bf16[384,1536]{1,0:T(8,128)(2,1)}, u32[]{:S(2)}, u32[]{:S(2)}) collective-permute-start(bf16[384,1536]{1,0:T(8,128)(2,1)} %shard_map.153), channel_id=1, source_target_pairs={{0,2},{1,3},{2,0},{3,1},{4,6},{5,7},{6,4},{7,5},{8,10},{9,11},{10,... | collective-permute-start | bytes 3538952 | tf_op jit(solution)/shard_map/ppermute | solution.py:16
  693.8 40.1 %collective-permute-start.48 = (bf16[384,1536]{1,0:T(8,128)(2,1)}, bf16[384,1536]{1,0:T(8,128)(2,1)}, u32[]{:S(2)}, u32[]{:S(2)}) collective-permute-start(bf16[384,1536]{1,0:T(8,128)(2,1)} %shard_map.156), channel_id=1, source_target_pairs={{0,2},{1,3},{2,0},{3,1},{4,6},{5,7},{6,4},{7,5},{8,10},{9,11},{10,... | collective-permute-start | bytes 3538952 | tf_op jit(solution)/shard_map/ppermute | solution.py:16
  (61 other events, 1088.6 us)
